TPU v7x, 512 devices: a whole 4x4x16 slice. The times are simulated.
512 devices in a mesh: dp: 128 (over z, x, core), layer: 4 (over y).
Axes of the slice: x: 4, y: 4, z: 16, core: 2. Of those that a mesh axis runs over, the one named last changes fastest.
Arguments:
- micro_grads: bfloat16 [4, 128, 256, 2048], P('layer', 'dp')
- master: float32 [4, 384, 2, 2048], P('layer', 'dp'), may hold values from -6 to 6
- moment_one: float32 [4, 384, 2, 2048], P('layer', 'dp'), may hold values from -4 to 4
- moment_two: float32 [4, 384, 2, 2048], P('layer', 'dp'), may hold values from 0.01 to 1
- owner: int32 [4, 128], P('layer'), may hold values from 0 to 127, as said below
- slot: int32 [4, 128], P('layer'), may hold values from 0 to 2, as said below
Outputs:
- new_master: float32 [4, 384, 2, 2048], P('layer', 'dp')
- new_moment_one: float32 [4, 384, 2, 2048], P('layer', 'dp')
- new_moment_two: float32 [4, 384, 2, 2048], P('layer', 'dp')
- weights: bfloat16 [4, 256, 2048], P('layer')
- grad_rms: float32 [], replicated
Inputs may be any that keep to these rules, and one draw needn't show every extreme that they name: In every layer no owner holds more than 3 blocks, and some owner holds exactly 3. The pairs (owner, slot) of one layer are all different.
All inputs are finite; a program needn't handle non-finite values.
Results may differ from a plain program's by a relative error of at most 0.0004.
Values may be sent and summed in bfloat16 or wider, within the bound.
No kernel may reach another device: no remote copies, remote signals or barrier semaphores. Data moves between devices by JAX's collectives and lax.ppermute only.
A program may use at most 64 MiB of HBM per device.

v0:
```python
import jax
import jax.numpy as jnp
from jax import lax
from jax.sharding import PartitionSpec as P

beta_one = 0.9
beta_two = 0.95
learn_rate = 0.0003
decay_rate = 0.1
adam_eps = 1e-08
step_number = 100.0


def adamw(param, first, second, grad):
    first_new = beta_one * first + (1.0 - beta_one) * grad
    second_new = beta_two * second + (1.0 - beta_two) * grad * grad
    corr_one = 1.0 - beta_one**step_number
    corr_two = 1.0 - beta_two**step_number
    update = (
        first_new / corr_one / (jnp.sqrt(second_new / corr_two) + adam_eps) + decay_rate * param
    )
    return (param - learn_rate * update, first_new, second_new)


def shards(micro_grads, master, moment_one, moment_two, owner, slot):
    my_index = lax.axis_index("dp")
    row_count = micro_grads.shape[2]
    feature_count = micro_grads.shape[3]
    capacity = master.shape[1]
    slab_rows = master.shape[2]
    block_count = owner.shape[1]
    summed = micro_grads[0, 0].astype(jnp.float32)
    flat_grad = summed.reshape(-1, 128)
    grad_share = lax.psum_scatter(flat_grad, "dp", scatter_dimension=0, tiled=True)
    reduced = lax.all_gather(grad_share, "dp", axis=0, tiled=True).reshape(row_count, feature_count)
    squares = lax.psum(jnp.sum(grad_share * grad_share), ("dp", "layer"))
    element_total = lax.axis_size("layer") * row_count * feature_count
    grad_rms = jnp.sqrt(squares / element_total + 1e-06)
    clip_factor = jnp.minimum(1.0, 1.0 / grad_rms)
    owners = owner[0]
    slots_of = slot[0]
    slot_ids = jnp.arange(capacity, dtype=jnp.int32)
    matches = (owners[None, :] == my_index) & (slots_of[None, :] == slot_ids[:, None])
    filled = jnp.any(matches, axis=1)
    block_of_slot = jnp.sum(
        jnp.where(matches, jnp.arange(block_count, dtype=jnp.int32)[None, :], 0), axis=1
    )
    blocks_grad = reduced.reshape(block_count, slab_rows, feature_count)
    grad_slots = jnp.take(blocks_grad, block_of_slot, axis=0) * clip_factor
    param, first, second = adamw(master[0], moment_one[0], moment_two[0], grad_slots)
    keep = filled[:, None, None]
    new_master = jnp.where(keep, param, master[0])
    new_first = jnp.where(keep, first, moment_one[0])
    new_second = jnp.where(keep, second, moment_two[0])
    slot_weights = param.astype(jnp.bfloat16)
    mine = owners == my_index
    block_weights = jnp.take(slot_weights, slots_of, axis=0)
    placed = jnp.where(mine[:, None, None], block_weights.astype(jnp.float32), 0.0).reshape(-1, 128)
    weight_share = lax.psum_scatter(placed, "dp", scatter_dimension=0, tiled=True).astype(
        jnp.bfloat16
    )
    weights = lax.all_gather(weight_share, "dp", axis=0, tiled=True).reshape(
        row_count, feature_count
    )
    return (new_master[None], new_first[None], new_second[None], weights[None], grad_rms)


def solution(mesh):
    in_specs = (
        P("layer", "dp", None, None),
        P("layer", "dp", None, None),
        P("layer", "dp", None, None),
        P("layer", "dp", None, None),
        P("layer", None),
        P("layer", None),
    )
    out_specs = (
        P("layer", "dp", None, None),
        P("layer", "dp", None, None),
        P("layer", "dp", None, None),
        P("layer", None, None),
        P(),
    )
    return jax.shard_map(shards, mesh=mesh, in_specs=in_specs, out_specs=out_specs, check_vma=False)
```

profile of v0, /device:TPU:1, one launch (start us, length us, event | category | flops | bytes accessed | tf_op | source)
XLA Modules:
  0.0 830.3 jit_solution(17510532060689569105)
XLA Ops:
  7.2 0.0 copy-start.4
  7.2 0.0 copy-start.3
  7.2 0.0 reduce-scatter.3.cloned.1.call-start
  7.2 2.6 reshape.111
  9.8 0.0 reduce-scatter.3.cloned.1.call-update
  9.9 0.0 all-gather.3.cloned.1.call-start
  9.9 258.4 %reduce-scatter.3.cloned.1.call-done = f32[32,128]{1,0:T(8,128)} async-done(((f32[4096,128]{1,0:T(8,128)}), f32[32,128]{1,0:T(8,128)}) %reduce-scatter.3.cloned.1.call-update) | async-done | bytes 16400 | tf_op jit(solution)/shard_map/reduce_scatter | solution.py:34
  268.3 0.0 all-gather.3.cloned.1.call-update
  268.3 0.0 reduce-scatter.5.cloned.1.call-start
  268.4 0.0 copy-done.4
  268.4 0.1 select_reduce_fusion
  268.6 1.3 multiply_reduce_fusion
  269.9 113.3 %psum.7 = f32[]{:T(128)} all-reduce(f32[]{:T(128)} %multiply_reduce_fusion), channel_id=1, replica_groups=mesh['dp'=128,'layer'=4] {'dp','layer'}, use_global_device_ids=true, to_apply=%region_4.5 | all-reduce | flops 1 | bytes 8 | tf_op jit(solution)/shard_map/psum | solution.py:36
  383.9 0.0 copy-start
  384.0 0.0 copy-start.1
  384.0 0.0 copy-start.2
  384.0 36.3 %all-gather.3.cloned.1.call-done = f32[4096,128]{1,0:T(8,128)} async-done(((f32[32,128]{1,0:T(8,128)}), f32[4096,128]{1,0:T(8,128)}) %all-gather.3.cloned.1.call-update) | async-done | bytes 2097168 | tf_op jit(solution)/shard_map/all_gather | solution.py:35
  420.3 2.3 reshape_reshape.3
  422.6 0.6 gather_fusion
  423.2 0.3 fusion.9
  423.5 2.7 gather_fusion.1
  426.2 2.0 convert_select_fusion
  428.2 2.7 select_n.93
  430.9 0.0 reduce-scatter.5.cloned.1.call-update
  430.9 0.0 all-gather.5.cloned.1.call-start
  431.0 246.2 %reduce-scatter.5.cloned.1.call-done = f32[32,128]{1,0:T(8,128)} async-done(((f32[4096,128]{1,0:T(8,128)}), f32[32,128]{1,0:T(8,128)}) %reduce-scatter.5.cloned.1.call-update) | async-done | bytes 16400 | tf_op jit(solution)/shard_map/reduce_scatter | solution.py:59
  677.2 1.3 convert_element_type.22
  678.6 0.0 all-gather.5.cloned.1.call-update
  678.6 0.1 fusion.11
  678.7 1.0 broadcast_select_fusion.1
  679.7 140.7 %all-gather.5.cloned.1.call-done = bf16[4096,128]{1,0:T(8,128)(2,1)} async-done(((bf16[32,128]{1,0:T(8,128)(2,1)}), bf16[4096,128]{1,0:T(8,128)(2,1)}) %all-gather.5.cloned.1.call-update) | async-done | bytes 1048592 | tf_op jit(solution)/shard_map/all_gather | solution.py:62
  820.3 2.3 broadcast_in_dim_reshape.3
  (11 shorter events, 0.1 us)
Async XLA Ops:
  7.2 261.2 %copy-start.4 = (s32[1,128]{1,0:T(1,128)S(1)}, s32[1,128]{1,0:T(1,128)}, u32[]{:S(2)}) copy-start(s32[1,128]{1,0:T(1,128)} %param.11) | copy-start | bytes 1540
  7.2 261.2 %copy-start.3 = (s32[1,128]{1,0:T(1,128)S(1)}, s32[1,128]{1,0:T(1,128)}, u32[]{:S(2)}) copy-start(s32[1,128]{1,0:T(1,128)} %param.10) | copy-start | bytes 1540
  7.2 261.1 %reduce-scatter.3.cloned.1.call-start = ((), (), s32[]{:S(2)}) async-start(), calls=%async_computation.2 | async-start | bytes 2113536 | tf_op jit(solution)/shard_map/reduce_scatter | solution.py:34
  9.9 410.4 %all-gather.3.cloned.1.call-start = ((), (), s32[]{:S(2)}) async-start(), calls=%async_computation.3 | async-start | bytes 2113536 | tf_op jit(solution)/shard_map/all_gather | solution.py:35
  268.3 408.9 %reduce-scatter.5.cloned.1.call-start = ((), (), s32[]{:S(2)}) async-start(), calls=%async_computation.4 | async-start | bytes 2113536 | tf_op jit(solution)/shard_map/reduce_scatter | solution.py:59
  383.9 39.3 %copy-start = (f32[1,3,2,2048]{3,2,1,0:T(2,128)S(1)}, f32[1,3,2,2048]{3,2,1,0:T(2,128)}, u32[]{:S(2)}) copy-start(f32[1,3,2,2048]{3,2,1,0:T(2,128)} %param.9) | copy-start | bytes 147460
  384.0 39.3 %copy-start.1 = (f32[1,3,2,2048]{3,2,1,0:T(2,128)S(1)}, f32[1,3,2,2048]{3,2,1,0:T(2,128)}, u32[]{:S(2)}) copy-start(f32[1,3,2,2048]{3,2,1,0:T(2,128)} %param.7) | copy-start | bytes 147460
  384.0 39.3 %copy-start.2 = (f32[1,3,2,2048]{3,2,1,0:T(2,128)S(1)}, f32[1,3,2,2048]{3,2,1,0:T(2,128)}, u32[]{:S(2)}) copy-start(f32[1,3,2,2048]{3,2,1,0:T(2,128)} %param.8) | copy-start | bytes 147460
  430.9 389.4 %all-gather.5.cloned.1.call-start = ((), (), s32[]{:S(2)}) async-start(), calls=%async_computation.5 | async-start | bytes 1056768 | tf_op jit(solution)/shard_map/all_gather | solution.py:62
Sparse Core Ops, SparseCore 0:
  12.6 255.6 reduce-scatter.2
  271.4 148.7 all-gather.2
  431.1 246.1 reduce-scatter.4
  680.6 139.6 all-gather.4
where the time goes:
time: 831 us; the launch traced here: 830 us
  waiting for transfers between devices  682 us (82%)
  blocking collectives  113 us (14%)
  between operations  15.8 us (2%)
  local copies, waits for them, and re-layouts  13.3 us (2%)
    reduce_scatter x1, waiting for transfers between devices, shards(): lax.psum_scatter(flat_grad, 'dp', scatter_dimension=0, tiled=True)  258 us
    reduce_scatter x1, waiting for transfers between devices, shards(): lax.psum_scatter(placed, 'dp', scatter_dimension=0, tiled=True)  246 us
    all_gather x1, waiting for transfers between devices, shards(): lax.all_gather(weight_share, 'dp', axis=0, tiled=True)  141 us
    psum x1, blocking collectives, shards(): squares = lax.psum(jnp.sum(grad_share * grad_share), ('dp', 'layer'))  113 us
    all_gather x1, waiting for transfers between devices, shards(): lax.all_gather(grad_share, 'dp', axis=0, tiled=True)  36.3 us
  transfers between devices with their start and end apart: 4, of which 4 were waited for; matrix products, arithmetic and copies ran while one was open for 0% of the time, Pallas kernels for 0%

commit v1 on v0

v1 whole, which is shorter than its diff:
```python
import jax
import jax.numpy as jnp
from jax import lax
from jax.sharding import Mesh
from jax.sharding import PartitionSpec as P

beta_one = 0.9
beta_two = 0.95
learn_rate = 0.0003
decay_rate = 0.1
adam_eps = 1e-08
step_number = 100.0

RING = "z"
PLANE = ("x", "c")
PLANE_SHAPE = (4, 2)


def adamw(param, first, second, grad):
    first_new = beta_one * first + (1.0 - beta_one) * grad
    second_new = beta_two * second + (1.0 - beta_two) * grad * grad
    corr_one = 1.0 - beta_one**step_number
    corr_two = 1.0 - beta_two**step_number
    update = (
        first_new / corr_one / (jnp.sqrt(second_new / corr_two) + adam_eps) + decay_rate * param
    )
    return (param - learn_rate * update, first_new, second_new)


def exchange(chunks, axis):
    return lax.all_to_all(chunks, axis, 0, 0, tiled=True)


def share(value, axis):
    copies = jnp.broadcast_to(value[None], (lax.axis_size(axis), *value.shape))
    return exchange(lax.optimization_barrier(copies), axis)


def shards(micro_grads, master, moment_one, moment_two, owner, slot):
    rows, width = micro_grads.shape[2:]
    capacity, slab = master.shape[1:3]
    ring = lax.axis_size(RING)
    plane = lax.axis_size(PLANE)
    lines = capacity * slab
    wide = width // plane
    home = owner[0] * capacity + slot[0]
    home_row = (home[:, None] * slab + jnp.arange(slab, dtype=jnp.int32)[None, :]).reshape(rows)

    local = micro_grads[0, 0].reshape(rows, plane, wide).transpose(1, 0, 2)
    raw = exchange(local, PLANE)
    plane_sum = jnp.sum(raw.astype(jnp.float32), axis=0)
    piece = jnp.sum(exchange(plane_sum.reshape(ring, rows // ring, wide), RING), axis=0)
    totals = share(piece, RING).reshape(rows, wide)

    squares = jnp.broadcast_to(jnp.sum(totals * totals), (8, 128))
    squares = jnp.sum(share(squares, (*PLANE, "layer"))[:, 0, 0])
    element_total = lax.axis_size("layer") * rows * width
    grad_rms = jnp.sqrt(squares / element_total + 1e-06)
    clip_factor = jnp.minimum(1.0, 1.0 / grad_rms)

    states = jnp.stack([master[0], moment_one[0], moment_two[0]]).reshape(3 * lines, plane, wide)
    states = exchange(states.transpose(1, 0, 2), PLANE).reshape(plane, 3, lines, wide)
    old = [states[:, i].reshape(plane * lines, wide) for i in range(3)]
    slot_row = lax.axis_index(RING) * plane * lines + jnp.arange(plane * lines, dtype=jnp.int32)
    pick = slot_row[:, None] == home_row[None, :]
    grad_slots = jnp.dot(pick.astype(jnp.float32), totals, precision=lax.Precision.HIGHEST)
    new = adamw(*old, grad_slots * clip_factor)
    keep = jnp.any(pick, axis=1)[:, None]
    new = [jnp.where(keep, n, o) for n, o in zip(new, old, strict=True)]
    strip = new[0].astype(jnp.bfloat16)

    strips = share(strip, RING).reshape(ring * plane * lines, wide)
    place = home_row[:, None] == jnp.arange(ring * plane * lines, dtype=jnp.int32)[None, :]
    placed = jnp.dot(
        place.astype(jnp.bfloat16), strips, preferred_element_type=jnp.float32
    ).astype(jnp.bfloat16)
    halves = lax.all_gather(placed, "x", axis=0, tiled=False)
    others = lax.ppermute(halves, "c", [(0, 1), (1, 0)])
    first_core = lax.axis_index("c") == 0
    pair = [jnp.where(first_core, halves, others), jnp.where(first_core, others, halves)]
    weights = jnp.stack(pair, axis=1).transpose(2, 0, 1, 3).reshape(rows, width)

    back = jnp.stack([n.reshape(plane, lines, wide) for n in new], axis=1)
    back = exchange(back.reshape(plane, 3 * lines, wide), PLANE)
    back = back.transpose(1, 0, 2).reshape(3, 1, capacity, slab, width)
    return (back[0], back[1], back[2], weights[None], grad_rms)


def solution(mesh):
    ring = mesh.shape["dp"] // (PLANE_SHAPE[0] * PLANE_SHAPE[1])
    devices = mesh.devices.reshape(ring, *PLANE_SHAPE, mesh.shape["layer"])
    split = Mesh(devices, (RING, *PLANE, "layer"))
    dp = (RING, *PLANE)
    in_specs = (
        P("layer", dp, None, None),
        P("layer", dp, None, None),
        P("layer", dp, None, None),
        P("layer", dp, None, None),
        P("layer", None),
        P("layer", None),
    )
    out_specs = (
        P("layer", dp, None, None),
        P("layer", dp, None, None),
        P("layer", dp, None, None),
        P("layer", None, None),
        P(),
    )
    return jax.shard_map(
        shards, mesh=split, in_specs=in_specs, out_specs=out_specs, check_vma=False
    )
```

time: 831 us -> 171 us (0.21)
  waiting for transfers between devices: 682 us -> 42.9 us
  blocking collectives: 113 us -> 57.3 us
  starting transfers between devices: 0.16 us -> 53.4 us
  between operations: 15.8 us -> 2.83 us
    reduce_scatter x2 -> x0, waiting for transfers between devices: 505 us -> none  [the longest x1 258 us: shards(): lax.psum_scatter(flat_grad, 'dp', scatter_dimension=0, tiled=True)]
    all_gather x2 -> x0, waiting for transfers between devices: 177 us -> none  [the longest x1 141 us: shards(): lax.all_gather(weight_share, 'dp', axis=0, tiled=True)]
    psum x1 -> x0, blocking collectives: 113 us -> none  [shards(): squares = lax.psum(jnp.sum(grad_share * grad_share), ('dp', 'layer'))]
    all_to_all x0 -> x2, blocking collectives: none -> 47.1 us  [exchange(): return lax.all_to_all(chunks, axis, 0, 0, tiled=True)]
    all_to_all x0 -> x5, waiting for transfers between devices: none -> 42.8 us  [exchange(): return lax.all_to_all(chunks, axis, 0, 0, tiled=True)]
    all_to_all x0 -> x5, starting transfers between devices: none -> 41.5 us  [exchange(): return lax.all_to_all(chunks, axis, 0, 0, tiled=True)]
    ppermute x0 -> x1, starting transfers between devices: none -> 11.9 us  [shards(): others = lax.ppermute(halves, 'c', [(0, 1), (1, 0)])]
    all_gather x0 -> x1, blocking collectives: none -> 10.2 us  [shards(): halves = lax.all_gather(placed, 'x', axis=0, tiled=False)]
  transfers between devices with their start and end apart: 4 -> 6, of which waited for: 4 -> 5; matrix products, arithmetic and copies ran while one was open for 0% -> 3% of each run, Pallas kernels for 0% -> 0%
where the time goes in v1:
time: 171 us; the launch traced here: 170 us
  blocking collectives  57.3 us (34%)
  starting transfers between devices  53.4 us (31%)
  waiting for transfers between devices  42.9 us (25%)
  local copies, waits for them, and re-layouts  10.7 us (6%)
  between operations  2.83 us (2%)
  other arithmetic  2.69 us (2%)
    all_to_all x2, blocking collectives, exchange(): return lax.all_to_all(chunks, axis, 0, 0, tiled=True)  47.1 us
    all_to_all x5, waiting for transfers between devices, exchange(): return lax.all_to_all(chunks, axis, 0, 0, tiled=True)  42.8 us
    all_to_all x5, starting transfers between devices, exchange(): return lax.all_to_all(chunks, axis, 0, 0, tiled=True)  41.5 us
    ppermute x1, starting transfers between devices, shards(): others = lax.ppermute(halves, 'c', [(0, 1), (1, 0)])  11.9 us
    all_gather x1, blocking collectives, shards(): halves = lax.all_gather(placed, 'x', axis=0, tiled=False)  10.2 us
  transfers between devices with their start and end apart: 6, of which 5 were waited for; matrix products, arithmetic and copies ran while one was open for 3% of the time, Pallas kernels for 0%

profile of v1, /device:TPU:1, one launch (start us, length us, event | category | flops | bytes accessed | tf_op | source)
XLA Modules:
  0.0 170.3 jit_solution(16689518540870504957)
XLA Ops:
  0.6 1.5 copy.54
  2.1 0.5 copy.55
  2.7 24.4 %all_to_all.35 = bf16[8,256,256]{2,1,0:T(8,128)(2,1)S(1)} all-to-all(bf16[8,256,256]{2,1,0:T(8,128)(2,1)S(1)} %copy.55), channel_id=1, replica_groups=mesh['z'=16,'x'=4,'c'=2,'layer'=4] {'x','c'}, dimensions={0} | all-to-all | bytes 2097152 | tf_op jit(solution)/shard_map/all_to_all | solution.py:31
  27.0 0.8 convert_reduce_fusion
  27.9 11.2 %all-to-all-start.2 = ((f32[16,16,256]{2,1,0:T(8,128)}), f32[16,16,256]{2,1,0:T(8,128)S(1)}, u32[]{:S(2)}, u32[]{:S(2)}) async-start(f32[16,16,256]{2,1,0:T(8,128)} %bitcast.5), calls=%async_computation.2 | async-start | bytes 524288 | tf_op jit(solution)/shard_map/all_to_all | solution.py:31
  39.3 0.7 copy.50
  40.1 12.0 %all-to-all-done.2 = f32[16,16,256]{2,1,0:T(8,128)S(1)} async-done(((f32[16,16,256]{2,1,0:T(8,128)}), f32[16,16,256]{2,1,0:T(8,128)S(1)}, u32[]{:S(2)}, u32[]{:S(2)}) %all-to-all-start.2) | async-done | bytes 262176 | tf_op jit(solution)/shard_map/all_to_all | solution.py:31
  52.0 9.8 %all-to-all-start = ((f32[8,18,256]{2,1,0:T(8,128)}), f32[8,18,256]{2,1,0:T(8,128)S(1)}, u32[]{:S(2)}, u32[]{:S(2)}) async-start(f32[8,18,256]{2,1,0:T(8,128)} %copy.50), calls=%async_computation | async-start | bytes 393216 | tf_op jit(solution)/shard_map/all_to_all | solution.py:31
  61.8 0.7 broadcast_in_dim.32
  62.6 5.2 %all-to-all-done = f32[8,18,256]{2,1,0:T(8,128)S(1)} async-done(((f32[8,18,256]{2,1,0:T(8,128)}), f32[8,18,256]{2,1,0:T(8,128)S(1)}, u32[]{:S(2)}, u32[]{:S(2)}) %all-to-all-start) | async-done | bytes 147488 | tf_op jit(solution)/shard_map/all_to_all | solution.py:31
  67.7 5.4 %all-to-all-start.3 = ((f32[16,16,256]{2,1,0:T(8,128)}), f32[16,16,256]{2,1,0:T(8,128)S(1)}, u32[]{:S(2)}, u32[]{:S(2)}) async-start(f32[16,16,256]{2,1,0:T(8,128)} %broadcast_in_dim.32), calls=%async_computation.3 | async-start | bytes 524288 | tf_op jit(solution)/shard_map/all_to_all | solution.py:31
  73.2 0.1 add.66
  73.4 0.2 compare_reduce_fusion
  73.6 12.4 %all-to-all-done.3 = f32[16,16,256]{2,1,0:T(8,128)S(1)} async-done(((f32[16,16,256]{2,1,0:T(8,128)}), f32[16,16,256]{2,1,0:T(8,128)S(1)}, u32[]{:S(2)}, u32[]{:S(2)}) %all-to-all-start.3) | async-done | bytes 262176 | tf_op jit(solution)/shard_map/all_to_all | solution.py:31
  86.1 0.7 multiply_reduce_fusion
  86.7 1.3 broadcast_in_dim_broadcast_in_dim_broadcast_in_dim.3
  88.1 11.8 %all-to-all-start.4 = ((f32[32,8,128]{2,1,0:T(8,128)}), f32[32,8,128]{2,1,0:T(8,128)S(1)}, u32[]{:S(2)}, u32[]{:S(2)}) async-start(f32[32,8,128]{2,1,0:T(8,128)} %broadcast_in_dim_broadcast_in_dim_broadcast_in_dim.3), calls=%async_computation.4 | async-start | bytes 262144 | tf_op jit(solution)/shard_map/all_to_all | solution.py:31
  100.0 7.4 %all-to-all-done.4 = f32[32,8,128]{2,1,0:T(8,128)S(1)} async-done(((f32[32,8,128]{2,1,0:T(8,128)}), f32[32,8,128]{2,1,0:T(8,128)S(1)}, u32[]{:S(2)}, u32[]{:S(2)}) %all-to-all-start.4) | async-done | bytes 131104 | tf_op jit(solution)/shard_map/all_to_all | solution.py:31
  107.4 0.6 slice_reduce_fusion
  108.8 0.3 fusion.7
  109.1 22.7 %all_to_all.36 = bf16[16,48,256]{2,1,0:T(8,128)(2,1)S(1)} all-to-all(bf16[16,48,256]{2,1,0:T(8,128)(2,1)S(1)} %broadcast_in_dim.33), channel_id=1, replica_groups=mesh['z'=16,'x'=4,'c'=2,'layer'=4] {'z'}, dimensions={0} | all-to-all | bytes 786432 | tf_op jit(solution)/shard_map/all_to_all | solution.py:31
  131.8 0.3 convolution_convert_fusion
  132.1 10.2 %all-gather = bf16[1024,256]{1,0:T(8,128)(2,1)S(1)} all-gather(bf16[256,256]{1,0:T(8,128)(2,1)S(1)} %convolution_convert_fusion), channel_id=2, replica_groups=mesh['z'=16,'x'=4,'c'=2,'layer'=4] {'x'}, dimensions={0}, use_global_device_ids=true | all-gather | bytes 655360 | tf_op jit(solution)/shard_map/all_gather | solution.py:77
  142.3 11.9 %collective-permute-start = (bf16[4,256,256]{2,1,0:T(8,128)(2,1)S(1)}, bf16[4,256,256]{2,1,0:T(8,128)(2,1)S(1)}, u32[]{:S(2)}, u32[]{:S(2)}) collective-permute-start(bf16[4,256,256]{2,1,0:T(8,128)(2,1)S(1)} %bitcast.29), channel_id=1, source_target_pairs={{0,4},{4,0},{1,5},{5,1},{2,6},{6,2},{3,7},{7,3},{8,12},{12,8},{9,1... | collective-permute-start | bytes 1572872 | tf_op jit(solution)/shard_map/ppermute | solution.py:78
  154.3 0.7 copy.59
  155.1 3.3 %all-to-all-start.5 = ((f32[8,18,256]{2,1,0:T(8,128)}), f32[8,18,256]{2,1,0:T(8,128)S(1)}, u32[]{:S(2)}, u32[]{:S(2)}) async-start(f32[8,18,256]{2,1,0:T(8,128)} %copy.59), calls=%async_computation.5 | async-start | bytes 393216 | tf_op jit(solution)/shard_map/all_to_all | solution.py:31
  158.4 5.9 %all-to-all-done.5 = f32[8,18,256]{2,1,0:T(8,128)S(1)} async-done(((f32[8,18,256]{2,1,0:T(8,128)}), f32[8,18,256]{2,1,0:T(8,128)S(1)}, u32[]{:S(2)}, u32[]{:S(2)}) %all-to-all-start.5) | async-done | bytes 147488 | tf_op jit(solution)/shard_map/all_to_all | solution.py:31
  164.3 0.7 squeeze.12
  165.0 0.7 squeeze.13
  165.7 0.7 squeeze.14
  166.5 1.1 copy.63
  167.6 1.6 broadcast_in_dim_reshape.2
  (37 shorter events, 0.8 us)
Async XLA Ops:
  27.0 12.1 %copy-start = (f32[1,3,2,2048]{3,2,1,0:T(2,128)S(1)}, f32[1,3,2,2048]{3,2,1,0:T(2,128)}, u32[]{:S(2)}) copy-start(f32[1,3,2,2048]{3,2,1,0:T(2,128)} %param.9) | copy-start | bytes 147460
  27.0 12.1 %copy-start.1 = (f32[1,3,2,2048]{3,2,1,0:T(2,128)S(1)}, f32[1,3,2,2048]{3,2,1,0:T(2,128)}, u32[]{:S(2)}) copy-start(f32[1,3,2,2048]{3,2,1,0:T(2,128)} %param.8) | copy-start | bytes 147460
  27.0 12.1 %copy-start.2 = (f32[1,3,2,2048]{3,2,1,0:T(2,128)S(1)}, f32[1,3,2,2048]{3,2,1,0:T(2,128)}, u32[]{:S(2)}) copy-start(f32[1,3,2,2048]{3,2,1,0:T(2,128)} %param.7) | copy-start | bytes 147460
  27.9 24.2 %all-to-all-start.2 = ((f32[16,16,256]{2,1,0:T(8,128)}), f32[16,16,256]{2,1,0:T(8,128)S(1)}, u32[]{:S(2)}, u32[]{:S(2)}) async-start(f32[16,16,256]{2,1,0:T(8,128)} %bitcast.5), calls=%async_computation.2 | async-start | bytes 524288 | tf_op jit(solution)/shard_map/all_to_all | solution.py:31
  39.2 33.9 %copy-start.3 = (s32[1,128]{1,0:T(1,128)S(1)}, s32[1,128]{1,0:T(1,128)}, u32[]{:S(2)}) copy-start(s32[1,128]{1,0:T(1,128)} %param.11) | copy-start | bytes 1540
  39.2 33.9 %copy-start.4 = (s32[1,128]{1,0:T(1,128)S(1)}, s32[1,128]{1,0:T(1,128)}, u32[]{:S(2)}) copy-start(s32[1,128]{1,0:T(1,128)} %param.10) | copy-start | bytes 1540
  52.0 15.7 %all-to-all-start = ((f32[8,18,256]{2,1,0:T(8,128)}), f32[8,18,256]{2,1,0:T(8,128)S(1)}, u32[]{:S(2)}, u32[]{:S(2)}) async-start(f32[8,18,256]{2,1,0:T(8,128)} %copy.50), calls=%async_computation | async-start | bytes 393216 | tf_op jit(solution)/shard_map/all_to_all | solution.py:31
  67.7 18.3 %all-to-all-start.3 = ((f32[16,16,256]{2,1,0:T(8,128)}), f32[16,16,256]{2,1,0:T(8,128)S(1)}, u32[]{:S(2)}, u32[]{:S(2)}) async-start(f32[16,16,256]{2,1,0:T(8,128)} %broadcast_in_dim.32), calls=%async_computation.3 | async-start | bytes 524288 | tf_op jit(solution)/shard_map/all_to_all | solution.py:31
  88.1 19.3 %all-to-all-start.4 = ((f32[32,8,128]{2,1,0:T(8,128)}), f32[32,8,128]{2,1,0:T(8,128)S(1)}, u32[]{:S(2)}, u32[]{:S(2)}) async-start(f32[32,8,128]{2,1,0:T(8,128)} %broadcast_in_dim_broadcast_in_dim_broadcast_in_dim.3), calls=%async_computation.4 | async-start | bytes 262144 | tf_op jit(solution)/shard_map/all_to_all | solution.py:31
  142.3 24.0 %collective-permute-start = (bf16[4,256,256]{2,1,0:T(8,128)(2,1)S(1)}, bf16[4,256,256]{2,1,0:T(8,128)(2,1)S(1)}, u32[]{:S(2)}, u32[]{:S(2)}) collective-permute-start(bf16[4,256,256]{2,1,0:T(8,128)(2,1)S(1)} %bitcast.29), channel_id=1, source_target_pairs={{0,4},{4,0},{1,5},{5,1},{2,6},{6,2},{3,7},{7,3},{8,12},{12,8},{9,1... | collective-permute-start | bytes 1572872 | tf_op jit(solution)/shard_map/ppermute | solution.py:78
  155.1 9.2 %all-to-all-start.5 = ((f32[8,18,256]{2,1,0:T(8,128)}), f32[8,18,256]{2,1,0:T(8,128)S(1)}, u32[]{:S(2)}, u32[]{:S(2)}) async-start(f32[8,18,256]{2,1,0:T(8,128)} %copy.59), calls=%async_computation.5 | async-start | bytes 393216 | tf_op jit(solution)/shard_map/all_to_all | solution.py:31

commit v2 on v1

v2 whole, which is shorter than its diff:
```python
import jax
import jax.numpy as jnp
from jax import lax
from jax.sharding import Mesh
from jax.sharding import PartitionSpec as P

beta_one = 0.9
beta_two = 0.95
learn_rate = 0.0003
decay_rate = 0.1
adam_eps = 1e-08
step_number = 100.0

RING = "z"
PLANE = ("x", "c")
PLANE_SHAPE = (4, 2)
SLOT_ROWS = 8


def adamw(param, first, second, grad):
    first_new = beta_one * first + (1.0 - beta_one) * grad
    second_new = beta_two * second + (1.0 - beta_two) * grad * grad
    corr_one = 1.0 - beta_one**step_number
    corr_two = 1.0 - beta_two**step_number
    update = (
        first_new / corr_one / (jnp.sqrt(second_new / corr_two) + adam_eps) + decay_rate * param
    )
    return (param - learn_rate * update, first_new, second_new)


def exchange(chunks, axis):
    return lax.all_to_all(chunks, axis, 0, 0, tiled=True)


def share(value, axis):
    copies = jnp.broadcast_to(value[None], (lax.axis_size(axis), *value.shape))
    return exchange(lax.optimization_barrier(copies), axis)


def split_terms(value):
    high = lax.reduce_precision(value, 8, 7)
    middle = lax.reduce_precision(value - high, 8, 7)
    return [high, middle, value - high - middle]


def shards(micro_grads, master, moment_one, moment_two, owner, slot):
    rows, width = micro_grads.shape[2:]
    capacity, slab = master.shape[1:3]
    ring = lax.axis_size(RING)
    plane = lax.axis_size(PLANE)
    lines = capacity * slab
    wide = width // plane
    layers = lax.axis_size("layer")
    bf16 = jnp.bfloat16
    home = (owner[0] * SLOT_ROWS + slot[0] * slab)[:, None]
    home = (home + jnp.arange(slab, dtype=jnp.int32)[None, :]).reshape(rows)

    states = [*split_terms(master[0]), moment_one[0], moment_two[0]]
    states = jnp.stack([s.astype(bf16) for s in states]).reshape(len(states), lines, width)
    states = jnp.pad(states, ((0, 0), (0, SLOT_ROWS - lines), (0, 0)))
    kinds = states.shape[0]
    local = jnp.concatenate([micro_grads[0, 0], states.reshape(kinds * SLOT_ROWS, width)])
    local = local.reshape(rows + kinds * SLOT_ROWS, plane, wide).transpose(1, 0, 2)
    raw = exchange(local, PLANE)
    plane_sum = jnp.sum(raw[:, :rows].astype(jnp.float32), axis=0)
    strips = raw[:, rows:].reshape(plane, kinds, SLOT_ROWS, wide).transpose(1, 0, 2, 3)
    strips = strips.reshape(kinds, plane * SLOT_ROWS, wide)

    strips = lax.all_gather(strips, RING, axis=0, tiled=False)

    piece = jnp.sum(exchange(plane_sum.reshape(ring, rows // ring, wide), RING), axis=0)
    totals = share(piece, RING).reshape(rows, wide)

    line = jnp.arange(plane * SLOT_ROWS, dtype=jnp.int32)
    pick = (lax.axis_index(RING) * plane * SLOT_ROWS + line)[:, None] == home[None, :]
    sent = jnp.dot(pick.astype(jnp.float32), totals, precision=lax.Precision.HIGHEST)
    sent = jnp.where((line % SLOT_ROWS == lines)[:, None], jnp.sum(totals * totals), sent)
    sent = jnp.broadcast_to(
        sent.reshape(plane, 1, SLOT_ROWS, wide), (plane, layers, SLOT_ROWS, wide)
    )
    got = exchange(sent.reshape(plane * layers, SLOT_ROWS, wide), (*PLANE, "layer"))
    squares = jnp.sum(got[:, lines, 0])
    grad_rms = jnp.sqrt(squares / (layers * rows * width) + 1e-06)
    clip_factor = jnp.minimum(1.0, 1.0 / grad_rms)

    strips = strips.transpose(1, 0, 2, 3).reshape(kinds, ring * plane * SLOT_ROWS, wide)
    place = home[:, None] == jnp.arange(strips.shape[1], dtype=jnp.int32)[None, :]
    place = place.astype(bf16)
    placed = [jnp.dot(place, s, preferred_element_type=jnp.float32) for s in strips]
    placed = [placed[0] + placed[1] + placed[2], placed[3], placed[4]]
    mine = adamw(*placed, totals * clip_factor)[0].astype(bf16)
    halves = share(mine, "x")
    others = lax.ppermute(halves, "c", [(0, 1), (1, 0)])
    first_core = lax.axis_index("c") == 0
    pair = [jnp.where(first_core, halves, others), jnp.where(first_core, others, halves)]
    weights = jnp.stack(pair, axis=1).transpose(2, 0, 1, 3).reshape(rows, width)

    own = got.reshape(plane, layers, SLOT_ROWS, wide)
    own = lax.dynamic_index_in_dim(own, lax.axis_index("layer"), 1, keepdims=False)
    own = own[:, :lines].transpose(1, 0, 2).reshape(capacity, slab, width) * clip_factor
    new = adamw(master[0], moment_one[0], moment_two[0], own)
    my_slots = lax.axis_index((RING, *PLANE)) * SLOT_ROWS
    my_slots = my_slots + slab * jnp.arange(capacity, dtype=jnp.int32)
    keep = jnp.any(home[None, :] == my_slots[:, None], axis=1)[:, None, None]
    old = (master[0], moment_one[0], moment_two[0])
    new = [jnp.where(keep, n, o)[None] for n, o in zip(new, old, strict=True)]
    return (*new, weights[None], grad_rms)


def solution(mesh):
    ring = mesh.shape["dp"] // (PLANE_SHAPE[0] * PLANE_SHAPE[1])
    devices = mesh.devices.reshape(ring, *PLANE_SHAPE, mesh.shape["layer"])
    split = Mesh(devices, (RING, *PLANE, "layer"))
    dp = (RING, *PLANE)
    in_specs = (
        P("layer", dp, None, None),
        P("layer", dp, None, None),
        P("layer", dp, None, None),
        P("layer", dp, None, None),
        P("layer", None),
        P("layer", None),
    )
    out_specs = (
        P("layer", dp, None, None),
        P("layer", dp, None, None),
        P("layer", dp, None, None),
        P("layer", None, None),
        P(),
    )
    return jax.shard_map(
        shards, mesh=split, in_specs=in_specs, out_specs=out_specs, check_vma=False
    )
```

time: 171 us -> 157 us (0.918)
  starting transfers between devices: 53.4 us -> 25.9 us
  waiting for transfers between devices: 42.9 us -> 28.8 us
  between operations: 2.83 us -> 16.3 us
  blocking collectives: 57.3 us -> 68.8 us
  other arithmetic: 2.69 us -> 5.55 us
  local copies, waits for them, and re-layouts: 10.7 us -> 8.02 us
  matrix products: 0.61 us -> 2.75 us
    all_to_all x5 -> x2, starting transfers between devices: 41.5 us -> 16.2 us  [exchange(): return lax.all_to_all(chunks, axis, 0, 0, tiled=True)]
    all_to_all x2 -> x3, blocking collectives: 47.1 us -> 68.8 us  [exchange(): return lax.all_to_all(chunks, axis, 0, 0, tiled=True)]
    all_to_all x5 -> x2, waiting for transfers between devices: 42.8 us -> 24.1 us  [exchange(): return lax.all_to_all(chunks, axis, 0, 0, tiled=True)]
    all_gather x1 -> x0, blocking collectives: 10.2 us -> none  [shards(): halves = lax.all_gather(placed, 'x', axis=0, tiled=False)]
    all_gather x0 -> x1, waiting for transfers between devices: none -> 4.18 us  [shards(): strips = lax.all_gather(strips, RING, axis=0, tiled=False)]
    convert_element_type x0 -> x3, other arithmetic: none -> 2.57 us  [shards(): s.astype(bf16)]
    ppermute x1, starting transfers between devices: 11.9 us -> 9.61 us  [shards(): others = lax.ppermute(halves, 'c', [(0, 1), (1, 0)])]
    squeeze x3 -> x1, local copies, waits for them, and re-layouts: 1.96 us -> 0.01 us  [shards(): lax.dynamic_index_in_dim(own, lax.axis_index('layer'), 1, keepdims=False)]
  transfers between devices with their start and end apart: 6 -> 4, of which waited for: 5 -> 4; matrix products, arithmetic and copies ran while one was open for 3% -> 3% of each run, Pallas kernels for 0% -> 0%
where the time goes in v2:
time: 157 us; the launch traced here: 156 us
  blocking collectives  68.8 us (44%)
  waiting for transfers between devices  28.8 us (18%)
  starting transfers between devices  25.9 us (16%)
  between operations  16.3 us (10%)
  local copies, waits for them, and re-layouts  8.02 us (5%)
  other arithmetic  5.55 us (4%)
  matrix products  2.75 us (2%)
    all_to_all x3, blocking collectives, exchange(): return lax.all_to_all(chunks, axis, 0, 0, tiled=True)  68.8 us
    all_to_all x2, waiting for transfers between devices, exchange(): return lax.all_to_all(chunks, axis, 0, 0, tiled=True)  24.1 us
    all_to_all x2, starting transfers between devices, exchange(): return lax.all_to_all(chunks, axis, 0, 0, tiled=True)  16.2 us
    ppermute x1, starting transfers between devices, shards(): others = lax.ppermute(halves, 'c', [(0, 1), (1, 0)])  9.61 us
    all_gather x1, waiting for transfers between devices, shards(): strips = lax.all_gather(strips, RING, axis=0, tiled=False)  4.18 us
  transfers between devices with their start and end apart: 4, of which 4 were waited for; matrix products, arithmetic and copies ran while one was open for 3% of the time, Pallas kernels for 0%

profile of v2, /device:TPU:1, one launch (start us, length us, event | category | flops | bytes accessed | tf_op | source)
XLA Modules:
  0.0 156.1 jit_solution(1796185071028147023)
XLA Ops:
  7.2 0.9 convert_element_type.33
  8.1 0.8 convert_element_type.34
  9.0 0.9 fusion.20
  10.1 0.3 copy.40
  10.4 0.5 copy.39
  11.1 0.8 copy.41
  11.8 26.2 %all_to_all.25 = bf16[8,296,256]{2,1,0:T(8,128)(2,1)S(1)} all-to-all(bf16[8,296,256]{2,1,0:T(8,128)(2,1)S(1)} %copy.41), channel_id=1, replica_groups=mesh['z'=16,'x'=4,'c'=2,'layer'=4] {'x','c'}, dimensions={0} | all-to-all | bytes 2424832 | tf_op jit(solution)/shard_map/all_to_all | solution.py:32
  38.1 0.7 copy_bitcast_fusion
  38.9 24.0 %all_to_all.26 = f32[16,16,256]{2,1,0:T(8,128)S(1)} all-to-all(f32[16,16,256]{2,1,0:T(8,128)S(1)} %bitcast.52), channel_id=1, replica_groups=mesh['z'=16,'x'=4,'c'=2,'layer'=4] {'z'}, dimensions={0} | all-to-all | bytes 524288 | tf_op jit(solution)/shard_map/all_to_all | solution.py:32
  62.9 0.7 broadcast_in_dim.57
  63.7 12.8 %all-to-all-start.2 = ((f32[16,16,256]{2,1,0:T(8,128)}), f32[16,16,256]{2,1,0:T(8,128)S(1)}, u32[]{:S(2)}, u32[]{:S(2)}) async-start(f32[16,16,256]{2,1,0:T(8,128)} %broadcast_in_dim.57), calls=%async_computation.2 | async-start | bytes 524288 | tf_op jit(solution)/shard_map/all_to_all | solution.py:32
  76.7 17.4 %all-to-all-done.2 = f32[16,16,256]{2,1,0:T(8,128)S(1)} async-done(((f32[16,16,256]{2,1,0:T(8,128)}), f32[16,16,256]{2,1,0:T(8,128)S(1)}, u32[]{:S(2)}, u32[]{:S(2)}) %all-to-all-start.2) | async-done | bytes 262176 | tf_op jit(solution)/shard_map/all_to_all | solution.py:32
  94.2 0.7 multiply_reduce_fusion
  94.8 0.9 fusion.11
  95.7 18.6 %all_to_all.27 = f32[32,8,256]{2,1,0:T(8,128)S(1)} all-to-all(f32[32,8,256]{2,1,0:T(8,128)S(1)} %bitcast.53), channel_id=1, replica_groups=mesh['z'=16,'x'=4,'c'=2,'layer'=4] {'x','c','layer'}, dimensions={0} | all-to-all | bytes 524288 | tf_op jit(solution)/shard_map/all_to_all | solution.py:32
  114.3 0.6 slice_reduce_fusion
  115.7 4.2 %all-gather.2.cloned.1.call-done = bf16[16,5,64,256]{3,2,1,0:T(8,128)(2,1)} async-done(((bf16[1,5,64,256]{3,2,1,0:T(8,128)(2,1)}), bf16[16,5,64,256]{3,2,1,0:T(8,128)(2,1)}) %all-gather.2.cloned.1.call-update) | async-done | bytes 2621456 | tf_op jit(solution)/shard_map/all_gather | solution.py:69
  119.9 1.9 %fusion.25 = (bf16[1,16,64,256]{3,2,0,1:T(8,128)(2,1)S(1)}, bf16[1,16,64,256]{3,2,0,1:T(8,128)(2,1)S(1)}, bf16[1,16,64,256]{3,2,0,1:T(8,128)(2,1)S(1)}, bf16[1,1...) fusion(bf16[5,16,64,256]{3,2,0,1:T(8,128)(2,1)} %bitcast.46), kind=kLoop, calls=%fused_computation.63 | loop fusion | bytes 5242880 | tf_op jit(solution)/shard_map/unstack | solution.py:89
  121.7 0.3 fusion.12
  122.1 0.4 fusion.9
  122.5 0.4 convolution_add_fusion.1
  122.9 0.4 convolution_add_fusion
  123.2 0.4 fusion.10
  123.7 0.8 broadcast_in_dim.61
  124.5 3.5 %all-to-all-start.4 = ((bf16[4,256,256]{2,1,0:T(8,128)(2,1)}), bf16[4,256,256]{2,1,0:T(8,128)(2,1)S(1)}, u32[]{:S(2)}, u32[]{:S(2)}) async-start(bf16[4,256,256]{2,1,0:T(8,128)(2,1)} %broadcast_in_dim.61), calls=%async_computation.4 | async-start | bytes 1048576 | tf_op jit(solution)/shard_map/all_to_all | solution.py:32
  128.0 0.2 compare_reduce_fusion
  128.2 6.7 %all-to-all-done.4 = bf16[4,256,256]{2,1,0:T(8,128)(2,1)S(1)} async-done(((bf16[4,256,256]{2,1,0:T(8,128)(2,1)}), bf16[4,256,256]{2,1,0:T(8,128)(2,1)S(1)}, u32[]{:S(2)}, u32[]{:S(2)}) %all-to-all-start.4) | async-done | bytes 524320 | tf_op jit(solution)/shard_map/all_to_all | solution.py:32
  134.9 9.6 %collective-permute-start = (bf16[4,256,256]{2,1,0:T(8,128)(2,1)S(1)}, bf16[4,256,256]{2,1,0:T(8,128)(2,1)S(1)}, u32[]{:S(2)}, u32[]{:S(2)}) collective-permute-start(bf16[4,256,256]{2,1,0:T(8,128)(2,1)S(1)} %all-to-all-done.4), channel_id=1, source_target_pairs={{0,4},{4,0},{1,5},{5,1},{2,6},{6,2},{3,7},{7,3},{8,12},{12,8},{9,1... | collective-permute-start | bytes 1572872 | tf_op jit(solution)/shard_map/ppermute | solution.py:93
  144.6 0.9 broadcast_select_fusion
  145.5 0.5 collective-permute-done
  146.2 0.5 copy.46
  146.7 1.4 copy.47
  (42 shorter events, 1.1 us)
Async XLA Ops:
  7.2 3.2 %copy-start = (bf16[1,1,256,2048]{3,2,1,0:T(8,128)(2,1)S(1)}, bf16[1,1,256,2048]{3,2,1,0:T(8,128)(2,1)}, u32[]{:S(2)}) copy-start(bf16[1,1,256,2048]{3,2,1,0:T(8,128)(2,1)} %param.6) | copy-start | bytes 3145732
  7.2 112.7 %all-gather.2.cloned.1.call-start = ((), (), s32[]{:S(2)}) async-start(), calls=%async_computation.5 | async-start | bytes 2785280 | tf_op jit(solution)/shard_map/all_gather | solution.py:69
  38.7 37.7 %copy-start.4 = (s32[1,128]{1,0:T(1,128)S(1)}, s32[1,128]{1,0:T(1,128)}, u32[]{:S(2)}) copy-start(s32[1,128]{1,0:T(1,128)} %param.11) | copy-start | bytes 1540
  38.7 37.7 %copy-start.5 = (s32[1,128]{1,0:T(1,128)S(1)}, s32[1,128]{1,0:T(1,128)}, u32[]{:S(2)}) copy-start(s32[1,128]{1,0:T(1,128)} %param.10) | copy-start | bytes 1540
  63.7 30.5 %all-to-all-start.2 = ((f32[16,16,256]{2,1,0:T(8,128)}), f32[16,16,256]{2,1,0:T(8,128)S(1)}, u32[]{:S(2)}, u32[]{:S(2)}) async-start(f32[16,16,256]{2,1,0:T(8,128)} %broadcast_in_dim.57), calls=%async_computation.2 | async-start | bytes 524288 | tf_op jit(solution)/shard_map/all_to_all | solution.py:32
  123.6 21.0 %copy-start.1 = (f32[1,3,2,2048]{3,2,1,0:T(2,128)S(1)}, f32[1,3,2,2048]{3,2,1,0:T(2,128)}, u32[]{:S(2)}) copy-start(f32[1,3,2,2048]{3,2,1,0:T(2,128)} %param.9) | copy-start | bytes 147460
  123.6 20.9 %copy-start.2 = (f32[1,3,2,2048]{3,2,1,0:T(2,128)S(1)}, f32[1,3,2,2048]{3,2,1,0:T(2,128)}, u32[]{:S(2)}) copy-start(f32[1,3,2,2048]{3,2,1,0:T(2,128)} %param.8) | copy-start | bytes 147460
  123.6 20.9 %copy-start.3 = (f32[1,3,2,2048]{3,2,1,0:T(2,128)S(1)}, f32[1,3,2,2048]{3,2,1,0:T(2,128)}, u32[]{:S(2)}) copy-start(f32[1,3,2,2048]{3,2,1,0:T(2,128)} %param.7) | copy-start | bytes 147460
  124.5 10.4 %all-to-all-start.4 = ((bf16[4,256,256]{2,1,0:T(8,128)(2,1)}), bf16[4,256,256]{2,1,0:T(8,128)(2,1)S(1)}, u32[]{:S(2)}, u32[]{:S(2)}) async-start(bf16[4,256,256]{2,1,0:T(8,128)(2,1)} %broadcast_in_dim.61), calls=%async_computation.4 | async-start | bytes 1048576 | tf_op jit(solution)/shard_map/all_to_all | solution.py:32
  134.9 11.1 %collective-permute-start = (bf16[4,256,256]{2,1,0:T(8,128)(2,1)S(1)}, bf16[4,256,256]{2,1,0:T(8,128)(2,1)S(1)}, u32[]{:S(2)}, u32[]{:S(2)}) collective-permute-start(bf16[4,256,256]{2,1,0:T(8,128)(2,1)S(1)} %all-to-all-done.4), channel_id=1, source_target_pairs={{0,4},{4,0},{1,5},{5,1},{2,6},{6,2},{3,7},{7,3},{8,12},{12,8},{9,1... | collective-permute-start | bytes 1572872 | tf_op jit(solution)/shard_map/ppermute | solution.py:93
Sparse Core Ops, SparseCore 0:
  38.9 80.9 all-gather.1

commit v3 on v2

--- a/solution.py
+++ b/solution.py
@@ -1,6 +1,8 @@
 import jax
 import jax.numpy as jnp
 from jax import lax
+from jax.experimental import pallas as pl
+from jax.experimental.pallas import tpu as pltpu
 from jax.sharding import Mesh
 from jax.sharding import PartitionSpec as P
 
@@ -15,6 +17,7 @@
 PLANE = ("x", "c")
 PLANE_SHAPE = (4, 2)
 SLOT_ROWS = 8
+KINDS = 5
 
 
 def adamw(param, first, second, grad):
@@ -37,10 +40,72 @@
     return exchange(lax.optimization_barrier(copies), axis)
 
 
-def split_terms(value):
-    high = lax.reduce_precision(value, 8, 7)
-    middle = lax.reduce_precision(value - high, 8, 7)
-    return [high, middle, value - high - middle]
+def split_kernel(grads, master, first, second, out, rows):
+    plane, _, wide = out.shape
+    count = grads.shape[0]
+    for k in range(plane):
+        out[k, :count, :] = grads[:, k * wide : (k + 1) * wide]
+    rows[...] = jnp.zeros_like(rows)
+    capacity, slab, _ = master.shape
+    for i, state in enumerate((master, first, second)):
+        for s in range(capacity):
+            rows[i, s * slab : (s + 1) * slab, :] = state[s]
+    value = rows[0]
+    high = value.astype(jnp.bfloat16)
+    rest = value - high.astype(jnp.float32)
+    middle = rest.astype(jnp.bfloat16)
+    low = (rest - middle.astype(jnp.float32)).astype(jnp.bfloat16)
+    terms = (high, middle, low, rows[1].astype(jnp.bfloat16), rows[2].astype(jnp.bfloat16))
+    for t, term in enumerate(terms):
+        at = count + t * SLOT_ROWS
+        for k in range(plane):
+            out[k, at : at + SLOT_ROWS, :] = term[:, k * wide : (k + 1) * wide]
+
+
+def split(grads, master, first, second, plane):
+    count, width = grads.shape
+    return pl.pallas_call(
+        split_kernel,
+        out_shape=jax.ShapeDtypeStruct(
+            (plane, count + KINDS * SLOT_ROWS, width // plane), grads.dtype
+        ),
+        in_specs=[pl.BlockSpec(memory_space=pltpu.VMEM)] * 4,
+        out_specs=pl.BlockSpec(memory_space=pltpu.VMEM),
+        scratch_shapes=[pltpu.VMEM((3, SLOT_ROWS, width), jnp.float32)],
+        name="split",
+    )(grads, master, first, second)
+
+
+def join_kernel(core, mine, other, out):
+    count, _, wide = mine.shape
+
+    def put(first, second):
+        for x in range(count):
+            out[:, 2 * x * wide : (2 * x + 1) * wide] = first[x]
+            out[:, (2 * x + 1) * wide : (2 * x + 2) * wide] = second[x]
+
+    @pl.when(core[0] == 0)
+    def _():
+        put(mine, other)
+
+    @pl.when(core[0] == 1)
+    def _():
+        put(other, mine)
+
+
+def join(mine, other):
+    count, rows, wide = mine.shape
+    return pl.pallas_call(
+        join_kernel,
+        out_shape=jax.ShapeDtypeStruct((rows, 2 * count * wide), mine.dtype),
+        in_specs=[
+            pl.BlockSpec(memory_space=pltpu.SMEM),
+            pl.BlockSpec(memory_space=pltpu.VMEM),
+            pl.BlockSpec(memory_space=pltpu.VMEM),
+        ],
+        out_specs=pl.BlockSpec(memory_space=pltpu.VMEM),
+        name="join",
+    )(lax.axis_index("c").astype(jnp.int32).reshape(1), mine, other)
 
 
 def shards(micro_grads, master, moment_one, moment_two, owner, slot):
@@ -54,19 +119,12 @@
     bf16 = jnp.bfloat16
     home = (owner[0] * SLOT_ROWS + slot[0] * slab)[:, None]
     home = (home + jnp.arange(slab, dtype=jnp.int32)[None, :]).reshape(rows)
+    tight = home // SLOT_ROWS * lines + home % SLOT_ROWS
 
-    states = [*split_terms(master[0]), moment_one[0], moment_two[0]]
-    states = jnp.stack([s.astype(bf16) for s in states]).reshape(len(states), lines, width)
-    states = jnp.pad(states, ((0, 0), (0, SLOT_ROWS - lines), (0, 0)))
-    kinds = states.shape[0]
-    local = jnp.concatenate([micro_grads[0, 0], states.reshape(kinds * SLOT_ROWS, width)])
-    local = local.reshape(rows + kinds * SLOT_ROWS, plane, wide).transpose(1, 0, 2)
-    raw = exchange(local, PLANE)
+    raw = exchange(split(micro_grads[0, 0], master[0], moment_one[0], moment_two[0], plane), PLANE)
     plane_sum = jnp.sum(raw[:, :rows].astype(jnp.float32), axis=0)
-    strips = raw[:, rows:].reshape(plane, kinds, SLOT_ROWS, wide).transpose(1, 0, 2, 3)
-    strips = strips.reshape(kinds, plane * SLOT_ROWS, wide)
-
-    strips = lax.all_gather(strips, RING, axis=0, tiled=False)
+    strips = raw[:, rows:].reshape(plane, KINDS, SLOT_ROWS, wide)[:, :, :lines]
+    strips = strips.transpose(1, 0, 2, 3).reshape(KINDS, plane * lines, wide).astype(jnp.float32)
 
     piece = jnp.sum(exchange(plane_sum.reshape(ring, rows // ring, wide), RING), axis=0)
     totals = share(piece, RING).reshape(rows, wide)
@@ -83,17 +141,16 @@
     grad_rms = jnp.sqrt(squares / (layers * rows * width) + 1e-06)
     clip_factor = jnp.minimum(1.0, 1.0 / grad_rms)
 
-    strips = strips.transpose(1, 0, 2, 3).reshape(kinds, ring * plane * SLOT_ROWS, wide)
-    place = home[:, None] == jnp.arange(strips.shape[1], dtype=jnp.int32)[None, :]
-    place = place.astype(bf16)
-    placed = [jnp.dot(place, s, preferred_element_type=jnp.float32) for s in strips]
-    placed = [placed[0] + placed[1] + placed[2], placed[3], placed[4]]
-    mine = adamw(*placed, totals * clip_factor)[0].astype(bf16)
-    halves = share(mine, "x")
-    others = lax.ppermute(halves, "c", [(0, 1), (1, 0)])
-    first_core = lax.axis_index("c") == 0
-    pair = [jnp.where(first_core, halves, others), jnp.where(first_core, others, halves)]
-    weights = jnp.stack(pair, axis=1).transpose(2, 0, 1, 3).reshape(rows, width)
+    line = jnp.arange(plane * lines, dtype=jnp.int32)
+    pick = (lax.axis_index(RING) * plane * lines + line)[:, None] == tight[None, :]
+    grads = jnp.dot(pick.astype(jnp.float32), totals, precision=lax.Precision.HIGHEST)
+    param = strips[0] + strips[1] + strips[2]
+    param = adamw(param, strips[3], strips[4], grads * clip_factor)[0].astype(bf16)
+    params = share(param, RING).reshape(ring * plane * lines, wide)
+    place = tight[:, None] == jnp.arange(params.shape[0], dtype=jnp.int32)[None, :]
+    placed = jnp.dot(place.astype(bf16), params, preferred_element_type=jnp.float32)
+    halves = share(placed.astype(bf16), "x")
+    weights = join(halves, lax.ppermute(halves, "c", [(0, 1), (1, 0)]))
 
     own = got.reshape(plane, layers, SLOT_ROWS, wide)
     own = lax.dynamic_index_in_dim(own, lax.axis_index("layer"), 1, keepdims=False)
@@ -110,7 +167,7 @@
 def solution(mesh):
     ring = mesh.shape["dp"] // (PLANE_SHAPE[0] * PLANE_SHAPE[1])
     devices = mesh.devices.reshape(ring, *PLANE_SHAPE, mesh.shape["layer"])
-    split = Mesh(devices, (RING, *PLANE, "layer"))
+    split_mesh = Mesh(devices, (RING, *PLANE, "layer"))
     dp = (RING, *PLANE)
     in_specs = (
         P("layer", dp, None, None),
@@ -128,5 +185,5 @@
         P(),
     )
     return jax.shard_map(
-        shards, mesh=split, in_specs=in_specs, out_specs=out_specs, check_vma=False
+        shards, mesh=split_mesh, in_specs=in_specs, out_specs=out_specs, check_vma=False
     )

time: 157 us -> 155 us (0.987)
  starting transfers between devices: 25.9 us -> 46.6 us
  blocking collectives: 68.8 us -> 50.3 us
  between operations: 16.3 us -> 2.79 us
  waiting for transfers between devices: 28.8 us -> 41.5 us
  Pallas kernels: 0 us -> 4.73 us
  local copies, waits for them, and re-layouts: 8.02 us -> 3.35 us
  other arithmetic: 5.55 us -> 3.42 us
    all_to_all x2 -> x4, starting transfers between devices: 16.2 us -> 36.6 us  [exchange(): return lax.all_to_all(chunks, axis, 0, 0, tiled=True)]
    all_to_all x3 -> x2, blocking collectives: 68.8 us -> 50.3 us  [exchange(): return lax.all_to_all(chunks, axis, 0, 0, tiled=True)]
    all_to_all x2 -> x4, waiting for transfers between devices: 24.1 us -> 41 us  [exchange(): return lax.all_to_all(chunks, axis, 0, 0, tiled=True)]
    pallas_call x0 -> x2, Pallas kernels: none -> 4.73 us  [the longest x1 2.43 us: split(): pl.pallas_call(split_kernel, out_shape=jax.ShapeDtypeStruct((plane, count...]
    all_gather x1 -> x0, waiting for transfers between devices: 4.18 us -> none  [shards(): strips = lax.all_gather(strips, RING, axis=0, tiled=False)]
    another operation x8 -> x0, local copies, waits for them, and re-layouts: 2.62 us -> none  [the longest x1 1.86 us: shards(): placed = [jnp.dot(place, s, preferred_element_type=jnp.float32) for s in...]
    convert_element_type x3 -> x1, other arithmetic: 2.57 us -> 0.02 us  [shards(): strips.transpose(1, 0, 2, 3).reshape(KINDS, plane * lines, wide)]
  transfers between devices with their start and end apart: 4 -> 5, of which waited for: 4 -> 5; matrix products, arithmetic and copies ran while one was open for 3% -> 1% of each run, Pallas kernels for 0% -> 0%
where the time goes in v3:
time: 155 us; the launch traced here: 154 us
  blocking collectives  50.3 us (32%)
  starting transfers between devices  46.6 us (30%)
  waiting for transfers between devices  41.5 us (27%)
  Pallas kernels  4.73 us (3%)
  other arithmetic  3.42 us (2%)
  local copies, waits for them, and re-layouts  3.35 us (2%)
  between operations  2.79 us (2%)
    all_to_all x2, blocking collectives, exchange(): return lax.all_to_all(chunks, axis, 0, 0, tiled=True)  50.3 us
    all_to_all x4, waiting for transfers between devices, exchange(): return lax.all_to_all(chunks, axis, 0, 0, tiled=True)  41 us
    all_to_all x4, starting transfers between devices, exchange(): return lax.all_to_all(chunks, axis, 0, 0, tiled=True)  36.6 us
    ppermute x1, starting transfers between devices, shards(): weights = join(halves, lax.ppermute(halves, 'c', [(0, 1), (1, 0)]))  10 us
  transfers between devices with their start and end apart: 5, of which 5 were waited for; matrix products, arithmetic and copies ran while one was open for 1% of the time, Pallas kernels for 0%

profile of v3, /device:TPU:1, one launch (start us, length us, event | category | flops | bytes accessed | tf_op | source)
XLA Modules:
  0.0 154.2 jit_solution(8405268032918278492)
XLA Ops:
  0.6 2.4 %split.1 = bf16[8,296,256]{2,1,0:T(8,128)(2,1)} custom-call(bf16[256,2048]{1,0:T(8,128)(2,1)} %bitcast.28, f32[3,2,2048]{2,1,0:T(2,128)} %bitcast.33, f32[3,2,2048]{2,1,0:T(2,128)} %bitcast.34, f32[3,2,2048]{2,1,0:T(2,128)} %bitcast.32), custom_call_target="tpu_custom_call" | custom-call | tf_op jit(solution)/shard_map/split/pallas_call | solution.py:67
  3.1 27.3 %all_to_all.30 = bf16[8,296,256]{2,1,0:T(8,128)(2,1)S(1)} all-to-all(bf16[8,296,256]{2,1,0:T(8,128)(2,1)} %split.1), channel_id=1, replica_groups=mesh['z'=16,'x'=4,'c'=2,'layer'=4] {'x','c'}, dimensions={0} | all-to-all | bytes 2424832 | tf_op jit(solution)/shard_map/all_to_all | solution.py:35
  30.4 0.8 convert_reduce_fusion
  31.2 10.4 %all-to-all-start.1 = ((f32[16,16,256]{2,1,0:T(8,128)}), f32[16,16,256]{2,1,0:T(8,128)S(1)}, u32[]{:S(2)}, u32[]{:S(2)}) async-start(f32[16,16,256]{2,1,0:T(8,128)} %bitcast.5), calls=%async_computation.1 | async-start | bytes 524288 | tf_op jit(solution)/shard_map/all_to_all | solution.py:35
  41.6 0.0 copy-done.5
  41.6 12.9 %all-to-all-done.1 = f32[16,16,256]{2,1,0:T(8,128)S(1)} async-done(((f32[16,16,256]{2,1,0:T(8,128)}), f32[16,16,256]{2,1,0:T(8,128)S(1)}, u32[]{:S(2)}, u32[]{:S(2)}) %all-to-all-start.1) | async-done | bytes 262176 | tf_op jit(solution)/shard_map/all_to_all | solution.py:35
  54.6 0.7 broadcast_in_dim.40
  55.3 11.1 %all-to-all-start.2 = ((f32[16,16,256]{2,1,0:T(8,128)}), f32[16,16,256]{2,1,0:T(8,128)S(1)}, u32[]{:S(2)}, u32[]{:S(2)}) async-start(f32[16,16,256]{2,1,0:T(8,128)} %broadcast_in_dim.40), calls=%async_computation.2 | async-start | bytes 524288 | tf_op jit(solution)/shard_map/all_to_all | solution.py:35
  66.4 0.1 iota_add_fusion
  66.5 0.1 add.177
  66.7 12.8 %all-to-all-done.2 = f32[16,16,256]{2,1,0:T(8,128)S(1)} async-done(((f32[16,16,256]{2,1,0:T(8,128)}), f32[16,16,256]{2,1,0:T(8,128)S(1)}, u32[]{:S(2)}, u32[]{:S(2)}) %all-to-all-start.2) | async-done | bytes 262176 | tf_op jit(solution)/shard_map/all_to_all | solution.py:35
  79.5 0.7 multiply_reduce_fusion
  80.2 0.9 fusion
  81.1 0.7 broadcast_in_dim.72
  81.8 11.6 %all-to-all-start.3 = ((f32[32,8,256]{2,1,0:T(8,128)}), f32[32,8,256]{2,1,0:T(8,128)S(1)}, u32[]{:S(2)}, u32[]{:S(2)}) async-start(f32[32,8,256]{2,1,0:T(8,128)} %bitcast.8), calls=%async_computation.3 | async-start | bytes 524288 | tf_op jit(solution)/shard_map/all_to_all | solution.py:35
  93.5 8.7 %all-to-all-done.3 = f32[32,8,256]{2,1,0:T(8,128)S(1)} async-done(((f32[32,8,256]{2,1,0:T(8,128)}), f32[32,8,256]{2,1,0:T(8,128)S(1)}, u32[]{:S(2)}, u32[]{:S(2)}) %all-to-all-start.3) | async-done | bytes 262176 | tf_op jit(solution)/shard_map/all_to_all | solution.py:35
  102.2 0.6 slice_reduce_fusion
  103.5 0.3 subtract_convert_fusion
  103.9 23.1 %all_to_all.31 = bf16[16,48,256]{2,1,0:T(8,128)(2,1)S(1)} all-to-all(bf16[16,48,256]{2,1,0:T(8,128)(2,1)S(1)} %broadcast_in_dim.73), channel_id=1, replica_groups=mesh['z'=16,'x'=4,'c'=2,'layer'=4] {'z'}, dimensions={0} | all-to-all | bytes 786432 | tf_op jit(solution)/shard_map/all_to_all | solution.py:35
  126.9 0.3 convolution_convert_fusion
  127.2 0.0 copy-start.2
  127.3 0.0 copy-start.3
  127.3 0.0 copy-start.4
  127.3 0.8 broadcast_in_dim.74
  128.1 3.5 %all-to-all-start.5 = ((bf16[4,256,256]{2,1,0:T(8,128)(2,1)}), bf16[4,256,256]{2,1,0:T(8,128)(2,1)S(1)}, u32[]{:S(2)}, u32[]{:S(2)}) async-start(bf16[4,256,256]{2,1,0:T(8,128)(2,1)} %broadcast_in_dim.74), calls=%async_computation.5 | async-start | bytes 1048576 | tf_op jit(solution)/shard_map/all_to_all | solution.py:35
  131.6 0.2 compare_reduce_fusion
  131.8 6.7 %all-to-all-done.5.mine = bf16[4,256,256]{2,1,0:T(8,128)(2,1)S(1)} async-done(((bf16[4,256,256]{2,1,0:T(8,128)(2,1)}), bf16[4,256,256]{2,1,0:T(8,128)(2,1)S(1)}, u32[]{:S(2)}, u32[]{:S(2)}) %all-to-all-start.5) | async-done | bytes 524320 | tf_op jit(solution)/shard_map/all_to_all | solution.py:35
  138.5 10.0 %collective-permute-start = (bf16[4,256,256]{2,1,0:T(8,128)(2,1)S(1)}, bf16[4,256,256]{2,1,0:T(8,128)(2,1)S(1)}, u32[]{:S(2)}, u32[]{:S(2)}) collective-permute-start(bf16[4,256,256]{2,1,0:T(8,128)(2,1)S(1)} %all-to-all-done.5.mine), channel_id=1, source_target_pairs={{0,4},{4,0},{1,5},{5,1},{2,6},{6,2},{3,7},{7,3},{8,12},{12,8},{9,1... | collective-permute-start | bytes 1572872 | tf_op jit(solution)/shard_map/ppermute | solution.py:153
  148.6 0.9 broadcast_select_fusion
  149.5 0.5 collective-permute-done.other
  150.0 0.8 copy-done.1
  150.8 2.3 %join.1 = bf16[256,2048]{1,0:T(8,128)(2,1)} custom-call(s32[1]{0:T(128)} %bitcast.12.core, bf16[4,256,256]{2,1,0:T(8,128)(2,1)} %copy-done, bf16[4,256,256]{2,1,0:T(8,128)(2,1)} %copy-done.1), custom_call_target="tpu_custom_call" | custom-call | tf_op jit(solution)/shard_map/join/pallas_call | solution.py:98
  (27 shorter events, 0.3 us)
Async XLA Ops:
  30.4 11.2 %copy-start.5 = (s32[1,128]{1,0:T(1,128)S(1)}, s32[1,128]{1,0:T(1,128)}, u32[]{:S(2)}) copy-start(s32[1,128]{1,0:T(1,128)} %param.11) | copy-start | bytes 1540
  30.4 11.2 %copy-start.6 = (s32[1,128]{1,0:T(1,128)S(1)}, s32[1,128]{1,0:T(1,128)}, u32[]{:S(2)}) copy-start(s32[1,128]{1,0:T(1,128)} %param.10) | copy-start | bytes 1540
  31.2 23.3 %all-to-all-start.1 = ((f32[16,16,256]{2,1,0:T(8,128)}), f32[16,16,256]{2,1,0:T(8,128)S(1)}, u32[]{:S(2)}, u32[]{:S(2)}) async-start(f32[16,16,256]{2,1,0:T(8,128)} %bitcast.5), calls=%async_computation.1 | async-start | bytes 524288 | tf_op jit(solution)/shard_map/all_to_all | solution.py:35
  55.3 24.2 %all-to-all-start.2 = ((f32[16,16,256]{2,1,0:T(8,128)}), f32[16,16,256]{2,1,0:T(8,128)S(1)}, u32[]{:S(2)}, u32[]{:S(2)}) async-start(f32[16,16,256]{2,1,0:T(8,128)} %broadcast_in_dim.40), calls=%async_computation.2 | async-start | bytes 524288 | tf_op jit(solution)/shard_map/all_to_all | solution.py:35
  81.8 20.4 %all-to-all-start.3 = ((f32[32,8,256]{2,1,0:T(8,128)}), f32[32,8,256]{2,1,0:T(8,128)S(1)}, u32[]{:S(2)}, u32[]{:S(2)}) async-start(f32[32,8,256]{2,1,0:T(8,128)} %bitcast.8), calls=%async_computation.3 | async-start | bytes 524288 | tf_op jit(solution)/shard_map/all_to_all | solution.py:35
  127.2 21.4 %copy-start.2 = (f32[1,3,2,2048]{3,2,1,0:T(2,128)S(1)}, f32[1,3,2,2048]{3,2,1,0:T(2,128)}, u32[]{:S(2)}) copy-start(f32[1,3,2,2048]{3,2,1,0:T(2,128)} %param.9) | copy-start | bytes 147460
  127.3 21.4 %copy-start.3 = (f32[1,3,2,2048]{3,2,1,0:T(2,128)S(1)}, f32[1,3,2,2048]{3,2,1,0:T(2,128)}, u32[]{:S(2)}) copy-start(f32[1,3,2,2048]{3,2,1,0:T(2,128)} %param.7) | copy-start | bytes 147460
  127.3 21.4 %copy-start.4 = (f32[1,3,2,2048]{3,2,1,0:T(2,128)S(1)}, f32[1,3,2,2048]{3,2,1,0:T(2,128)}, u32[]{:S(2)}) copy-start(f32[1,3,2,2048]{3,2,1,0:T(2,128)} %param.8) | copy-start | bytes 147460
  128.1 10.4 %all-to-all-start.5 = ((bf16[4,256,256]{2,1,0:T(8,128)(2,1)}), bf16[4,256,256]{2,1,0:T(8,128)(2,1)S(1)}, u32[]{:S(2)}, u32[]{:S(2)}) async-start(bf16[4,256,256]{2,1,0:T(8,128)(2,1)} %broadcast_in_dim.74), calls=%async_computation.5 | async-start | bytes 1048576 | tf_op jit(solution)/shard_map/all_to_all | solution.py:35
  138.5 11.6 %copy-start = (bf16[4,256,256]{2,1,0:T(8,128)(2,1)}, bf16[4,256,256]{2,1,0:T(8,128)(2,1)S(1)}, u32[]{:S(2)}) copy-start(bf16[4,256,256]{2,1,0:T(8,128)(2,1)S(1)} %all-to-all-done.5.mine) | copy-start | bytes 1572868
  138.5 11.6 %collective-permute-start = (bf16[4,256,256]{2,1,0:T(8,128)(2,1)S(1)}, bf16[4,256,256]{2,1,0:T(8,128)(2,1)S(1)}, u32[]{:S(2)}, u32[]{:S(2)}) collective-permute-start(bf16[4,256,256]{2,1,0:T(8,128)(2,1)S(1)} %all-to-all-done.5.mine), channel_id=1, source_target_pairs={{0,4},{4,0},{1,5},{5,1},{2,6},{6,2},{3,7},{7,3},{8,12},{12,8},{9,1... | collective-permute-start | bytes 1572872 | tf_op jit(solution)/shard_map/ppermute | solution.py:153
  150.0 0.8 copy-start.1

commit v4 on v3

--- a/solution.py
+++ b/solution.py
@@ -17,7 +17,7 @@
 PLANE = ("x", "c")
 PLANE_SHAPE = (4, 2)
 SLOT_ROWS = 8
-KINDS = 5
+KINDS = 4
 
 
 def adamw(param, first, second, grad):
@@ -35,9 +35,16 @@
     return lax.all_to_all(chunks, axis, 0, 0, tiled=True)
 
 
-def share(value, axis):
-    copies = jnp.broadcast_to(value[None], (lax.axis_size(axis), *value.shape))
-    return exchange(lax.optimization_barrier(copies), axis)
+def two_terms(value):
+    high = value.astype(jnp.bfloat16)
+    return high, (value - high.astype(jnp.float32)).astype(jnp.bfloat16)
+
+
+def choose(matrix, values):
+    return jnp.dot(matrix, values, preferred_element_type=jnp.float32)
+
+
+VMEM = pl.BlockSpec(memory_space=pltpu.VMEM)
 
 
 def split_kernel(grads, master, first, second, out, rows):
@@ -50,12 +57,8 @@
     for i, state in enumerate((master, first, second)):
         for s in range(capacity):
             rows[i, s * slab : (s + 1) * slab, :] = state[s]
-    value = rows[0]
-    high = value.astype(jnp.bfloat16)
-    rest = value - high.astype(jnp.float32)
-    middle = rest.astype(jnp.bfloat16)
-    low = (rest - middle.astype(jnp.float32)).astype(jnp.bfloat16)
-    terms = (high, middle, low, rows[1].astype(jnp.bfloat16), rows[2].astype(jnp.bfloat16))
+    high, low = two_terms(rows[0])
+    terms = (high, low, rows[1].astype(jnp.bfloat16), rows[2].astype(jnp.bfloat16))
     for t, term in enumerate(terms):
         at = count + t * SLOT_ROWS
         for k in range(plane):
@@ -108,6 +111,74 @@
     )(lax.axis_index("c").astype(jnp.int32).reshape(1), mine, other)
 
 
+def pack_kernel(raw, order, route, out):
+    plane, count, _ = raw.shape
+    ring = out.shape[0]
+    rows = order.shape[0]
+    part = rows // ring
+    total = raw[0, :rows, :].astype(jnp.float32)
+    for j in range(1, plane):
+        total = total + raw[j, :rows, :].astype(jnp.float32)
+    lines = [
+        raw[j, at : at + SLOT_ROWS, :] for at in range(rows, count, SLOT_ROWS) for j in range(plane)
+    ]
+    high, low = two_terms(total)
+    sources = ((order, high), (order, low), (route, jnp.concatenate(lines, axis=0)))
+    for i, (matrix, source) in enumerate(sources):
+        chosen = choose(matrix[...], source).astype(out.dtype)
+        for z in range(ring):
+            out[z, i * part : (i + 1) * part, :] = chosen[z * part : (z + 1) * part, :]
+
+
+def reduce_kernel(got, take, out):
+    ring, count, _ = got.shape
+    part = count // 3
+    total = got[0, :part, :].astype(jnp.float32) + got[0, part : 2 * part, :].astype(jnp.float32)
+    for z in range(1, ring):
+        total = total + (
+            got[z, :part, :].astype(jnp.float32) + got[z, part : 2 * part, :].astype(jnp.float32)
+        )
+    high, low = two_terms(total)
+    out[:part, :] = high
+    out[part : 2 * part, :] = low
+    lines = jnp.concatenate([got[z, 2 * part :, :] for z in range(ring)], axis=0)
+    out[2 * part :, :] = choose(take[...], lines).astype(out.dtype)
+
+
+def ordered(every, term, part):
+    return jnp.concatenate(
+        [every[z, term * part : (term + 1) * part, :] for z in range(every.shape[0])], axis=0
+    )
+
+
+def send_kernel(every, pick, out):
+    plane, layers, _, wide = out.shape
+    part = pick.shape[1] // every.shape[0]
+    high, low = ordered(every, 0, part), ordered(every, 1, part)
+    total = high.astype(jnp.float32) + low.astype(jnp.float32)
+    squares = jnp.sum(total * total)
+    sent = choose(pick[...], high) + choose(pick[...], low)
+    line = lax.broadcasted_iota(jnp.int32, sent.shape, 0)
+    sent = jnp.where(line % SLOT_ROWS == SLOT_ROWS - 1, squares, sent)
+    for j in range(plane):
+        for layer in range(layers):
+            out[j, layer] = sent[j * SLOT_ROWS : (j + 1) * SLOT_ROWS, :]
+
+
+def step_kernel(element_total, every, got, place, copies, rms):
+    part = place.shape[1] // every.shape[0]
+    squares = jnp.sum(got[...], axis=0)[SLOT_ROWS - 1 :, :]
+    grad_rms = jnp.sqrt(squares / element_total + 1e-06)
+    rms[...] = grad_rms
+    clip_factor = jnp.minimum(1.0, 1.0 / grad_rms)
+    terms = [ordered(every, t, part).astype(jnp.float32) for t in range(2 + KINDS)]
+    grad = (terms[0] + terms[1]) * clip_factor
+    param = adamw(terms[2] + terms[3], terms[4], terms[5], grad)[0]
+    weights = choose(place[...], param.astype(copies.dtype)).astype(copies.dtype)
+    for x in range(copies.shape[0]):
+        copies[x] = weights
+
+
 def shards(micro_grads, master, moment_one, moment_two, owner, slot):
     rows, width = micro_grads.shape[2:]
     capacity, slab = master.shape[1:3]
@@ -116,49 +187,87 @@
     lines = capacity * slab
     wide = width // plane
     layers = lax.axis_size("layer")
-    bf16 = jnp.bfloat16
-    home = (owner[0] * SLOT_ROWS + slot[0] * slab)[:, None]
-    home = (home + jnp.arange(slab, dtype=jnp.int32)[None, :]).reshape(rows)
-    tight = home // SLOT_ROWS * lines + home % SLOT_ROWS
+    my_z = lax.axis_index(RING)
+    part = rows // ring
+    plane_lines = plane * SLOT_ROWS
+    bf16, f32, i32 = jnp.bfloat16, jnp.float32, jnp.int32
+    count = jnp.arange(rows, dtype=i32)
+    few = jnp.arange(plane_lines, dtype=i32)
+
+    home = owner[0] * capacity + slot[0]
+    rank = jnp.sum((home[None, :] < home[:, None]).astype(i32), axis=1)
+    line = owner[0] * SLOT_ROWS + slot[0] * slab
+    member, turn = rank % ring, rank // ring
+
+    def per_row(value):
+        return (value[:, None] + jnp.arange(slab, dtype=i32)[None, :]).reshape(rows)
+
+    line_of = per_row(line)
+    dealt = per_row(member * part + turn * slab)
+    pair_of = per_row(member * 2 * slab + turn % 2 * slab)
+    order = dealt[None, :] == count[:, None]
+    place = dealt[:, None] == count[None, :]
+    line_at = jnp.sum(jnp.where(order, line_of[None, :], 0), axis=1)
+    pick = (my_z * plane_lines + few)[:, None] == line_at[None, :]
+    mine = line_of[None, :] == (my_z * plane_lines + few)[:, None]
+    pair_at = jnp.sum(jnp.where(mine, pair_of[None, :] + 1, 0), axis=1) - 1
+    kind = jnp.arange(KINDS, dtype=i32)[:, None]
+    goes = jnp.where(pair_at < 0, -1, pair_at)[None, :]
+    goes = jnp.where(goes < 0, -1, goes // (2 * slab) * part + kind * 2 * slab + goes % (2 * slab))
+    route = goes.reshape(1, KINDS * plane_lines) == count[:, None]
+    own_line = lax.dynamic_slice_in_dim(line_at, my_z * part, part)
+    within = jnp.arange(part, dtype=i32) % (2 * slab)
+    comes = (own_line // plane_lines * part + within)[None, :] + kind * 2 * slab
+    take = comes.reshape(KINDS * part, 1) == count[None, :]
 
     raw = exchange(split(micro_grads[0, 0], master[0], moment_one[0], moment_two[0], plane), PLANE)
-    plane_sum = jnp.sum(raw[:, :rows].astype(jnp.float32), axis=0)
-    strips = raw[:, rows:].reshape(plane, KINDS, SLOT_ROWS, wide)[:, :, :lines]
-    strips = strips.transpose(1, 0, 2, 3).reshape(KINDS, plane * lines, wide).astype(jnp.float32)
-
-    piece = jnp.sum(exchange(plane_sum.reshape(ring, rows // ring, wide), RING), axis=0)
-    totals = share(piece, RING).reshape(rows, wide)
-
-    line = jnp.arange(plane * SLOT_ROWS, dtype=jnp.int32)
-    pick = (lax.axis_index(RING) * plane * SLOT_ROWS + line)[:, None] == home[None, :]
-    sent = jnp.dot(pick.astype(jnp.float32), totals, precision=lax.Precision.HIGHEST)
-    sent = jnp.where((line % SLOT_ROWS == lines)[:, None], jnp.sum(totals * totals), sent)
-    sent = jnp.broadcast_to(
-        sent.reshape(plane, 1, SLOT_ROWS, wide), (plane, layers, SLOT_ROWS, wide)
-    )
+    packed = pl.pallas_call(
+        pack_kernel,
+        out_shape=jax.ShapeDtypeStruct((ring, 3 * part, wide), bf16),
+        in_specs=[VMEM] * 3,
+        out_specs=VMEM,
+        name="pack",
+    )(raw, order.astype(bf16), route.astype(bf16))
+    reduced = pl.pallas_call(
+        reduce_kernel,
+        out_shape=jax.ShapeDtypeStruct(((2 + KINDS) * part, wide), bf16),
+        in_specs=[VMEM] * 2,
+        out_specs=VMEM,
+        name="reduce",
+    )(exchange(packed, RING), take.astype(bf16))
+    every = lax.all_gather(reduced, RING, axis=0, tiled=False)
+
+    sent = pl.pallas_call(
+        send_kernel,
+        out_shape=jax.ShapeDtypeStruct((plane, layers, SLOT_ROWS, wide), f32),
+        in_specs=[VMEM] * 2,
+        out_specs=VMEM,
+        name="send",
+    )(every, pick.astype(bf16))
     got = exchange(sent.reshape(plane * layers, SLOT_ROWS, wide), (*PLANE, "layer"))
-    squares = jnp.sum(got[:, lines, 0])
-    grad_rms = jnp.sqrt(squares / (layers * rows * width) + 1e-06)
+
+    copies, rms = pl.pallas_call(
+        lambda *refs: step_kernel(float(layers * rows * width), *refs),
+        out_shape=(
+            jax.ShapeDtypeStruct((lax.axis_size("x"), rows, wide), bf16),
+            jax.ShapeDtypeStruct((1, wide), f32),
+        ),
+        in_specs=[VMEM] * 3,
+        out_specs=(VMEM, VMEM),
+        name="step",
+    )(every, got, place.astype(bf16))
+    halves = exchange(copies, "x")
+    weights = join(halves, lax.ppermute(halves, "c", [(0, 1), (1, 0)]))
+    grad_rms = rms[0, 0]
     clip_factor = jnp.minimum(1.0, 1.0 / grad_rms)
-
-    line = jnp.arange(plane * lines, dtype=jnp.int32)
-    pick = (lax.axis_index(RING) * plane * lines + line)[:, None] == tight[None, :]
-    grads = jnp.dot(pick.astype(jnp.float32), totals, precision=lax.Precision.HIGHEST)
-    param = strips[0] + strips[1] + strips[2]
-    param = adamw(param, strips[3], strips[4], grads * clip_factor)[0].astype(bf16)
-    params = share(param, RING).reshape(ring * plane * lines, wide)
-    place = tight[:, None] == jnp.arange(params.shape[0], dtype=jnp.int32)[None, :]
-    placed = jnp.dot(place.astype(bf16), params, preferred_element_type=jnp.float32)
-    halves = share(placed.astype(bf16), "x")
-    weights = join(halves, lax.ppermute(halves, "c", [(0, 1), (1, 0)]))
 
     own = got.reshape(plane, layers, SLOT_ROWS, wide)
     own = lax.dynamic_index_in_dim(own, lax.axis_index("layer"), 1, keepdims=False)
     own = own[:, :lines].transpose(1, 0, 2).reshape(capacity, slab, width) * clip_factor
     new = adamw(master[0], moment_one[0], moment_two[0], own)
     my_slots = lax.axis_index((RING, *PLANE)) * SLOT_ROWS
-    my_slots = my_slots + slab * jnp.arange(capacity, dtype=jnp.int32)
-    keep = jnp.any(home[None, :] == my_slots[:, None], axis=1)[:, None, None]
+    my_slots = my_slots + slab * jnp.arange(capacity, dtype=i32)
+    keep = jnp.any(line[None, :] == my_slots[:, None], axis=1)[:, None, None]
     old = (master[0], moment_one[0], moment_two[0])
     new = [jnp.where(keep, n, o)[None] for n, o in zip(new, old, strict=True)]
     return (*new, weights[None], grad_rms)

time: 155 us -> 148 us (0.955)
  starting transfers between devices: 46.6 us -> 27.6 us
  Pallas kernels: 4.73 us -> 13.5 us
  blocking collectives: 50.3 us -> 57.8 us
  waiting for transfers between devices: 41.5 us -> 37.2 us
  local copies, waits for them, and re-layouts: 3.35 us -> 5.22 us
    all_gather x0 -> x1, blocking collectives: none -> 33.4 us  [shards(): every = lax.all_gather(reduced, RING, axis=0, tiled=False)]
    all_to_all x2 -> x1, blocking collectives: 50.3 us -> 24.3 us  [exchange(): return lax.all_to_all(chunks, axis, 0, 0, tiled=True)]
    all_to_all x4 -> x3, starting transfers between devices: 36.6 us -> 24.3 us  [exchange(): return lax.all_to_all(chunks, axis, 0, 0, tiled=True)]
    pallas_call x0 -> x4, Pallas kernels: none -> 8.79 us  [the longest x1 2.5 us: shards(): pl.pallas_call(lambda *refs: step_kernel(float(layers * rows * width), *r...]
    ppermute x1, starting transfers between devices: 10 us -> 3.34 us  [shards(): weights = join(halves, lax.ppermute(halves, 'c', [(0, 1), (1, 0)]))]
    all_to_all x4 -> x3, waiting for transfers between devices: 41 us -> 36.7 us  [exchange(): return lax.all_to_all(chunks, axis, 0, 0, tiled=True)]
    broadcast_in_dim x4 -> x0, local copies, waits for them, and re-layouts: 2.31 us -> none  [the longest x3 1.58 us: share(): copies = jnp.broadcast_to(value[None], (lax.axis_size(axis), *value.shape))]
    convert_element_type x1 -> x3, other arithmetic: 0.02 us -> 2.21 us  [the longest x1 0.82 us: shards(): place.astype(bf16)]
  transfers between devices with their start and end apart: 5 -> 4, of which waited for: 5 -> 4; matrix products, arithmetic and copies ran while one was open for 1% -> 5% of each run, Pallas kernels for 0% -> 0%
where the time goes in v4:
time: 148 us; the launch traced here: 147 us
  blocking collectives  57.8 us (39%)
  waiting for transfers between devices  37.2 us (25%)
  starting transfers between devices  27.6 us (19%)
  Pallas kernels  13.5 us (9%)
  local copies, waits for them, and re-layouts  5.22 us (4%)
  other arithmetic  4.29 us (3%)
  between operations  1.53 us (1%)
    all_to_all x3, waiting for transfers between devices, exchange(): return lax.all_to_all(chunks, axis, 0, 0, tiled=True)  36.7 us
    all_gather x1, blocking collectives, shards(): every = lax.all_gather(reduced, RING, axis=0, tiled=False)  33.4 us
    all_to_all x1, blocking collectives, exchange(): return lax.all_to_all(chunks, axis, 0, 0, tiled=True)  24.3 us
    all_to_all x3, starting transfers between devices, exchange(): return lax.all_to_all(chunks, axis, 0, 0, tiled=True)  24.3 us
    ppermute x1, starting transfers between devices, shards(): weights = join(halves, lax.ppermute(halves, 'c', [(0, 1), (1, 0)]))  3.34 us
  transfers between devices with their start and end apart: 4, of which 4 were waited for; matrix products, arithmetic and copies ran while one was open for 5% of the time, Pallas kernels for 0%

profile of v4, /device:TPU:1, one launch (start us, length us, event | category | flops | bytes accessed | tf_op | source)
XLA Modules:
  0.0 147.2 jit_solution(5316268233314609026)
XLA Ops:
  0.6 2.4 %split.1 = bf16[8,288,256]{2,1,0:T(8,128)(2,1)} custom-call(bf16[256,2048]{1,0:T(8,128)(2,1)} %bitcast.23, f32[3,2,2048]{2,1,0:T(2,128)} %bitcast.27, f32[3,2,2048]{2,1,0:T(2,128)} %bitcast.28, f32[3,2,2048]{2,1,0:T(2,128)} %bitcast.26), custom_call_target="tpu_custom_call" | custom-call | tf_op jit(solution)/shard_map/split/pallas_call | solution.py:70
  3.1 10.5 %all-to-all-start = ((bf16[8,288,256]{2,1,0:T(8,128)(2,1)}), bf16[8,288,256]{2,1,0:T(8,128)(2,1)S(1)}, u32[]{:S(2)}, u32[]{:S(2)}) async-start(bf16[8,288,256]{2,1,0:T(8,128)(2,1)} %split.1), calls=%async_computation | async-start | bytes 2359296 | tf_op jit(solution)/shard_map/all_to_all | solution.py:35
  13.6 0.2 convert_reduce_fusion
  14.1 0.1 add.294
  14.2 0.1 add.308
  14.3 0.1 add.298
  14.5 0.2 select_reduce_fusion.1
  14.9 0.8 fusion.2
  15.7 14.4 %all-to-all-done.raw = bf16[8,288,256]{2,1,0:T(8,128)(2,1)S(1)} async-done(((bf16[8,288,256]{2,1,0:T(8,128)(2,1)}), bf16[8,288,256]{2,1,0:T(8,128)(2,1)S(1)}, u32[]{:S(2)}, u32[]{:S(2)}) %all-to-all-start) | async-done | bytes 1179680 | tf_op jit(solution)/shard_map/all_to_all | solution.py:35
  30.1 1.0 copy-done
  31.1 2.5 %pack.1 = bf16[16,48,256]{2,1,0:T(8,128)(2,1)} custom-call(bf16[8,288,256]{2,1,0:T(8,128)(2,1)} %copy-done, bf16[256,256]{1,0:T(8,128)(2,1)} %get-tuple-element.16.order, bf16[256,256]{1,0:T(8,128)(2,1)} %get-tuple-element.21.route), custom_call_target="tpu_custom_call" | custom-call | tf_op jit(solution)/shard_map/pack/pallas_call | solution.py:224
  33.5 10.4 %all-to-all-start.1 = ((bf16[16,48,256]{2,1,0:T(8,128)(2,1)}), bf16[16,48,256]{2,1,0:T(8,128)(2,1)S(1)}, u32[]{:S(2)}, u32[]{:S(2)}) async-start(bf16[16,48,256]{2,1,0:T(8,128)(2,1)} %pack.1), calls=%async_computation.1 | async-start | bytes 786432 | tf_op jit(solution)/shard_map/all_to_all | solution.py:35
  43.9 0.1 select_reduce_fusion
  44.3 0.7 fusion.4.take
  45.0 0.7 compare_convert_fusion.pick
  45.7 16.3 %all-to-all-done.1.got = bf16[16,48,256]{2,1,0:T(8,128)(2,1)S(1)} async-done(((bf16[16,48,256]{2,1,0:T(8,128)(2,1)}), bf16[16,48,256]{2,1,0:T(8,128)(2,1)S(1)}, u32[]{:S(2)}, u32[]{:S(2)}) %all-to-all-start.1) | async-done | bytes 393248 | tf_op jit(solution)/shard_map/all_to_all | solution.py:35
  62.0 0.7 copy-done.2
  62.7 1.8 %reduce.1 = bf16[96,256]{1,0:T(8,128)(2,1)} custom-call(bf16[16,48,256]{2,1,0:T(8,128)(2,1)} %copy-done.2, bf16[64,256]{1,0:T(8,128)(2,1)} %fusion.4.take), custom_call_target="tpu_custom_call" | custom-call | tf_op jit(solution)/shard_map/reduce/pallas_call | solution.py:231
  64.5 33.4 %all-gather = bf16[1536,256]{1,0:T(8,128)(2,1)} all-gather(bf16[96,256]{1,0:T(8,128)(2,1)} %reduce.1), channel_id=2, replica_groups=mesh['z'=16,'x'=4,'c'=2,'layer'=4] {'z'}, dimensions={0}, use_global_device_ids=true | all-gather | bytes 835584 | tf_op jit(solution)/shard_map/all_gather | solution.py:238
  97.9 2.1 %send.1 = f32[8,4,8,256]{3,2,1,0:T(8,128)} custom-call(bf16[16,96,256]{2,1,0:T(8,128)(2,1)} %bitcast.20, bf16[64,256]{1,0:T(8,128)(2,1)} %compare_convert_fusion.pick), custom_call_target="tpu_custom_call" | custom-call | tf_op jit(solution)/shard_map/send/pallas_call | solution.py:240
  100.0 24.3 %all_to_all.20.refs_1_ = f32[32,8,256]{2,1,0:T(8,128)} all-to-all(f32[32,8,256]{2,1,0:T(8,128)} %bitcast.25), channel_id=1, replica_groups=mesh['z'=16,'x'=4,'c'=2,'layer'=4] {'x','c','layer'}, dimensions={0} | all-to-all | bytes 524288 | tf_op jit(solution)/shard_map/all_to_all | solution.py:35
  124.3 2.5 %step.1 = (bf16[4,256,256]{2,1,0:T(8,128)(2,1)}, f32[1,256]{1,0:T(1,128)}) custom-call(bf16[16,96,256]{2,1,0:T(8,128)(2,1)} %bitcast.21, f32[32,8,256]{2,1,0:T(8,128)} %all_to_all.20.refs_1_, bf16[256,256]{1,0:T(8,128)(2,1)} %get-tuple-element.15.refs_2_), custom_call_target="tpu_custom_call" | custom-call | tf_op jit(solution)/shard_map/step/pallas_call | solution.py:249
  126.8 3.5 %all-to-all-start.3 = ((bf16[4,256,256]{2,1,0:T(8,128)(2,1)}), bf16[4,256,256]{2,1,0:T(8,128)(2,1)S(1)}, u32[]{:S(2)}, u32[]{:S(2)}) async-start(bf16[4,256,256]{2,1,0:T(8,128)(2,1)} %get-tuple-element.8), calls=%async_computation.3 | async-start | bytes 1048576 | tf_op jit(solution)/shard_map/all_to_all | solution.py:35
  130.3 0.2 compare_reduce_fusion
  130.5 1.2 slice.7
  132.4 0.9 dynamic-slice_bitcast_fusion
  133.2 6.0 %all-to-all-done.3.mine = bf16[4,256,256]{2,1,0:T(8,128)(2,1)S(1)} async-done(((bf16[4,256,256]{2,1,0:T(8,128)(2,1)}), bf16[4,256,256]{2,1,0:T(8,128)(2,1)S(1)}, u32[]{:S(2)}, u32[]{:S(2)}) %all-to-all-start.3) | async-done | bytes 524320 | tf_op jit(solution)/shard_map/all_to_all | solution.py:35
  139.2 3.3 %collective-permute-start = (bf16[4,256,256]{2,1,0:T(8,128)(2,1)S(1)}, bf16[4,256,256]{2,1,0:T(8,128)(2,1)S(1)}, u32[]{:S(2)}, u32[]{:S(2)}) collective-permute-start(bf16[4,256,256]{2,1,0:T(8,128)(2,1)S(1)} %all-to-all-done.3.mine), channel_id=1, source_target_pairs={{0,4},{4,0},{1,5},{5,1},{2,6},{6,2},{3,7},{7,3},{8,12},{12,8},{9,1... | collective-permute-start | bytes 1572872 | tf_op jit(solution)/shard_map/ppermute | solution.py:260
  142.7 0.9 broadcast_select_fusion
  143.6 0.5 collective-permute-done.other
  144.1 0.8 copy-done.3
  144.9 2.3 %join.1 = bf16[256,2048]{1,0:T(8,128)(2,1)} custom-call(s32[1]{0:T(128)} %bitcast.12.core, bf16[4,256,256]{2,1,0:T(8,128)(2,1)} %copy-done.1, bf16[4,256,256]{2,1,0:T(8,128)(2,1)} %copy-done.3), custom_call_target="tpu_custom_call" | custom-call | tf_op jit(solution)/shard_map/join/pallas_call | solution.py:101
  (34 shorter events, 0.8 us)
Async XLA Ops:
  3.1 10.5 %copy-start.7 = (s32[1,128]{1,0:T(1,128)S(1)}, s32[1,128]{1,0:T(1,128)}, u32[]{:S(2)}) copy-start(s32[1,128]{1,0:T(1,128)} %param.11) | copy-start | bytes 1540
  3.1 10.5 %copy-start.8 = (s32[1,128]{1,0:T(1,128)S(1)}, s32[1,128]{1,0:T(1,128)}, u32[]{:S(2)}) copy-start(s32[1,128]{1,0:T(1,128)} %param.10) | copy-start | bytes 1540
  3.1 27.0 %all-to-all-start = ((bf16[8,288,256]{2,1,0:T(8,128)(2,1)}), bf16[8,288,256]{2,1,0:T(8,128)(2,1)S(1)}, u32[]{:S(2)}, u32[]{:S(2)}) async-start(bf16[8,288,256]{2,1,0:T(8,128)(2,1)} %split.1), calls=%async_computation | async-start | bytes 2359296 | tf_op jit(solution)/shard_map/all_to_all | solution.py:35
  30.1 1.0 copy-start
  33.5 28.4 %all-to-all-start.1 = ((bf16[16,48,256]{2,1,0:T(8,128)(2,1)}), bf16[16,48,256]{2,1,0:T(8,128)(2,1)S(1)}, u32[]{:S(2)}, u32[]{:S(2)}) async-start(bf16[16,48,256]{2,1,0:T(8,128)(2,1)} %pack.1), calls=%async_computation.1 | async-start | bytes 786432 | tf_op jit(solution)/shard_map/all_to_all | solution.py:35
  62.0 0.7 copy-start.2
  124.3 18.4 %copy-start.4 = (f32[1,3,2,2048]{3,2,1,0:T(2,128)S(1)}, f32[1,3,2,2048]{3,2,1,0:T(2,128)}, u32[]{:S(2)}) copy-start(f32[1,3,2,2048]{3,2,1,0:T(2,128)} %param.9) | copy-start | bytes 147460
  124.3 18.4 %copy-start.5 = (f32[1,3,2,2048]{3,2,1,0:T(2,128)S(1)}, f32[1,3,2,2048]{3,2,1,0:T(2,128)}, u32[]{:S(2)}) copy-start(f32[1,3,2,2048]{3,2,1,0:T(2,128)} %param.7) | copy-start | bytes 147460
  124.3 18.4 %copy-start.6 = (f32[1,3,2,2048]{3,2,1,0:T(2,128)S(1)}, f32[1,3,2,2048]{3,2,1,0:T(2,128)}, u32[]{:S(2)}) copy-start(f32[1,3,2,2048]{3,2,1,0:T(2,128)} %param.8) | copy-start | bytes 147460
  126.8 12.4 %all-to-all-start.3 = ((bf16[4,256,256]{2,1,0:T(8,128)(2,1)}), bf16[4,256,256]{2,1,0:T(8,128)(2,1)S(1)}, u32[]{:S(2)}, u32[]{:S(2)}) async-start(bf16[4,256,256]{2,1,0:T(8,128)(2,1)} %get-tuple-element.8), calls=%async_computation.3 | async-start | bytes 1048576 | tf_op jit(solution)/shard_map/all_to_all | solution.py:35
  139.2 4.9 %copy-start.1 = (bf16[4,256,256]{2,1,0:T(8,128)(2,1)}, bf16[4,256,256]{2,1,0:T(8,128)(2,1)S(1)}, u32[]{:S(2)}) copy-start(bf16[4,256,256]{2,1,0:T(8,128)(2,1)S(1)} %all-to-all-done.3.mine) | copy-start | bytes 1572868
  139.2 4.9 %collective-permute-start = (bf16[4,256,256]{2,1,0:T(8,128)(2,1)S(1)}, bf16[4,256,256]{2,1,0:T(8,128)(2,1)S(1)}, u32[]{:S(2)}, u32[]{:S(2)}) collective-permute-start(bf16[4,256,256]{2,1,0:T(8,128)(2,1)S(1)} %all-to-all-done.3.mine), channel_id=1, source_target_pairs={{0,4},{4,0},{1,5},{5,1},{2,6},{6,2},{3,7},{7,3},{8,12},{12,8},{9,1... | collective-permute-start | bytes 1572872 | tf_op jit(solution)/shard_map/ppermute | solution.py:260
  144.1 0.8 copy-start.3

commit v5 on v4

--- a/solution.py
+++ b/solution.py
@@ -45,6 +45,10 @@
 
 
 VMEM = pl.BlockSpec(memory_space=pltpu.VMEM)
+
+
+def near(value):
+    return pltpu.with_memory_space_constraint(value, pltpu.VMEM)
 
 
 def split_kernel(grads, master, first, second, out, rows):
@@ -69,9 +73,7 @@
     count, width = grads.shape
     return pl.pallas_call(
         split_kernel,
-        out_shape=jax.ShapeDtypeStruct(
-            (plane, count + KINDS * SLOT_ROWS, width // plane), grads.dtype
-        ),
+        out_shape=pltpu.VMEM((plane, count + KINDS * SLOT_ROWS, width // plane), grads.dtype),
         in_specs=[pl.BlockSpec(memory_space=pltpu.VMEM)] * 4,
         out_specs=pl.BlockSpec(memory_space=pltpu.VMEM),
         scratch_shapes=[pltpu.VMEM((3, SLOT_ROWS, width), jnp.float32)],
@@ -108,7 +110,7 @@
         ],
         out_specs=pl.BlockSpec(memory_space=pltpu.VMEM),
         name="join",
-    )(lax.axis_index("c").astype(jnp.int32).reshape(1), mine, other)
+    )(lax.axis_index("c").astype(jnp.int32).reshape(1), near(mine), near(other))
 
 
 def pack_kernel(raw, order, route, out):
@@ -223,39 +225,39 @@
     raw = exchange(split(micro_grads[0, 0], master[0], moment_one[0], moment_two[0], plane), PLANE)
     packed = pl.pallas_call(
         pack_kernel,
-        out_shape=jax.ShapeDtypeStruct((ring, 3 * part, wide), bf16),
+        out_shape=pltpu.VMEM((ring, 3 * part, wide), bf16),
         in_specs=[VMEM] * 3,
         out_specs=VMEM,
         name="pack",
-    )(raw, order.astype(bf16), route.astype(bf16))
+    )(near(raw), near(order.astype(bf16)), near(route.astype(bf16)))
     reduced = pl.pallas_call(
         reduce_kernel,
-        out_shape=jax.ShapeDtypeStruct(((2 + KINDS) * part, wide), bf16),
+        out_shape=pltpu.VMEM(((2 + KINDS) * part, wide), bf16),
         in_specs=[VMEM] * 2,
         out_specs=VMEM,
         name="reduce",
-    )(exchange(packed, RING), take.astype(bf16))
+    )(near(exchange(packed, RING)), near(take.astype(bf16)))
     every = lax.all_gather(reduced, RING, axis=0, tiled=False)
 
     sent = pl.pallas_call(
         send_kernel,
-        out_shape=jax.ShapeDtypeStruct((plane, layers, SLOT_ROWS, wide), f32),
+        out_shape=pltpu.VMEM((plane, layers, SLOT_ROWS, wide), f32),
         in_specs=[VMEM] * 2,
         out_specs=VMEM,
         name="send",
-    )(every, pick.astype(bf16))
+    )(near(every), near(pick.astype(bf16)))
     got = exchange(sent.reshape(plane * layers, SLOT_ROWS, wide), (*PLANE, "layer"))
 
     copies, rms = pl.pallas_call(
         lambda *refs: step_kernel(float(layers * rows * width), *refs),
         out_shape=(
-            jax.ShapeDtypeStruct((lax.axis_size("x"), rows, wide), bf16),
+            pltpu.VMEM((lax.axis_size("x"), rows, wide), bf16),
             jax.ShapeDtypeStruct((1, wide), f32),
         ),
         in_specs=[VMEM] * 3,
         out_specs=(VMEM, VMEM),
         name="step",
-    )(every, got, place.astype(bf16))
+    )(near(every), near(got), near(place.astype(bf16)))
     halves = exchange(copies, "x")
     weights = join(halves, lax.ppermute(halves, "c", [(0, 1), (1, 0)]))
     grad_rms = rms[0, 0]

time: 148 us -> 135 us (0.912)
  Pallas kernels: 13.5 us -> 6.28 us
  local copies, waits for them, and re-layouts: 5.22 us -> 1.84 us
  waiting for transfers between devices: 37.2 us -> 40 us
  blocking collectives: 57.8 us -> 55.1 us
  other arithmetic: 4.29 us -> 2.35 us
    pallas_call x4, Pallas kernels: 8.72 us -> 3.91 us  [the longest x1 2.43 us: split(): pl.pallas_call(split_kernel, out_shape=pltpu.VMEM((plane, count + KINDS *...]
    all_to_all x3, waiting for transfers between devices: 36.7 us -> 39.5 us  [exchange(): return lax.all_to_all(chunks, axis, 0, 0, tiled=True)]
    all_gather x1, blocking collectives: 33.4 us -> 30.7 us  [shards(): every = lax.all_gather(reduced, RING, axis=0, tiled=False)]
    unnamed x18 -> x10, local copies, waits for them, and re-layouts: 2.56 us -> 0.02 us
  transfers between devices with their start and end apart: 4 -> 4, of which waited for: 4 -> 4; matrix products, arithmetic and copies ran while one was open for 5% -> 3% of each run, Pallas kernels for 0% -> 0%
where the time goes in v5:
time: 135 us
  blocking collectives  55.1 us (41%)
  waiting for transfers between devices  40 us (30%)
  starting transfers between devices  27.6 us (20%)
  Pallas kernels  6.28 us (5%)
  other arithmetic  2.35 us (2%)
  local copies, waits for them, and re-layouts  1.84 us (1%)
  between operations  1.56 us (1%)
    all_to_all x3, waiting for transfers between devices, exchange(): return lax.all_to_all(chunks, axis, 0, 0, tiled=True)  39.5 us
    all_gather x1, blocking collectives, shards(): every = lax.all_gather(reduced, RING, axis=0, tiled=False)  30.7 us
    all_to_all x1, blocking collectives, exchange(): return lax.all_to_all(chunks, axis, 0, 0, tiled=True)  24.5 us
    all_to_all x3, starting transfers between devices, exchange(): return lax.all_to_all(chunks, axis, 0, 0, tiled=True)  24.3 us
    ppermute x1, starting transfers between devices, shards(): weights = join(halves, lax.ppermute(halves, 'c', [(0, 1), (1, 0)]))  3.33 us
  transfers between devices with their start and end apart: 4, of which 4 were waited for; matrix products, arithmetic and copies ran while one was open for 3% of the time, Pallas kernels for 0%

profile of v5, /device:TPU:1, one launch (start us, length us, event | category | flops | bytes accessed | tf_op | source)
XLA Modules:
  0.0 134.8 jit_solution(5194456290017552328)
XLA Ops:
  0.6 2.4 %split.1 = bf16[8,288,256]{2,1,0:T(8,128)(2,1)} custom-call(bf16[256,2048]{1,0:T(8,128)(2,1)} %bitcast.24, f32[3,2,2048]{2,1,0:T(2,128)} %bitcast.27, f32[3,2,2048]{2,1,0:T(2,128)} %bitcast.28, f32[3,2,2048]{2,1,0:T(2,128)} %bitcast.26), custom_call_target="tpu_custom_call" | custom-call | tf_op jit(solution)/shard_map/split/pallas_call | solution.py:74
  3.1 10.5 %all-to-all-start = ((bf16[8,288,256]{2,1,0:T(8,128)(2,1)}), bf16[8,288,256]{2,1,0:T(8,128)(2,1)S(1)}, u32[]{:S(2)}, u32[]{:S(2)}) async-start(bf16[8,288,256]{2,1,0:T(8,128)(2,1)} %split.1), calls=%async_computation | async-start | bytes 2359296 | tf_op jit(solution)/shard_map/all_to_all | solution.py:35
  13.6 0.2 convert_reduce_fusion
  13.8 0.1 iota_add_fusion.1
  13.9 0.1 add_add_fusion
  14.1 0.1 add.294
  14.2 0.1 add.308
  14.3 0.1 add.298
  14.5 0.2 select_reduce_fusion.1
  14.8 0.1 select_n.127
  14.9 0.1 fusion.2
  15.0 15.1 %all-to-all-done.raw = bf16[8,288,256]{2,1,0:T(8,128)(2,1)S(1)} async-done(((bf16[8,288,256]{2,1,0:T(8,128)(2,1)}), bf16[8,288,256]{2,1,0:T(8,128)(2,1)S(1)}, u32[]{:S(2)}, u32[]{:S(2)}) %all-to-all-start) | async-done | bytes 1179680 | tf_op jit(solution)/shard_map/all_to_all | solution.py:35
  30.1 1.1 pack.1
  31.2 10.4 %all-to-all-start.1 = ((bf16[16,48,256]{2,1,0:T(8,128)(2,1)}), bf16[16,48,256]{2,1,0:T(8,128)(2,1)S(1)}, u32[]{:S(2)}, u32[]{:S(2)}) async-start(bf16[16,48,256]{2,1,0:T(8,128)(2,1)} %pack.1), calls=%async_computation.1 | async-start | bytes 786432 | tf_op jit(solution)/shard_map/all_to_all | solution.py:35
  41.5 0.1 select_reduce_fusion
  41.7 0.1 fusion.6
  41.8 0.1 add.321
  41.9 0.1 fusion.4.take
  42.1 17.5 %all-to-all-done.1.got = bf16[16,48,256]{2,1,0:T(8,128)(2,1)S(1)} async-done(((bf16[16,48,256]{2,1,0:T(8,128)(2,1)}), bf16[16,48,256]{2,1,0:T(8,128)(2,1)S(1)}, u32[]{:S(2)}, u32[]{:S(2)}) %all-to-all-start.1) | async-done | bytes 393248 | tf_op jit(solution)/shard_map/all_to_all | solution.py:35
  59.6 0.1 reduce.1
  59.8 30.7 %all-gather = bf16[1536,256]{1,0:T(8,128)(2,1)S(1)} all-gather(bf16[96,256]{1,0:T(8,128)(2,1)S(1)} %reduce.1), channel_id=2, replica_groups=mesh['z'=16,'x'=4,'c'=2,'layer'=4] {'z'}, dimensions={0}, use_global_device_ids=true | all-gather | bytes 835584 | tf_op jit(solution)/shard_map/all_gather | solution.py:240
  90.4 0.2 send.1
  90.6 24.5 %all_to_all.20.refs_1_ = f32[32,8,256]{2,1,0:T(8,128)S(1)} all-to-all(f32[32,8,256]{2,1,0:T(8,128)S(1)} %bitcast.23), channel_id=1, replica_groups=mesh['z'=16,'x'=4,'c'=2,'layer'=4] {'x','c','layer'}, dimensions={0} | all-to-all | bytes 524288 | tf_op jit(solution)/shard_map/all_to_all | solution.py:35
  115.1 1.3 step.1
  116.4 3.5 %all-to-all-start.3 = ((bf16[4,256,256]{2,1,0:T(8,128)(2,1)}), bf16[4,256,256]{2,1,0:T(8,128)(2,1)S(1)}, u32[]{:S(2)}, u32[]{:S(2)}) async-start(bf16[4,256,256]{2,1,0:T(8,128)(2,1)} %get-tuple-element.8), calls=%async_computation.3 | async-start | bytes 1048576 | tf_op jit(solution)/shard_map/all_to_all | solution.py:35
  119.9 0.2 compare_reduce_fusion
  120.1 1.2 slice.7
  122.0 6.9 %all-to-all-done.3.mine = bf16[4,256,256]{2,1,0:T(8,128)(2,1)S(1)} async-done(((bf16[4,256,256]{2,1,0:T(8,128)(2,1)}), bf16[4,256,256]{2,1,0:T(8,128)(2,1)S(1)}, u32[]{:S(2)}, u32[]{:S(2)}) %all-to-all-start.3) | async-done | bytes 524320 | tf_op jit(solution)/shard_map/all_to_all | solution.py:35
  128.8 3.3 %collective-permute-start = (bf16[4,256,256]{2,1,0:T(8,128)(2,1)S(1)}, bf16[4,256,256]{2,1,0:T(8,128)(2,1)S(1)}, u32[]{:S(2)}, u32[]{:S(2)}) collective-permute-start(bf16[4,256,256]{2,1,0:T(8,128)(2,1)S(1)} %all-to-all-done.3.mine), channel_id=1, source_target_pairs={{0,4},{4,0},{1,5},{5,1},{2,6},{6,2},{3,7},{7,3},{8,12},{12,8},{9,1... | collective-permute-start | bytes 1572872 | tf_op jit(solution)/shard_map/ppermute | solution.py:262
  132.3 0.9 broadcast_select_fusion
  133.2 0.5 collective-permute-done.other
  133.7 1.1 join.1
  (26 shorter events, 0.5 us)
Async XLA Ops:
  3.1 10.5 %copy-start.3 = (s32[1,128]{1,0:T(1,128)S(1)}, s32[1,128]{1,0:T(1,128)}, u32[]{:S(2)}) copy-start(s32[1,128]{1,0:T(1,128)} %param.11) | copy-start | bytes 1540
  3.1 10.5 %copy-start.4 = (s32[1,128]{1,0:T(1,128)S(1)}, s32[1,128]{1,0:T(1,128)}, u32[]{:S(2)}) copy-start(s32[1,128]{1,0:T(1,128)} %param.10) | copy-start | bytes 1540
  3.1 27.0 %all-to-all-start = ((bf16[8,288,256]{2,1,0:T(8,128)(2,1)}), bf16[8,288,256]{2,1,0:T(8,128)(2,1)S(1)}, u32[]{:S(2)}, u32[]{:S(2)}) async-start(bf16[8,288,256]{2,1,0:T(8,128)(2,1)} %split.1), calls=%async_computation | async-start | bytes 2359296 | tf_op jit(solution)/shard_map/all_to_all | solution.py:35
  31.2 28.4 %all-to-all-start.1 = ((bf16[16,48,256]{2,1,0:T(8,128)(2,1)}), bf16[16,48,256]{2,1,0:T(8,128)(2,1)S(1)}, u32[]{:S(2)}, u32[]{:S(2)}) async-start(bf16[16,48,256]{2,1,0:T(8,128)(2,1)} %pack.1), calls=%async_computation.1 | async-start | bytes 786432 | tf_op jit(solution)/shard_map/all_to_all | solution.py:35
  115.1 17.1 %copy-start = (f32[1,3,2,2048]{3,2,1,0:T(2,128)S(1)}, f32[1,3,2,2048]{3,2,1,0:T(2,128)}, u32[]{:S(2)}) copy-start(f32[1,3,2,2048]{3,2,1,0:T(2,128)} %param.9) | copy-start | bytes 147460
  115.1 17.2 %copy-start.1 = (f32[1,3,2,2048]{3,2,1,0:T(2,128)S(1)}, f32[1,3,2,2048]{3,2,1,0:T(2,128)}, u32[]{:S(2)}) copy-start(f32[1,3,2,2048]{3,2,1,0:T(2,128)} %param.7) | copy-start | bytes 147460
  115.1 17.2 %copy-start.2 = (f32[1,3,2,2048]{3,2,1,0:T(2,128)S(1)}, f32[1,3,2,2048]{3,2,1,0:T(2,128)}, u32[]{:S(2)}) copy-start(f32[1,3,2,2048]{3,2,1,0:T(2,128)} %param.8) | copy-start | bytes 147460
  116.4 12.4 %all-to-all-start.3 = ((bf16[4,256,256]{2,1,0:T(8,128)(2,1)}), bf16[4,256,256]{2,1,0:T(8,128)(2,1)S(1)}, u32[]{:S(2)}, u32[]{:S(2)}) async-start(bf16[4,256,256]{2,1,0:T(8,128)(2,1)} %get-tuple-element.8), calls=%async_computation.3 | async-start | bytes 1048576 | tf_op jit(solution)/shard_map/all_to_all | solution.py:35
  128.8 4.9 %collective-permute-start = (bf16[4,256,256]{2,1,0:T(8,128)(2,1)S(1)}, bf16[4,256,256]{2,1,0:T(8,128)(2,1)S(1)}, u32[]{:S(2)}, u32[]{:S(2)}) collective-permute-start(bf16[4,256,256]{2,1,0:T(8,128)(2,1)S(1)} %all-to-all-done.3.mine), channel_id=1, source_target_pairs={{0,4},{4,0},{1,5},{5,1},{2,6},{6,2},{3,7},{7,3},{8,12},{12,8},{9,1... | collective-permute-start | bytes 1572872 | tf_op jit(solution)/shard_map/ppermute | solution.py:262

commit v6 on v5

--- a/solution.py
+++ b/solution.py
@@ -1,3 +1,5 @@
+import math
+
 import jax
 import jax.numpy as jnp
 from jax import lax
@@ -14,8 +16,9 @@
 step_number = 100.0
 
 RING = "z"
-PLANE = ("x", "c")
-PLANE_SHAPE = (4, 2)
+PLANE = ("pair", "x", "c")
+PLANE_SHAPE = (2, 4, 2)
+HALF = ("pair", "x")
 SLOT_ROWS = 8
 KINDS = 4
 
@@ -128,23 +131,26 @@
     sources = ((order, high), (order, low), (route, jnp.concatenate(lines, axis=0)))
     for i, (matrix, source) in enumerate(sources):
         chosen = choose(matrix[...], source).astype(out.dtype)
+        size = chosen.shape[0] // ring
         for z in range(ring):
-            out[z, i * part : (i + 1) * part, :] = chosen[z * part : (z + 1) * part, :]
+            out[z, i * part : i * part + size, :] = chosen[z * size : (z + 1) * size, :]
 
 
 def reduce_kernel(got, take, out):
-    ring, count, _ = got.shape
-    part = count // 3
+    ring = got.shape[0]
+    part = out.shape[1] // (2 + KINDS)
     total = got[0, :part, :].astype(jnp.float32) + got[0, part : 2 * part, :].astype(jnp.float32)
     for z in range(1, ring):
         total = total + (
             got[z, :part, :].astype(jnp.float32) + got[z, part : 2 * part, :].astype(jnp.float32)
         )
     high, low = two_terms(total)
-    out[:part, :] = high
-    out[part : 2 * part, :] = low
     lines = jnp.concatenate([got[z, 2 * part :, :] for z in range(ring)], axis=0)
-    out[2 * part :, :] = choose(take[...], lines).astype(out.dtype)
+    lines = choose(take[...], lines).astype(out.dtype)
+    for z in range(ring):
+        out[z, :part, :] = high
+        out[z, part : 2 * part, :] = low
+        out[z, 2 * part :, :] = lines
 
 
 def ordered(every, term, part):
@@ -196,6 +202,8 @@
     count = jnp.arange(rows, dtype=i32)
     few = jnp.arange(plane_lines, dtype=i32)
 
+    deal = -(-plane * capacity // ring)
+    pair = deal * slab
     home = owner[0] * capacity + slot[0]
     rank = jnp.sum((home[None, :] < home[:, None]).astype(i32), axis=1)
     line = owner[0] * SLOT_ROWS + slot[0] * slab
@@ -206,7 +214,7 @@
 
     line_of = per_row(line)
     dealt = per_row(member * part + turn * slab)
-    pair_of = per_row(member * 2 * slab + turn % 2 * slab)
+    pair_of = per_row(member * pair + turn % deal * slab)
     order = dealt[None, :] == count[:, None]
     place = dealt[:, None] == count[None, :]
     line_at = jnp.sum(jnp.where(order, line_of[None, :], 0), axis=1)
@@ -215,29 +223,30 @@
     pair_at = jnp.sum(jnp.where(mine, pair_of[None, :] + 1, 0), axis=1) - 1
     kind = jnp.arange(KINDS, dtype=i32)[:, None]
     goes = jnp.where(pair_at < 0, -1, pair_at)[None, :]
-    goes = jnp.where(goes < 0, -1, goes // (2 * slab) * part + kind * 2 * slab + goes % (2 * slab))
-    route = goes.reshape(1, KINDS * plane_lines) == count[:, None]
+    goes = jnp.where(goes < 0, -1, (goes // pair * KINDS + kind) * pair + goes % pair)
+    chunks = jnp.arange(ring * KINDS * pair, dtype=i32)
+    route = goes.reshape(1, KINDS * plane_lines) == chunks[:, None]
     own_line = lax.dynamic_slice_in_dim(line_at, my_z * part, part)
-    within = jnp.arange(part, dtype=i32) % (2 * slab)
-    comes = (own_line // plane_lines * part + within)[None, :] + kind * 2 * slab
-    take = comes.reshape(KINDS * part, 1) == count[None, :]
+    within = jnp.arange(part, dtype=i32) % pair
+    comes = (own_line // plane_lines * KINDS + kind) * pair + within[None, :]
+    take = comes.reshape(KINDS * part, 1) == chunks[None, :]
 
     raw = exchange(split(micro_grads[0, 0], master[0], moment_one[0], moment_two[0], plane), PLANE)
     packed = pl.pallas_call(
         pack_kernel,
-        out_shape=pltpu.VMEM((ring, 3 * part, wide), bf16),
+        out_shape=pltpu.VMEM((ring, 2 * part + KINDS * pair, wide), bf16),
         in_specs=[VMEM] * 3,
         out_specs=VMEM,
         name="pack",
     )(near(raw), near(order.astype(bf16)), near(route.astype(bf16)))
     reduced = pl.pallas_call(
         reduce_kernel,
-        out_shape=pltpu.VMEM(((2 + KINDS) * part, wide), bf16),
+        out_shape=pltpu.VMEM((ring, (2 + KINDS) * part, wide), bf16),
         in_specs=[VMEM] * 2,
         out_specs=VMEM,
         name="reduce",
     )(near(exchange(packed, RING)), near(take.astype(bf16)))
-    every = lax.all_gather(reduced, RING, axis=0, tiled=False)
+    every = exchange(reduced, RING)
 
     sent = pl.pallas_call(
         send_kernel,
@@ -251,14 +260,14 @@
     copies, rms = pl.pallas_call(
         lambda *refs: step_kernel(float(layers * rows * width), *refs),
         out_shape=(
-            pltpu.VMEM((lax.axis_size("x"), rows, wide), bf16),
+            pltpu.VMEM((lax.axis_size(HALF), rows, wide), bf16),
             jax.ShapeDtypeStruct((1, wide), f32),
         ),
         in_specs=[VMEM] * 3,
         out_specs=(VMEM, VMEM),
         name="step",
     )(near(every), near(got), near(place.astype(bf16)))
-    halves = exchange(copies, "x")
+    halves = exchange(copies, HALF)
     weights = join(halves, lax.ppermute(halves, "c", [(0, 1), (1, 0)]))
     grad_rms = rms[0, 0]
     clip_factor = jnp.minimum(1.0, 1.0 / grad_rms)
@@ -276,7 +285,7 @@
 
 
 def solution(mesh):
-    ring = mesh.shape["dp"] // (PLANE_SHAPE[0] * PLANE_SHAPE[1])
+    ring = mesh.shape["dp"] // math.prod(PLANE_SHAPE)
     devices = mesh.devices.reshape(ring, *PLANE_SHAPE, mesh.shape["layer"])
     split_mesh = Mesh(devices, (RING, *PLANE, "layer"))
     dp = (RING, *PLANE)

time: 135 us -> 130 us (0.963)
  blocking collectives: 55.1 us -> 17.9 us
  waiting for transfers between devices: 40 us -> 63.7 us
  starting transfers between devices: 27.6 us -> 35.9 us
    all_gather x1 -> x0, blocking collectives: 30.7 us -> none  [shards(): every = lax.all_gather(reduced, RING, axis=0, tiled=False)]
    all_to_all x3 -> x4, waiting for transfers between devices: 39.5 us -> 63.2 us  [exchange(): return lax.all_to_all(chunks, axis, 0, 0, tiled=True)]
    all_to_all x3 -> x4, starting transfers between devices: 24.3 us -> 31.9 us  [exchange(): return lax.all_to_all(chunks, axis, 0, 0, tiled=True)]
    all_to_all x1, blocking collectives: 24.5 us -> 17.9 us  [exchange(): return lax.all_to_all(chunks, axis, 0, 0, tiled=True)]
  transfers between devices with their start and end apart: 4 -> 5, of which waited for: 4 -> 5; matrix products, arithmetic and copies ran while one was open for 3% -> 2% of each run, Pallas kernels for 0% -> 0%
where the time goes in v6:
time: 130 us; the launch traced here: 129 us
  waiting for transfers between devices  63.7 us (49%)
  starting transfers between devices  35.9 us (28%)
  blocking collectives  17.9 us (14%)
  Pallas kernels  7.23 us (6%)
  other arithmetic  2.33 us (2%)
  between operations  1.57 us (1%)
    all_to_all x4, waiting for transfers between devices, exchange(): return lax.all_to_all(chunks, axis, 0, 0, tiled=True)  63.2 us
    all_to_all x4, starting transfers between devices, exchange(): return lax.all_to_all(chunks, axis, 0, 0, tiled=True)  31.9 us
    all_to_all x1, blocking collectives, exchange(): return lax.all_to_all(chunks, axis, 0, 0, tiled=True)  17.9 us
    ppermute x1, starting transfers between devices, shards(): weights = join(halves, lax.ppermute(halves, 'c', [(0, 1), (1, 0)]))  3.98 us
  transfers between devices with their start and end apart: 5, of which 5 were waited for; matrix products, arithmetic and copies ran while one was open for 2% of the time, Pallas kernels for 0%

profile of v6, /device:TPU:1, one launch (start us, length us, event | category | flops | bytes accessed | tf_op | source)
XLA Modules:
  0.0 129.2 jit_solution(14801857044233642736)
XLA Ops:
  0.6 2.5 %split.1 = bf16[16,288,128]{2,1,0:T(8,128)(2,1)} custom-call(bf16[256,2048]{1,0:T(8,128)(2,1)} %bitcast.24, f32[3,2,2048]{2,1,0:T(2,128)} %bitcast.27, f32[3,2,2048]{2,1,0:T(2,128)} %bitcast.28, f32[3,2,2048]{2,1,0:T(2,128)} %bitcast.26), custom_call_target="tpu_custom_call" | custom-call | tf_op jit(solution)/shard_map/split/pallas_call | solution.py:77
  3.2 10.5 %all-to-all-start = ((bf16[16,288,128]{2,1,0:T(8,128)(2,1)}), bf16[16,288,128]{2,1,0:T(8,128)(2,1)S(1)}, u32[]{:S(2)}, u32[]{:S(2)}) async-start(bf16[16,288,128]{2,1,0:T(8,128)(2,1)} %split.1), calls=%async_computation | async-start | bytes 2359296 | tf_op jit(solution)/shard_map/all_to_all | solution.py:38
  13.7 0.2 convert_reduce_fusion
  14.0 0.1 add.312
  14.2 0.1 add_add_fusion
  14.2 0.1 add.326
  14.4 0.1 iota_add_fusion
  14.5 0.1 add.316
  14.6 0.2 select_reduce_fusion.1
  14.9 0.1 fusion.2
  15.0 0.1 fusion.route
  15.1 16.0 %all-to-all-done.raw = bf16[16,288,128]{2,1,0:T(8,128)(2,1)S(1)} async-done(((bf16[16,288,128]{2,1,0:T(8,128)(2,1)}), bf16[16,288,128]{2,1,0:T(8,128)(2,1)S(1)}, u32[]{:S(2)}, u32[]{:S(2)}) %all-to-all-start) | async-done | bytes 1179680 | tf_op jit(solution)/shard_map/all_to_all | solution.py:38
  31.0 1.1 pack.1
  32.2 10.7 %all-to-all-start.1 = ((bf16[8,112,128]{2,1,0:T(8,128)(2,1)}), bf16[8,112,128]{2,1,0:T(8,128)(2,1)S(1)}, u32[]{:S(2)}, u32[]{:S(2)}) async-start(bf16[8,112,128]{2,1,0:T(8,128)(2,1)} %pack.1), calls=%async_computation.1 | async-start | bytes 458752 | tf_op jit(solution)/shard_map/all_to_all | solution.py:38
  42.8 0.1 select_reduce_fusion
  43.0 0.1 fusion.8
  43.0 0.1 add.340
  43.1 0.1 fusion.3.take
  43.2 14.9 %all-to-all-done.1.got = bf16[8,112,128]{2,1,0:T(8,128)(2,1)S(1)} async-done(((bf16[8,112,128]{2,1,0:T(8,128)(2,1)}), bf16[8,112,128]{2,1,0:T(8,128)(2,1)S(1)}, u32[]{:S(2)}, u32[]{:S(2)}) %all-to-all-start.1) | async-done | bytes 229408 | tf_op jit(solution)/shard_map/all_to_all | solution.py:38
  58.1 0.9 reduce.1
  59.1 7.2 %all-to-all-start.2 = ((bf16[8,192,128]{2,1,0:T(8,128)(2,1)}), bf16[8,192,128]{2,1,0:T(8,128)(2,1)S(1)}, u32[]{:S(2)}, u32[]{:S(2)}) async-start(bf16[8,192,128]{2,1,0:T(8,128)(2,1)} %reduce.1), calls=%async_computation.2 | async-start | bytes 786432 | tf_op jit(solution)/shard_map/all_to_all | solution.py:38
  66.4 25.0 %all-to-all-done.2.every.refs_0_ = bf16[8,192,128]{2,1,0:T(8,128)(2,1)S(1)} async-done(((bf16[8,192,128]{2,1,0:T(8,128)(2,1)}), bf16[8,192,128]{2,1,0:T(8,128)(2,1)S(1)}, u32[]{:S(2)}, u32[]{:S(2)}) %all-to-all-start.2) | async-done | bytes 393248 | tf_op jit(solution)/shard_map/all_to_all | solution.py:38
  91.4 0.2 send.1
  91.6 17.9 %all_to_all.25.refs_1_ = f32[64,8,128]{2,1,0:T(8,128)S(1)} all-to-all(f32[64,8,128]{2,1,0:T(8,128)S(1)} %bitcast.23), channel_id=1, replica_groups=mesh['z'=8,'pair'=2,'x'=4,'c'=2,'layer'=4] {'pair','x','c','layer'}, dimensions={0} | all-to-all | bytes 524288 | tf_op jit(solution)/shard_map/all_to_all | solution.py:38
  109.5 1.2 step.1
  110.7 3.5 %all-to-all-start.4 = ((bf16[8,256,128]{2,1,0:T(8,128)(2,1)}), bf16[8,256,128]{2,1,0:T(8,128)(2,1)S(1)}, u32[]{:S(2)}, u32[]{:S(2)}) async-start(bf16[8,256,128]{2,1,0:T(8,128)(2,1)} %get-tuple-element.8), calls=%async_computation.4 | async-start | bytes 1048576 | tf_op jit(solution)/shard_map/all_to_all | solution.py:38
  114.2 0.2 compare_reduce_fusion
  115.1 7.3 %all-to-all-done.4.mine = bf16[8,256,128]{2,1,0:T(8,128)(2,1)S(1)} async-done(((bf16[8,256,128]{2,1,0:T(8,128)(2,1)}), bf16[8,256,128]{2,1,0:T(8,128)(2,1)S(1)}, u32[]{:S(2)}, u32[]{:S(2)}) %all-to-all-start.4) | async-done | bytes 524320 | tf_op jit(solution)/shard_map/all_to_all | solution.py:38
  122.4 4.0 %collective-permute-start = (bf16[8,256,128]{2,1,0:T(8,128)(2,1)S(1)}, bf16[8,256,128]{2,1,0:T(8,128)(2,1)S(1)}, u32[]{:S(2)}, u32[]{:S(2)}) collective-permute-start(bf16[8,256,128]{2,1,0:T(8,128)(2,1)S(1)} %all-to-all-done.4.mine), channel_id=1, source_target_pairs={{0,4},{4,0},{1,5},{5,1},{2,6},{6,2},{3,7},{7,3},{8,12},{12,8},{9,1... | collective-permute-start | bytes 1572872 | tf_op jit(solution)/shard_map/ppermute | solution.py:271
  126.5 0.9 broadcast_select_fusion
  127.4 0.5 collective-permute-done.other
  127.9 1.3 join.1
  (26 shorter events, 0.3 us)
Async XLA Ops:
  3.2 10.5 %copy-start.3 = (s32[1,128]{1,0:T(1,128)S(1)}, s32[1,128]{1,0:T(1,128)}, u32[]{:S(2)}) copy-start(s32[1,128]{1,0:T(1,128)} %param.11) | copy-start | bytes 1540
  3.2 10.5 %copy-start.4 = (s32[1,128]{1,0:T(1,128)S(1)}, s32[1,128]{1,0:T(1,128)}, u32[]{:S(2)}) copy-start(s32[1,128]{1,0:T(1,128)} %param.10) | copy-start | bytes 1540
  3.2 27.9 %all-to-all-start = ((bf16[16,288,128]{2,1,0:T(8,128)(2,1)}), bf16[16,288,128]{2,1,0:T(8,128)(2,1)S(1)}, u32[]{:S(2)}, u32[]{:S(2)}) async-start(bf16[16,288,128]{2,1,0:T(8,128)(2,1)} %split.1), calls=%async_computation | async-start | bytes 2359296 | tf_op jit(solution)/shard_map/all_to_all | solution.py:38
  32.2 26.0 %all-to-all-start.1 = ((bf16[8,112,128]{2,1,0:T(8,128)(2,1)}), bf16[8,112,128]{2,1,0:T(8,128)(2,1)S(1)}, u32[]{:S(2)}, u32[]{:S(2)}) async-start(bf16[8,112,128]{2,1,0:T(8,128)(2,1)} %pack.1), calls=%async_computation.1 | async-start | bytes 458752 | tf_op jit(solution)/shard_map/all_to_all | solution.py:38
  59.1 32.3 %all-to-all-start.2 = ((bf16[8,192,128]{2,1,0:T(8,128)(2,1)}), bf16[8,192,128]{2,1,0:T(8,128)(2,1)S(1)}, u32[]{:S(2)}, u32[]{:S(2)}) async-start(bf16[8,192,128]{2,1,0:T(8,128)(2,1)} %reduce.1), calls=%async_computation.2 | async-start | bytes 786432 | tf_op jit(solution)/shard_map/all_to_all | solution.py:38
  109.5 17.0 %copy-start = (f32[1,3,2,2048]{3,2,1,0:T(2,128)S(1)}, f32[1,3,2,2048]{3,2,1,0:T(2,128)}, u32[]{:S(2)}) copy-start(f32[1,3,2,2048]{3,2,1,0:T(2,128)} %param.9) | copy-start | bytes 147460
  109.5 17.0 %copy-start.1 = (f32[1,3,2,2048]{3,2,1,0:T(2,128)S(1)}, f32[1,3,2,2048]{3,2,1,0:T(2,128)}, u32[]{:S(2)}) copy-start(f32[1,3,2,2048]{3,2,1,0:T(2,128)} %param.7) | copy-start | bytes 147460
  109.5 17.0 %copy-start.2 = (f32[1,3,2,2048]{3,2,1,0:T(2,128)S(1)}, f32[1,3,2,2048]{3,2,1,0:T(2,128)}, u32[]{:S(2)}) copy-start(f32[1,3,2,2048]{3,2,1,0:T(2,128)} %param.8) | copy-start | bytes 147460
  110.7 11.7 %all-to-all-start.4 = ((bf16[8,256,128]{2,1,0:T(8,128)(2,1)}), bf16[8,256,128]{2,1,0:T(8,128)(2,1)S(1)}, u32[]{:S(2)}, u32[]{:S(2)}) async-start(bf16[8,256,128]{2,1,0:T(8,128)(2,1)} %get-tuple-element.8), calls=%async_computation.4 | async-start | bytes 1048576 | tf_op jit(solution)/shard_map/all_to_all | solution.py:38
  122.4 5.5 %collective-permute-start = (bf16[8,256,128]{2,1,0:T(8,128)(2,1)S(1)}, bf16[8,256,128]{2,1,0:T(8,128)(2,1)S(1)}, u32[]{:S(2)}, u32[]{:S(2)}) collective-permute-start(bf16[8,256,128]{2,1,0:T(8,128)(2,1)S(1)} %all-to-all-done.4.mine), channel_id=1, source_target_pairs={{0,4},{4,0},{1,5},{5,1},{2,6},{6,2},{3,7},{7,3},{8,12},{12,8},{9,1... | collective-permute-start | bytes 1572872 | tf_op jit(solution)/shard_map/ppermute | solution.py:271

commit v7 on v6

--- a/solution.py
+++ b/solution.py
@@ -48,72 +48,106 @@
 
 
 VMEM = pl.BlockSpec(memory_space=pltpu.VMEM)
+SMEM = pl.BlockSpec(memory_space=pltpu.SMEM)
+ANY = pl.BlockSpec(memory_space=pl.ANY)
 
 
 def near(value):
     return pltpu.with_memory_space_constraint(value, pltpu.VMEM)
 
 
-def split_kernel(grads, master, first, second, out, rows):
+def split_kernel(grads, master, first, second, out, rows, terms, grad_sem, term_sem):
     plane, _, wide = out.shape
     count = grads.shape[0]
-    for k in range(plane):
-        out[k, :count, :] = grads[:, k * wide : (k + 1) * wide]
+    moves = [
+        pltpu.make_async_copy(
+            grads.at[:, pl.ds(k * wide, wide)], out.at[k, pl.ds(0, count), :], grad_sem.at[k]
+        )
+        for k in range(plane)
+    ]
+    for move in moves:
+        move.start()
     rows[...] = jnp.zeros_like(rows)
     capacity, slab, _ = master.shape
     for i, state in enumerate((master, first, second)):
         for s in range(capacity):
             rows[i, s * slab : (s + 1) * slab, :] = state[s]
     high, low = two_terms(rows[0])
-    terms = (high, low, rows[1].astype(jnp.bfloat16), rows[2].astype(jnp.bfloat16))
-    for t, term in enumerate(terms):
-        at = count + t * SLOT_ROWS
+    values = (high, low, rows[1].astype(jnp.bfloat16), rows[2].astype(jnp.bfloat16))
+    for t, value in enumerate(values):
         for k in range(plane):
-            out[k, at : at + SLOT_ROWS, :] = term[:, k * wide : (k + 1) * wide]
+            at = slice(t * SLOT_ROWS, (t + 1) * SLOT_ROWS)
+            terms[k, at, :] = value[:, k * wide : (k + 1) * wide]
+    last = pltpu.make_async_copy(terms, out.at[:, pl.ds(count, terms.shape[1]), :], term_sem)
+    last.start()
+    for move in moves:
+        move.wait()
+    last.wait()
 
 
 def split(grads, master, first, second, plane):
     count, width = grads.shape
+    wide = width // plane
     return pl.pallas_call(
         split_kernel,
-        out_shape=pltpu.VMEM((plane, count + KINDS * SLOT_ROWS, width // plane), grads.dtype),
-        in_specs=[pl.BlockSpec(memory_space=pltpu.VMEM)] * 4,
-        out_specs=pl.BlockSpec(memory_space=pltpu.VMEM),
-        scratch_shapes=[pltpu.VMEM((3, SLOT_ROWS, width), jnp.float32)],
+        out_shape=jax.ShapeDtypeStruct((plane, count + KINDS * SLOT_ROWS, wide), grads.dtype),
+        in_specs=[ANY, VMEM, VMEM, VMEM],
+        out_specs=ANY,
+        scratch_shapes=[
+            pltpu.VMEM((3, SLOT_ROWS, width), jnp.float32),
+            pltpu.VMEM((plane, KINDS * SLOT_ROWS, wide), grads.dtype),
+            pltpu.SemaphoreType.DMA((plane,)),
+            pltpu.SemaphoreType.DMA,
+        ],
         name="split",
     )(grads, master, first, second)
 
 
-def join_kernel(core, mine, other, out):
-    count, _, wide = mine.shape
-
-    def put(first, second):
-        for x in range(count):
-            out[:, 2 * x * wide : (2 * x + 1) * wide] = first[x]
-            out[:, (2 * x + 1) * wide : (2 * x + 2) * wide] = second[x]
-
-    @pl.when(core[0] == 0)
-    def _():
-        put(mine, other)
-
-    @pl.when(core[0] == 1)
-    def _():
-        put(other, mine)
-
-
-def join(mine, other):
-    count, rows, wide = mine.shape
+def join_kernel(core, strips, *refs):
+    out, sem = refs[-2:]
+    count, _, wide = strips.shape
+    moves = [
+        pltpu.make_async_copy(
+            strips.at[i],
+            out.at[:, pl.ds(pl.multiple_of((2 * i + core[0]) * wide, wide), wide)],
+            sem.at[i],
+        )
+        for i in range(count)
+    ]
+    for move in moves:
+        move.start()
+    for move in moves:
+        move.wait()
+
+
+def join(core, strips, *before):
+    count, rows, wide = strips.shape
     return pl.pallas_call(
         join_kernel,
-        out_shape=jax.ShapeDtypeStruct((rows, 2 * count * wide), mine.dtype),
-        in_specs=[
-            pl.BlockSpec(memory_space=pltpu.SMEM),
-            pl.BlockSpec(memory_space=pltpu.VMEM),
-            pl.BlockSpec(memory_space=pltpu.VMEM),
-        ],
-        out_specs=pl.BlockSpec(memory_space=pltpu.VMEM),
+        out_shape=jax.ShapeDtypeStruct((rows, 2 * count * wide), strips.dtype),
+        in_specs=[SMEM, VMEM] + [ANY] * len(before),
+        out_specs=ANY,
+        scratch_shapes=[pltpu.SemaphoreType.DMA((count,))],
+        input_output_aliases={2: 0} if before else {},
         name="join",
-    )(lax.axis_index("c").astype(jnp.int32).reshape(1), near(mine), near(other))
+    )(core.reshape(1), near(strips), *before)
+
+
+def own_kernel(at, got, rms, master, first, second, *refs):
+    outs, rows = refs[:3], refs[3]
+    wide = got.shape[2]
+    count = rows.shape[1] // wide
+    layers = got.shape[0] // count
+    for k in range(count):
+        rows[:, k * wide : (k + 1) * wide] = got[k * layers + at[0]]
+    clip_factor = jnp.minimum(1.0, 1.0 / rms[:, :1])
+    capacity, slab, _ = master.shape
+    for s in range(capacity):
+        old = (master[s], first[s], second[s])
+        new = adamw(*old, rows[s * slab : (s + 1) * slab, :] * clip_factor)
+        keep = at[1 + s] > 0
+        for out, n, o in zip(outs, new, old, strict=True):
+            out[s] = jnp.where(keep, n, o)
 
 
 def pack_kernel(raw, order, route, out):
@@ -232,20 +266,23 @@
     take = comes.reshape(KINDS * part, 1) == chunks[None, :]
 
     raw = exchange(split(micro_grads[0, 0], master[0], moment_one[0], moment_two[0], plane), PLANE)
+    tables = [t.astype(bf16) for t in (order, route, take, pick, place)]
+    raw, *tables = lax.optimization_barrier((raw, *tables))
+    order, route, take, pick, place = [near(t) for t in tables]
     packed = pl.pallas_call(
         pack_kernel,
         out_shape=pltpu.VMEM((ring, 2 * part + KINDS * pair, wide), bf16),
         in_specs=[VMEM] * 3,
         out_specs=VMEM,
         name="pack",
-    )(near(raw), near(order.astype(bf16)), near(route.astype(bf16)))
+    )(near(raw), order, route)
     reduced = pl.pallas_call(
         reduce_kernel,
         out_shape=pltpu.VMEM((ring, (2 + KINDS) * part, wide), bf16),
         in_specs=[VMEM] * 2,
         out_specs=VMEM,
         name="reduce",
-    )(near(exchange(packed, RING)), near(take.astype(bf16)))
+    )(near(exchange(packed, RING)), take)
     every = exchange(reduced, RING)
 
     sent = pl.pallas_call(
@@ -254,7 +291,7 @@
         in_specs=[VMEM] * 2,
         out_specs=VMEM,
         name="send",
-    )(near(every), near(pick.astype(bf16)))
+    )(near(every), pick)
     got = exchange(sent.reshape(plane * layers, SLOT_ROWS, wide), (*PLANE, "layer"))
 
     copies, rms = pl.pallas_call(
@@ -266,22 +303,27 @@
         in_specs=[VMEM] * 3,
         out_specs=(VMEM, VMEM),
         name="step",
-    )(near(every), near(got), near(place.astype(bf16)))
-    halves = exchange(copies, HALF)
-    weights = join(halves, lax.ppermute(halves, "c", [(0, 1), (1, 0)]))
-    grad_rms = rms[0, 0]
-    clip_factor = jnp.minimum(1.0, 1.0 / grad_rms)
-
-    own = got.reshape(plane, layers, SLOT_ROWS, wide)
-    own = lax.dynamic_index_in_dim(own, lax.axis_index("layer"), 1, keepdims=False)
-    own = own[:, :lines].transpose(1, 0, 2).reshape(capacity, slab, width) * clip_factor
-    new = adamw(master[0], moment_one[0], moment_two[0], own)
+    )(near(every), near(got), place)
+    core = lax.axis_index("c")
+    halves, got, rms = lax.optimization_barrier((exchange(copies, HALF), got, rms))
+    others = lax.ppermute(halves, "c", [(0, 1), (1, 0)])
+    weights = join(core, halves)
+
     my_slots = lax.axis_index((RING, *PLANE)) * SLOT_ROWS
     my_slots = my_slots + slab * jnp.arange(capacity, dtype=i32)
-    keep = jnp.any(line[None, :] == my_slots[:, None], axis=1)[:, None, None]
-    old = (master[0], moment_one[0], moment_two[0])
-    new = [jnp.where(keep, n, o)[None] for n, o in zip(new, old, strict=True)]
-    return (*new, weights[None], grad_rms)
+    keep = jnp.any(line[None, :] == my_slots[:, None], axis=1).astype(i32)
+    at = jnp.concatenate([lax.axis_index("layer").astype(i32).reshape(1), keep])
+    new = pl.pallas_call(
+        own_kernel,
+        out_shape=(jax.ShapeDtypeStruct(master.shape[1:], f32),) * 3,
+        in_specs=[SMEM] + [VMEM] * 5,
+        out_specs=(VMEM,) * 3,
+        scratch_shapes=[pltpu.VMEM((SLOT_ROWS, width), f32)],
+        name="own",
+    )(at, near(got), near(rms), master[0], moment_one[0], moment_two[0])
+    others, weights = lax.optimization_barrier((others, weights))
+    weights = join(1 - core, others, weights)
+    return (new[0][None], new[1][None], new[2][None], weights[None], rms[0, 0])
 
 
 def solution(mesh):

time: 130 us -> 160 us (1.23)
  blocking collectives: 17.9 us -> 87.7 us
  waiting for transfers between devices: 63.7 us -> 15.5 us
  Pallas kernels: 7.23 us -> 38.6 us
  starting transfers between devices: 35.9 us -> 14.5 us
    all_to_all x1 -> x4, blocking collectives: 17.9 us -> 87.7 us  [exchange(): return lax.all_to_all(chunks, axis, 0, 0, tiled=True)]
    all_to_all x4 -> x1, waiting for transfers between devices: 63.2 us -> 15.5 us  [exchange(): return lax.all_to_all(chunks, axis, 0, 0, tiled=True)]
    pallas_call x1 -> x2, Pallas kernels: 2.54 us -> 35.5 us  [the longest x1 33.9 us: split(): pl.pallas_call(split_kernel, out_shape=jax.ShapeDtypeStruct((plane, count...]
    all_to_all x4 -> x1, starting transfers between devices: 31.9 us -> 10.4 us  [exchange(): return lax.all_to_all(chunks, axis, 0, 0, tiled=True)]
  transfers between devices with their start and end apart: 5 -> 2, of which waited for: 5 -> 1; matrix products, arithmetic and copies ran while one was open for 2% -> 2% of each run, Pallas kernels for 0% -> 2%
where the time goes in v7:
time: 160 us
  blocking collectives  87.7 us (55%)
  Pallas kernels  38.6 us (24%)
  waiting for transfers between devices  15.5 us (10%)
  starting transfers between devices  14.5 us (9%)
  other arithmetic  2.09 us (1%)
    all_to_all x4, blocking collectives, exchange(): return lax.all_to_all(chunks, axis, 0, 0, tiled=True)  87.7 us
    pallas_call x1, Pallas kernels, split(): pl.pallas_call(split_kernel, out_shape=jax.ShapeDtypeStruct((plane, count...  33.9 us
    all_to_all x1, waiting for transfers between devices, exchange(): return lax.all_to_all(chunks, axis, 0, 0, tiled=True)  15.5 us
    all_to_all x1, starting transfers between devices, exchange(): return lax.all_to_all(chunks, axis, 0, 0, tiled=True)  10.4 us
    ppermute x1, starting transfers between devices, shards(): others = lax.ppermute(halves, 'c', [(0, 1), (1, 0)])  4.16 us
  transfers between devices with their start and end apart: 2, of which 1 were waited for; matrix products, arithmetic and copies ran while one was open for 2% of the time, Pallas kernels for 2%

profile of v7, /device:TPU:1, one launch (start us, length us, event | category | flops | bytes accessed | tf_op | source)
XLA Modules:
  0.0 159.8 jit_solution(2782420720824622417)
XLA Ops:
  0.6 33.9 %split.1 = bf16[16,288,128]{2,1,0:T(8,128)(2,1)} custom-call(bf16[256,2048]{1,0:T(8,128)(2,1)} %bitcast.23, f32[3,2,2048]{2,1,0:T(2,128)} %bitcast.24, f32[3,2,2048]{2,1,0:T(2,128)} %bitcast.26, f32[3,2,2048]{2,1,0:T(2,128)} %bitcast.28), custom_call_target="tpu_custom_call" | custom-call | tf_op jit(solution)/shard_map/split/pallas_call | solution.py:91
  34.5 10.4 %all-to-all-start = ((bf16[16,288,128]{2,1,0:T(8,128)(2,1)}), bf16[16,288,128]{2,1,0:T(8,128)(2,1)S(1)}, u32[]{:S(2)}, u32[]{:S(2)}) async-start(bf16[16,288,128]{2,1,0:T(8,128)(2,1)} %split.1), calls=%async_computation | async-start | bytes 2359296 | tf_op jit(solution)/shard_map/all_to_all | solution.py:38
  44.9 0.2 convert_reduce_fusion
  45.2 0.1 iota_add_fusion.1
  45.2 0.1 add.287
  45.4 0.1 add_add_fusion
  45.5 0.1 add.301
  45.6 0.1 iota_add_fusion
  45.7 0.1 add.291
  45.8 0.1 select_reduce_fusion
  46.0 0.1 and_select_fusion
  46.1 0.1 add.315
  46.2 0.2 select_reduce_fusion.1
  46.4 0.1 compare_convert_fusion.pick
  46.5 0.1 fusion.3.take
  46.6 0.1 fusion.2
  46.7 0.1 fusion.route
  46.8 15.5 %all-to-all-done.raw = bf16[16,288,128]{2,1,0:T(8,128)(2,1)S(1)} async-done(((bf16[16,288,128]{2,1,0:T(8,128)(2,1)}), bf16[16,288,128]{2,1,0:T(8,128)(2,1)S(1)}, u32[]{:S(2)}, u32[]{:S(2)}) %all-to-all-start) | async-done | bytes 1179680 | tf_op jit(solution)/shard_map/all_to_all | solution.py:38
  62.3 0.5 pack.1
  62.7 25.8 %all_to_all.25.got = bf16[8,112,128]{2,1,0:T(8,128)(2,1)S(1)} all-to-all(bf16[8,112,128]{2,1,0:T(8,128)(2,1)S(1)} %pack.1), channel_id=1, replica_groups=mesh['z'=8,'pair'=2,'x'=4,'c'=2,'layer'=4] {'z'}, dimensions={0} | all-to-all | bytes 458752 | tf_op jit(solution)/shard_map/all_to_all | solution.py:38
  88.5 0.2 reduce.1
  88.7 31.3 %all_to_all.26.every.refs_0_ = bf16[8,192,128]{2,1,0:T(8,128)(2,1)S(1)} all-to-all(bf16[8,192,128]{2,1,0:T(8,128)(2,1)S(1)} %reduce.1), channel_id=1, replica_groups=mesh['z'=8,'pair'=2,'x'=4,'c'=2,'layer'=4] {'z'}, dimensions={0} | all-to-all | bytes 786432 | tf_op jit(solution)/shard_map/all_to_all | solution.py:38
  120.0 0.2 send.1
  120.2 19.3 %all_to_all.27.refs_1_.got = f32[64,8,128]{2,1,0:T(8,128)S(1)} all-to-all(f32[64,8,128]{2,1,0:T(8,128)S(1)} %bitcast.20), channel_id=1, replica_groups=mesh['z'=8,'pair'=2,'x'=4,'c'=2,'layer'=4] {'pair','x','c','layer'}, dimensions={0} | all-to-all | bytes 524288 | tf_op jit(solution)/shard_map/all_to_all | solution.py:38
  139.5 0.6 step.1
  140.1 11.2 %all_to_all.28.strips = bf16[8,256,128]{2,1,0:T(8,128)(2,1)S(1)} all-to-all(bf16[8,256,128]{2,1,0:T(8,128)(2,1)S(1)} %get-tuple-element.27), channel_id=1, replica_groups=mesh['z'=8,'pair'=2,'x'=4,'c'=2,'layer'=4] {'pair','x'}, dimensions={0} | all-to-all | bytes 1048576 | tf_op jit(solution)/shard_map/all_to_all | solution.py:38
  151.4 4.2 %collective-permute-start = (bf16[8,256,128]{2,1,0:T(8,128)(2,1)S(1)}, bf16[8,256,128]{2,1,0:T(8,128)(2,1)S(1)}, u32[]{:S(2)}, u32[]{:S(2)}) collective-permute-start(bf16[8,256,128]{2,1,0:T(8,128)(2,1)S(1)} %all_to_all.28.strips), channel_id=1, source_target_pairs={{0,4},{4,0},{1,5},{5,1},{2,6},{6,2},{3,7},{7,3},{8,12},{12,8},{9,1... | collective-permute-start | bytes 1572872 | tf_op jit(solution)/shard_map/ppermute | solution.py:309
  155.6 0.2 compare_reduce_fusion
  155.8 0.7 pad_add_fusion.at
  156.4 0.8 join.2.refs_0_
  157.3 1.6 %own.1 = (f32[3,2,2048]{2,1,0:T(2,128)}, f32[3,2,2048]{2,1,0:T(2,128)}, f32[3,2,2048]{2,1,0:T(2,128)}) custom-call(s32[4]{0:T(128)} %pad_add_fusion.at, f32[64,8,128]{2,1,0:T(8,128)S(1)} %all_to_all.27.refs_1_.got, f32[1,128]{1,0:T(1,128)S(1)} %copy-done, f32[3,2,2048]{2,1,0:T(2,128)} %bitcast.25, f32[3,2,2048]{2,1,0:T(2,128)} %bitcast.27, ...), custom_call_target="tpu_custom_call" | custom-call | tf_op jit(solution)/shard_map/own/pallas_call | solution.py:316
  158.9 0.8 join.3
  (17 shorter events, 0.1 us)
Async XLA Ops:
  34.5 10.4 %copy-start.1 = (s32[1,128]{1,0:T(1,128)S(1)}, s32[1,128]{1,0:T(1,128)}, u32[]{:S(2)}) copy-start(s32[1,128]{1,0:T(1,128)} %param.11) | copy-start | bytes 1540
  34.5 10.4 %copy-start.2 = (s32[1,128]{1,0:T(1,128)S(1)}, s32[1,128]{1,0:T(1,128)}, u32[]{:S(2)}) copy-start(s32[1,128]{1,0:T(1,128)} %param.10) | copy-start | bytes 1540
  34.5 27.7 %all-to-all-start = ((bf16[16,288,128]{2,1,0:T(8,128)(2,1)}), bf16[16,288,128]{2,1,0:T(8,128)(2,1)S(1)}, u32[]{:S(2)}, u32[]{:S(2)}) async-start(bf16[16,288,128]{2,1,0:T(8,128)(2,1)} %split.1), calls=%async_computation | async-start | bytes 2359296 | tf_op jit(solution)/shard_map/all_to_all | solution.py:38
  140.1 17.1 %copy-start = (f32[1,128]{1,0:T(1,128)S(1)}, f32[1,128]{1,0:T(1,128)}, u32[]{:S(2)}) copy-start(f32[1,128]{1,0:T(1,128)} %get-tuple-element.30.rms) | copy-start | bytes 1540
  151.4 7.6 %collective-permute-start = (bf16[8,256,128]{2,1,0:T(8,128)(2,1)S(1)}, bf16[8,256,128]{2,1,0:T(8,128)(2,1)S(1)}, u32[]{:S(2)}, u32[]{:S(2)}) collective-permute-start(bf16[8,256,128]{2,1,0:T(8,128)(2,1)S(1)} %all_to_all.28.strips), channel_id=1, source_target_pairs={{0,4},{4,0},{1,5},{5,1},{2,6},{6,2},{3,7},{7,3},{8,12},{12,8},{9,1... | collective-permute-start | bytes 1572872 | tf_op jit(solution)/shard_map/ppermute | solution.py:309

commit v8 on v7

--- a/solution.py
+++ b/solution.py
@@ -56,17 +56,19 @@
     return pltpu.with_memory_space_constraint(value, pltpu.VMEM)
 
 
-def split_kernel(grads, master, first, second, out, rows, terms, grad_sem, term_sem):
+def split_kernel(grads, master, first, second, out, held, rows, terms, in_sem, out_sem, term_sem):
     plane, _, wide = out.shape
     count = grads.shape[0]
-    moves = [
+    pieces = in_sem.shape[0]
+    size = count // pieces
+    arrivals = [
         pltpu.make_async_copy(
-            grads.at[:, pl.ds(k * wide, wide)], out.at[k, pl.ds(0, count), :], grad_sem.at[k]
+            grads.at[pl.ds(i * size, size), :], held.at[pl.ds(i * size, size), :], in_sem.at[i]
         )
-        for k in range(plane)
+        for i in range(pieces)
     ]
-    for move in moves:
-        move.start()
+    for arrival in arrivals:
+        arrival.start()
     rows[...] = jnp.zeros_like(rows)
     capacity, slab, _ = master.shape
     for i, state in enumerate((master, first, second)):
@@ -78,25 +80,39 @@
         for k in range(plane):
             at = slice(t * SLOT_ROWS, (t + 1) * SLOT_ROWS)
             terms[k, at, :] = value[:, k * wide : (k + 1) * wide]
-    last = pltpu.make_async_copy(terms, out.at[:, pl.ds(count, terms.shape[1]), :], term_sem)
-    last.start()
+    moves = [
+        pltpu.make_async_copy(terms, out.at[:, pl.ds(count, terms.shape[1]), :], term_sem)
+    ]
+    moves[0].start()
+    for i, arrival in enumerate(arrivals):
+        arrival.wait()
+        for k in range(plane):
+            move = pltpu.make_async_copy(
+                held.at[pl.ds(i * size, size), pl.ds(k * wide, wide)],
+                out.at[k, pl.ds(i * size, size), :],
+                out_sem.at[i, k],
+            )
+            move.start()
+            moves.append(move)
     for move in moves:
         move.wait()
-    last.wait()
 
 
 def split(grads, master, first, second, plane):
     count, width = grads.shape
     wide = width // plane
+    pieces = 4
     return pl.pallas_call(
         split_kernel,
         out_shape=jax.ShapeDtypeStruct((plane, count + KINDS * SLOT_ROWS, wide), grads.dtype),
         in_specs=[ANY, VMEM, VMEM, VMEM],
         out_specs=ANY,
         scratch_shapes=[
+            pltpu.VMEM((count, width), grads.dtype),
             pltpu.VMEM((3, SLOT_ROWS, width), jnp.float32),
             pltpu.VMEM((plane, KINDS * SLOT_ROWS, wide), grads.dtype),
-            pltpu.SemaphoreType.DMA((plane,)),
+            pltpu.SemaphoreType.DMA((pieces,)),
+            pltpu.SemaphoreType.DMA((pieces, plane)),
             pltpu.SemaphoreType.DMA,
         ],
         name="split",
@@ -266,8 +282,12 @@
     take = comes.reshape(KINDS * part, 1) == chunks[None, :]
 
     raw = exchange(split(micro_grads[0, 0], master[0], moment_one[0], moment_two[0], plane), PLANE)
+    my_slots = lax.axis_index((RING, *PLANE)) * SLOT_ROWS
+    my_slots = my_slots + slab * jnp.arange(capacity, dtype=i32)
+    keep = jnp.any(line[None, :] == my_slots[:, None], axis=1).astype(i32)
+    at = jnp.concatenate([lax.axis_index("layer").astype(i32).reshape(1), keep])
     tables = [t.astype(bf16) for t in (order, route, take, pick, place)]
-    raw, *tables = lax.optimization_barrier((raw, *tables))
+    raw, at, *tables = lax.optimization_barrier((raw, at, *tables))
     order, route, take, pick, place = [near(t) for t in tables]
     packed = pl.pallas_call(
         pack_kernel,
@@ -309,10 +329,6 @@
     others = lax.ppermute(halves, "c", [(0, 1), (1, 0)])
     weights = join(core, halves)
 
-    my_slots = lax.axis_index((RING, *PLANE)) * SLOT_ROWS
-    my_slots = my_slots + slab * jnp.arange(capacity, dtype=i32)
-    keep = jnp.any(line[None, :] == my_slots[:, None], axis=1).astype(i32)
-    at = jnp.concatenate([lax.axis_index("layer").astype(i32).reshape(1), keep])
     new = pl.pallas_call(
         own_kernel,
         out_shape=(jax.ShapeDtypeStruct(master.shape[1:], f32),) * 3,
@@ -320,7 +336,7 @@
         out_specs=(VMEM,) * 3,
         scratch_shapes=[pltpu.VMEM((SLOT_ROWS, width), f32)],
         name="own",
-    )(at, near(got), near(rms), master[0], moment_one[0], moment_two[0])
+    )(at, near(got), near(rms), *[near(o[0]) for o in (master, moment_one, moment_two)])
     others, weights = lax.optimization_barrier((others, weights))
     weights = join(1 - core, others, weights)
     return (new[0][None], new[1][None], new[2][None], weights[None], rms[0, 0])

time: 160 us -> 129 us (0.81)
  Pallas kernels: 38.6 us -> 8 us
    pallas_call x1, Pallas kernels: 33.9 us -> 3.46 us  [split(): pl.pallas_call(split_kernel, out_shape=jax.ShapeDtypeStruct((plane, count...]
where the time goes in v8:
time: 129 us; the launch traced here: 128 us
  blocking collectives  87.7 us (68%)
  waiting for transfers between devices  14.6 us (11%)
  starting transfers between devices  14.5 us (11%)
  Pallas kernels  8 us (6%)
  other arithmetic  2.1 us (2%)
    all_to_all x4, blocking collectives, exchange(): return lax.all_to_all(chunks, axis, 0, 0, tiled=True)  87.7 us
    all_to_all x1, waiting for transfers between devices, exchange(): return lax.all_to_all(chunks, axis, 0, 0, tiled=True)  14.6 us
    all_to_all x1, starting transfers between devices, exchange(): return lax.all_to_all(chunks, axis, 0, 0, tiled=True)  10.4 us
    ppermute x1, starting transfers between devices, shards(): others = lax.ppermute(halves, 'c', [(0, 1), (1, 0)])  4.16 us
    pallas_call x1, Pallas kernels, split(): pl.pallas_call(split_kernel, out_shape=jax.ShapeDtypeStruct((plane, count...  3.46 us
  transfers between devices with their start and end apart: 2, of which 1 were waited for; matrix products, arithmetic and copies ran while one was open for 2% of the time, Pallas kernels for 2%

profile of v8, /device:TPU:1, one launch (start us, length us, event | category | flops | bytes accessed | tf_op | source)
XLA Modules:
  0.0 128.4 jit_solution(14831209487598350746)
XLA Ops:
  0.6 3.5 %split.1 = bf16[16,288,128]{2,1,0:T(8,128)(2,1)} custom-call(bf16[256,2048]{1,0:T(8,128)(2,1)} %bitcast.29, f32[3,2,2048]{2,1,0:T(2,128)} %bitcast.21, f32[3,2,2048]{2,1,0:T(2,128)} %bitcast.23, f32[3,2,2048]{2,1,0:T(2,128)} %bitcast.25), custom_call_target="tpu_custom_call" | custom-call | tf_op jit(solution)/shard_map/split/pallas_call | solution.py:105
  4.1 10.4 %all-to-all-start = ((bf16[16,288,128]{2,1,0:T(8,128)(2,1)}), bf16[16,288,128]{2,1,0:T(8,128)(2,1)S(1)}, u32[]{:S(2)}, u32[]{:S(2)}) async-start(bf16[16,288,128]{2,1,0:T(8,128)(2,1)} %split.1), calls=%async_computation | async-start | bytes 2359296 | tf_op jit(solution)/shard_map/all_to_all | solution.py:38
  14.5 0.2 compare_reduce_fusion
  14.7 0.2 convert_reduce_fusion
  15.0 0.1 iota_add_fusion.1
  15.0 0.1 add.287
  15.2 0.1 add_add_fusion
  15.3 0.1 add.301
  15.4 0.1 iota_add_fusion
  15.5 0.1 add.291
  15.6 0.1 select_reduce_fusion
  15.8 0.1 and_select_fusion
  15.9 0.1 add.315
  15.9 0.7 pad_add_fusion.at
  16.6 0.2 select_reduce_fusion.1
  16.8 0.1 compare_convert_fusion.pick
  16.9 0.1 fusion.3.take
  17.0 0.1 fusion.2
  17.1 0.1 fusion.route
  17.2 14.6 %all-to-all-done.raw = bf16[16,288,128]{2,1,0:T(8,128)(2,1)S(1)} async-done(((bf16[16,288,128]{2,1,0:T(8,128)(2,1)}), bf16[16,288,128]{2,1,0:T(8,128)(2,1)S(1)}, u32[]{:S(2)}, u32[]{:S(2)}) %all-to-all-start) | async-done | bytes 1179680 | tf_op jit(solution)/shard_map/all_to_all | solution.py:38
  31.9 0.5 pack.1
  32.3 25.8 %all_to_all.25.got = bf16[8,112,128]{2,1,0:T(8,128)(2,1)S(1)} all-to-all(bf16[8,112,128]{2,1,0:T(8,128)(2,1)S(1)} %pack.1), channel_id=1, replica_groups=mesh['z'=8,'pair'=2,'x'=4,'c'=2,'layer'=4] {'z'}, dimensions={0} | all-to-all | bytes 458752 | tf_op jit(solution)/shard_map/all_to_all | solution.py:38
  58.1 0.2 reduce.1
  58.3 31.3 %all_to_all.26.every.refs_0_ = bf16[8,192,128]{2,1,0:T(8,128)(2,1)S(1)} all-to-all(bf16[8,192,128]{2,1,0:T(8,128)(2,1)S(1)} %reduce.1), channel_id=1, replica_groups=mesh['z'=8,'pair'=2,'x'=4,'c'=2,'layer'=4] {'z'}, dimensions={0} | all-to-all | bytes 786432 | tf_op jit(solution)/shard_map/all_to_all | solution.py:38
  89.6 0.2 send.1
  89.8 19.3 %all_to_all.27.refs_1_.got = f32[64,8,128]{2,1,0:T(8,128)S(1)} all-to-all(f32[64,8,128]{2,1,0:T(8,128)S(1)} %bitcast.20), channel_id=1, replica_groups=mesh['z'=8,'pair'=2,'x'=4,'c'=2,'layer'=4] {'pair','x','c','layer'}, dimensions={0} | all-to-all | bytes 524288 | tf_op jit(solution)/shard_map/all_to_all | solution.py:38
  109.1 0.6 step.1
  109.7 11.3 %all_to_all.28.strips = bf16[8,256,128]{2,1,0:T(8,128)(2,1)S(1)} all-to-all(bf16[8,256,128]{2,1,0:T(8,128)(2,1)S(1)} %get-tuple-element.29), channel_id=1, replica_groups=mesh['z'=8,'pair'=2,'x'=4,'c'=2,'layer'=4] {'pair','x'}, dimensions={0} | all-to-all | bytes 1048576 | tf_op jit(solution)/shard_map/all_to_all | solution.py:38
  121.0 4.2 %collective-permute-start = (bf16[8,256,128]{2,1,0:T(8,128)(2,1)S(1)}, bf16[8,256,128]{2,1,0:T(8,128)(2,1)S(1)}, u32[]{:S(2)}, u32[]{:S(2)}) collective-permute-start(bf16[8,256,128]{2,1,0:T(8,128)(2,1)S(1)} %all_to_all.28.strips), channel_id=1, source_target_pairs={{0,4},{4,0},{1,5},{5,1},{2,6},{6,2},{3,7},{7,3},{8,12},{12,8},{9,1... | collective-permute-start | bytes 1572872 | tf_op jit(solution)/shard_map/ppermute | solution.py:329
  125.2 0.9 join.2.refs_0_
  126.0 1.5 %own.1 = (f32[3,2,2048]{2,1,0:T(2,128)}, f32[3,2,2048]{2,1,0:T(2,128)}, f32[3,2,2048]{2,1,0:T(2,128)}) custom-call(s32[4]{0:T(128)} %pad_add_fusion.at, f32[64,8,128]{2,1,0:T(8,128)S(1)} %all_to_all.27.refs_1_.got, f32[1,128]{1,0:T(1,128)S(1)} %copy-done.3, f32[3,2,2048]{2,1,0:T(2,128)S(1)} %bitcast.22, f32[3,2,2048]{2,1,0:T(2,128)S(1)} %bitcast.24, ...), custom_call_target="tpu_custom_call" | custom-call | tf_op jit(solution)/shard_map/own/pallas_call | solution.py:332
  127.5 0.8 join.3
  (23 shorter events, 0.1 us)
Async XLA Ops:
  4.1 10.4 %copy-start.4 = (s32[1,128]{1,0:T(1,128)S(1)}, s32[1,128]{1,0:T(1,128)}, u32[]{:S(2)}) copy-start(s32[1,128]{1,0:T(1,128)} %param.11) | copy-start | bytes 1540
  4.1 10.4 %copy-start.5 = (s32[1,128]{1,0:T(1,128)S(1)}, s32[1,128]{1,0:T(1,128)}, u32[]{:S(2)}) copy-start(s32[1,128]{1,0:T(1,128)} %param.10) | copy-start | bytes 1540
  4.1 27.7 %all-to-all-start = ((bf16[16,288,128]{2,1,0:T(8,128)(2,1)}), bf16[16,288,128]{2,1,0:T(8,128)(2,1)S(1)}, u32[]{:S(2)}, u32[]{:S(2)}) async-start(bf16[16,288,128]{2,1,0:T(8,128)(2,1)} %split.1), calls=%async_computation | async-start | bytes 2359296 | tf_op jit(solution)/shard_map/all_to_all | solution.py:38
  109.7 16.3 %copy-start = (f32[1,3,2,2048]{3,2,1,0:T(2,128)S(1)}, f32[1,3,2,2048]{3,2,1,0:T(2,128)}, u32[]{:S(2)}) copy-start(f32[1,3,2,2048]{3,2,1,0:T(2,128)} %param.7) | copy-start | bytes 147460
  109.7 16.3 %copy-start.1 = (f32[1,3,2,2048]{3,2,1,0:T(2,128)S(1)}, f32[1,3,2,2048]{3,2,1,0:T(2,128)}, u32[]{:S(2)}) copy-start(f32[1,3,2,2048]{3,2,1,0:T(2,128)} %param.8) | copy-start | bytes 147460
  109.7 16.3 %copy-start.2 = (f32[1,3,2,2048]{3,2,1,0:T(2,128)S(1)}, f32[1,3,2,2048]{3,2,1,0:T(2,128)}, u32[]{:S(2)}) copy-start(f32[1,3,2,2048]{3,2,1,0:T(2,128)} %param.9) | copy-start | bytes 147460
  109.7 16.3 %copy-start.3 = (f32[1,128]{1,0:T(1,128)S(1)}, f32[1,128]{1,0:T(1,128)}, u32[]{:S(2)}) copy-start(f32[1,128]{1,0:T(1,128)} %get-tuple-element.32.rms) | copy-start | bytes 1540
  121.0 6.5 %collective-permute-start = (bf16[8,256,128]{2,1,0:T(8,128)(2,1)S(1)}, bf16[8,256,128]{2,1,0:T(8,128)(2,1)S(1)}, u32[]{:S(2)}, u32[]{:S(2)}) collective-permute-start(bf16[8,256,128]{2,1,0:T(8,128)(2,1)S(1)} %all_to_all.28.strips), channel_id=1, source_target_pairs={{0,4},{4,0},{1,5},{5,1},{2,6},{6,2},{3,7},{7,3},{8,12},{12,8},{9,1... | collective-permute-start | bytes 1572872 | tf_op jit(solution)/shard_map/ppermute | solution.py:329

commit v9 on v8

--- a/solution.py
+++ b/solution.py
@@ -56,8 +56,16 @@
     return pltpu.with_memory_space_constraint(value, pltpu.VMEM)
 
 
-def split_kernel(grads, master, first, second, out, held, rows, terms, in_sem, out_sem, term_sem):
-    plane, _, wide = out.shape
+def fill_rows(rows, states):
+    capacity, slab, _ = states[0].shape
+    for i, state in enumerate(states):
+        for s in range(capacity):
+            rows[i, s * slab : (s + 1) * slab, :] = state[s]
+        rows[i, capacity * slab :, :] = jnp.ones_like(rows[i, capacity * slab :, :])
+
+
+def split_kernel(grads, master, first, second, out, held, rows, strips, in_sem, out_sem):
+    plane, total, wide = out.shape
     count = grads.shape[0]
     pieces = in_sem.shape[0]
     size = count // pieces
@@ -69,51 +77,46 @@
     ]
     for arrival in arrivals:
         arrival.start()
-    rows[...] = jnp.zeros_like(rows)
-    capacity, slab, _ = master.shape
-    for i, state in enumerate((master, first, second)):
-        for s in range(capacity):
-            rows[i, s * slab : (s + 1) * slab, :] = state[s]
+    fill_rows(rows, (master, first, second))
     high, low = two_terms(rows[0])
     values = (high, low, rows[1].astype(jnp.bfloat16), rows[2].astype(jnp.bfloat16))
     for t, value in enumerate(values):
+        at = count + t * SLOT_ROWS
         for k in range(plane):
-            at = slice(t * SLOT_ROWS, (t + 1) * SLOT_ROWS)
-            terms[k, at, :] = value[:, k * wide : (k + 1) * wide]
-    moves = [
-        pltpu.make_async_copy(terms, out.at[:, pl.ds(count, terms.shape[1]), :], term_sem)
-    ]
-    moves[0].start()
-    for i, arrival in enumerate(arrivals):
-        arrival.wait()
-        for k in range(plane):
-            move = pltpu.make_async_copy(
-                held.at[pl.ds(i * size, size), pl.ds(k * wide, wide)],
-                out.at[k, pl.ds(i * size, size), :],
-                out_sem.at[i, k],
-            )
-            move.start()
-            moves.append(move)
+            strips[k, at : at + SLOT_ROWS, :] = value[:, k * wide : (k + 1) * wide]
+    moves = []
+    for i in range(pieces + 1):
+        at, length = i * size, size
+        if i < pieces:
+            arrivals[i].wait()
+            for k in range(plane):
+                strips[k, at : at + size, :] = held[at : at + size, k * wide : (k + 1) * wide]
+        else:
+            length = total - count
+        here = pl.ds(at, length)
+        moves.append(
+            pltpu.make_async_copy(strips.at[:, here, :], out.at[:, here, :], out_sem.at[i])
+        )
+        moves[-1].start()
     for move in moves:
         move.wait()
 
 
 def split(grads, master, first, second, plane):
     count, width = grads.shape
-    wide = width // plane
+    shape = (plane, count + KINDS * SLOT_ROWS, width // plane)
     pieces = 4
     return pl.pallas_call(
         split_kernel,
-        out_shape=jax.ShapeDtypeStruct((plane, count + KINDS * SLOT_ROWS, wide), grads.dtype),
+        out_shape=jax.ShapeDtypeStruct(shape, grads.dtype),
         in_specs=[ANY, VMEM, VMEM, VMEM],
         out_specs=ANY,
         scratch_shapes=[
             pltpu.VMEM((count, width), grads.dtype),
             pltpu.VMEM((3, SLOT_ROWS, width), jnp.float32),
-            pltpu.VMEM((plane, KINDS * SLOT_ROWS, wide), grads.dtype),
+            pltpu.VMEM(shape, grads.dtype),
             pltpu.SemaphoreType.DMA((pieces,)),
-            pltpu.SemaphoreType.DMA((pieces, plane)),
-            pltpu.SemaphoreType.DMA,
+            pltpu.SemaphoreType.DMA((pieces + 1,)),
         ],
         name="split",
     )(grads, master, first, second)
@@ -150,20 +153,20 @@
 
 
 def own_kernel(at, got, rms, master, first, second, *refs):
-    outs, rows = refs[:3], refs[3]
+    outs, rows, grads = refs[:3], refs[3], refs[4]
     wide = got.shape[2]
-    count = rows.shape[1] // wide
+    count = grads.shape[1] // wide
     layers = got.shape[0] // count
     for k in range(count):
-        rows[:, k * wide : (k + 1) * wide] = got[k * layers + at[0]]
+        grads[:, k * wide : (k + 1) * wide] = got[k * layers + at[0]]
+    fill_rows(rows, (master, first, second))
     clip_factor = jnp.minimum(1.0, 1.0 / rms[:, :1])
+    new = adamw(rows[0], rows[1], rows[2], grads[...] * clip_factor)
     capacity, slab, _ = master.shape
-    for s in range(capacity):
-        old = (master[s], first[s], second[s])
-        new = adamw(*old, rows[s * slab : (s + 1) * slab, :] * clip_factor)
-        keep = at[1 + s] > 0
-        for out, n, o in zip(outs, new, old, strict=True):
-            out[s] = jnp.where(keep, n, o)
+    for i, (out, old) in enumerate(zip(outs, (master, first, second), strict=True)):
+        rows[i] = new[i]
+        for s in range(capacity):
+            out[s] = jnp.where(at[1 + s] > 0, rows[i, s * slab : (s + 1) * slab, :], old[s])
 
 
 def pack_kernel(raw, order, route, out):
@@ -334,7 +337,10 @@
         out_shape=(jax.ShapeDtypeStruct(master.shape[1:], f32),) * 3,
         in_specs=[SMEM] + [VMEM] * 5,
         out_specs=(VMEM,) * 3,
-        scratch_shapes=[pltpu.VMEM((SLOT_ROWS, width), f32)],
+        scratch_shapes=[
+            pltpu.VMEM((3, SLOT_ROWS, width), f32),
+            pltpu.VMEM((SLOT_ROWS, width), f32),
+        ],
         name="own",
     )(at, near(got), near(rms), *[near(o[0]) for o in (master, moment_one, moment_two)])
     others, weights = lax.optimization_barrier((others, weights))

time: 129 us -> 128 us (level)
  no operation moved by 1% of the time
where the time goes in v9:
time: 128 us
  blocking collectives  87.7 us (69%)
  waiting for transfers between devices  14.6 us (11%)
  starting transfers between devices  14.5 us (11%)
  Pallas kernels  7.55 us (6%)
  other arithmetic  2.1 us (2%)
    all_to_all x4, blocking collectives, exchange(): return lax.all_to_all(chunks, axis, 0, 0, tiled=True)  87.7 us
    all_to_all x1, waiting for transfers between devices, exchange(): return lax.all_to_all(chunks, axis, 0, 0, tiled=True)  14.6 us
    all_to_all x1, starting transfers between devices, exchange(): return lax.all_to_all(chunks, axis, 0, 0, tiled=True)  10.4 us
    ppermute x1, starting transfers between devices, shards(): others = lax.ppermute(halves, 'c', [(0, 1), (1, 0)])  4.16 us
    pallas_call x1, Pallas kernels, split(): pl.pallas_call(split_kernel, out_shape=jax.ShapeDtypeStruct(shape, grads....  2.96 us
  transfers between devices with their start and end apart: 2, of which 1 were waited for; matrix products, arithmetic and copies ran while one was open for 2% of the time, Pallas kernels for 2%

profile of v9, /device:TPU:1, one launch (start us, length us, event | category | flops | bytes accessed | tf_op | source)
XLA Modules:
  0.0 127.9 jit_solution(4109616939950085652)
XLA Ops:
  0.6 3.0 %split.1 = bf16[16,288,128]{2,1,0:T(8,128)(2,1)} custom-call(bf16[256,2048]{1,0:T(8,128)(2,1)} %bitcast.29, f32[3,2,2048]{2,1,0:T(2,128)} %bitcast.21, f32[3,2,2048]{2,1,0:T(2,128)} %bitcast.23, f32[3,2,2048]{2,1,0:T(2,128)} %bitcast.25), custom_call_target="tpu_custom_call" | custom-call | tf_op jit(solution)/shard_map/split/pallas_call | solution.py:109
  3.6 10.4 %all-to-all-start = ((bf16[16,288,128]{2,1,0:T(8,128)(2,1)}), bf16[16,288,128]{2,1,0:T(8,128)(2,1)S(1)}, u32[]{:S(2)}, u32[]{:S(2)}) async-start(bf16[16,288,128]{2,1,0:T(8,128)(2,1)} %split.1), calls=%async_computation | async-start | bytes 2359296 | tf_op jit(solution)/shard_map/all_to_all | solution.py:38
  14.0 0.2 compare_reduce_fusion
  14.2 0.2 convert_reduce_fusion
  14.5 0.1 iota_add_fusion.1
  14.5 0.1 add.287
  14.7 0.1 add_add_fusion
  14.8 0.1 add.301
  14.9 0.1 iota_add_fusion
  15.0 0.1 add.291
  15.1 0.1 select_reduce_fusion
  15.3 0.1 and_select_fusion
  15.4 0.1 add.315
  15.5 0.7 pad_add_fusion.at
  16.1 0.2 select_reduce_fusion.1
  16.3 0.1 compare_convert_fusion.pick
  16.4 0.1 fusion.3.take
  16.5 0.1 fusion.2
  16.6 0.1 fusion.route
  16.7 14.6 %all-to-all-done.raw = bf16[16,288,128]{2,1,0:T(8,128)(2,1)S(1)} async-done(((bf16[16,288,128]{2,1,0:T(8,128)(2,1)}), bf16[16,288,128]{2,1,0:T(8,128)(2,1)S(1)}, u32[]{:S(2)}, u32[]{:S(2)}) %all-to-all-start) | async-done | bytes 1179680 | tf_op jit(solution)/shard_map/all_to_all | solution.py:38
  31.4 0.5 pack.1
  31.8 25.8 %all_to_all.25.got = bf16[8,112,128]{2,1,0:T(8,128)(2,1)S(1)} all-to-all(bf16[8,112,128]{2,1,0:T(8,128)(2,1)S(1)} %pack.1), channel_id=1, replica_groups=mesh['z'=8,'pair'=2,'x'=4,'c'=2,'layer'=4] {'z'}, dimensions={0} | all-to-all | bytes 458752 | tf_op jit(solution)/shard_map/all_to_all | solution.py:38
  57.6 0.2 reduce.1
  57.8 31.3 %all_to_all.26.every.refs_0_ = bf16[8,192,128]{2,1,0:T(8,128)(2,1)S(1)} all-to-all(bf16[8,192,128]{2,1,0:T(8,128)(2,1)S(1)} %reduce.1), channel_id=1, replica_groups=mesh['z'=8,'pair'=2,'x'=4,'c'=2,'layer'=4] {'z'}, dimensions={0} | all-to-all | bytes 786432 | tf_op jit(solution)/shard_map/all_to_all | solution.py:38
  89.1 0.2 send.1
  89.3 19.3 %all_to_all.27.refs_1_.got = f32[64,8,128]{2,1,0:T(8,128)S(1)} all-to-all(f32[64,8,128]{2,1,0:T(8,128)S(1)} %bitcast.20), channel_id=1, replica_groups=mesh['z'=8,'pair'=2,'x'=4,'c'=2,'layer'=4] {'pair','x','c','layer'}, dimensions={0} | all-to-all | bytes 524288 | tf_op jit(solution)/shard_map/all_to_all | solution.py:38
  108.6 0.6 step.1
  109.2 11.3 %all_to_all.28.strips = bf16[8,256,128]{2,1,0:T(8,128)(2,1)S(1)} all-to-all(bf16[8,256,128]{2,1,0:T(8,128)(2,1)S(1)} %get-tuple-element.29), channel_id=1, replica_groups=mesh['z'=8,'pair'=2,'x'=4,'c'=2,'layer'=4] {'pair','x'}, dimensions={0} | all-to-all | bytes 1048576 | tf_op jit(solution)/shard_map/all_to_all | solution.py:38
  120.5 4.2 %collective-permute-start = (bf16[8,256,128]{2,1,0:T(8,128)(2,1)S(1)}, bf16[8,256,128]{2,1,0:T(8,128)(2,1)S(1)}, u32[]{:S(2)}, u32[]{:S(2)}) collective-permute-start(bf16[8,256,128]{2,1,0:T(8,128)(2,1)S(1)} %all_to_all.28.strips), channel_id=1, source_target_pairs={{0,4},{4,0},{1,5},{5,1},{2,6},{6,2},{3,7},{7,3},{8,12},{12,8},{9,1... | collective-permute-start | bytes 1572872 | tf_op jit(solution)/shard_map/ppermute | solution.py:332
  124.7 0.9 join.2.refs_0_
  125.6 1.5 %own.1 = (f32[3,2,2048]{2,1,0:T(2,128)}, f32[3,2,2048]{2,1,0:T(2,128)}, f32[3,2,2048]{2,1,0:T(2,128)}) custom-call(s32[4]{0:T(128)} %pad_add_fusion.at, f32[64,8,128]{2,1,0:T(8,128)S(1)} %all_to_all.27.refs_1_.got, f32[1,128]{1,0:T(1,128)S(1)} %copy-done.3, f32[3,2,2048]{2,1,0:T(2,128)S(1)} %bitcast.22, f32[3,2,2048]{2,1,0:T(2,128)S(1)} %bitcast.24, ...), custom_call_target="tpu_custom_call" | custom-call | tf_op jit(solution)/shard_map/own/pallas_call | solution.py:335
  127.1 0.8 join.3
  (23 shorter events, 0.1 us)
Async XLA Ops:
  3.6 10.4 %copy-start.4 = (s32[1,128]{1,0:T(1,128)S(1)}, s32[1,128]{1,0:T(1,128)}, u32[]{:S(2)}) copy-start(s32[1,128]{1,0:T(1,128)} %param.11) | copy-start | bytes 1540
  3.6 10.4 %copy-start.5 = (s32[1,128]{1,0:T(1,128)S(1)}, s32[1,128]{1,0:T(1,128)}, u32[]{:S(2)}) copy-start(s32[1,128]{1,0:T(1,128)} %param.10) | copy-start | bytes 1540
  3.6 27.7 %all-to-all-start = ((bf16[16,288,128]{2,1,0:T(8,128)(2,1)}), bf16[16,288,128]{2,1,0:T(8,128)(2,1)S(1)}, u32[]{:S(2)}, u32[]{:S(2)}) async-start(bf16[16,288,128]{2,1,0:T(8,128)(2,1)} %split.1), calls=%async_computation | async-start | bytes 2359296 | tf_op jit(solution)/shard_map/all_to_all | solution.py:38
  109.2 16.3 %copy-start = (f32[1,3,2,2048]{3,2,1,0:T(2,128)S(1)}, f32[1,3,2,2048]{3,2,1,0:T(2,128)}, u32[]{:S(2)}) copy-start(f32[1,3,2,2048]{3,2,1,0:T(2,128)} %param.7) | copy-start | bytes 147460
  109.2 16.3 %copy-start.1 = (f32[1,3,2,2048]{3,2,1,0:T(2,128)S(1)}, f32[1,3,2,2048]{3,2,1,0:T(2,128)}, u32[]{:S(2)}) copy-start(f32[1,3,2,2048]{3,2,1,0:T(2,128)} %param.8) | copy-start | bytes 147460
  109.2 16.3 %copy-start.2 = (f32[1,3,2,2048]{3,2,1,0:T(2,128)S(1)}, f32[1,3,2,2048]{3,2,1,0:T(2,128)}, u32[]{:S(2)}) copy-start(f32[1,3,2,2048]{3,2,1,0:T(2,128)} %param.9) | copy-start | bytes 147460
  109.2 16.3 %copy-start.3 = (f32[1,128]{1,0:T(1,128)S(1)}, f32[1,128]{1,0:T(1,128)}, u32[]{:S(2)}) copy-start(f32[1,128]{1,0:T(1,128)} %get-tuple-element.32.rms) | copy-start | bytes 1540
  120.5 6.6 %collective-permute-start = (bf16[8,256,128]{2,1,0:T(8,128)(2,1)S(1)}, bf16[8,256,128]{2,1,0:T(8,128)(2,1)S(1)}, u32[]{:S(2)}, u32[]{:S(2)}) collective-permute-start(bf16[8,256,128]{2,1,0:T(8,128)(2,1)S(1)} %all_to_all.28.strips), channel_id=1, source_target_pairs={{0,4},{4,0},{1,5},{5,1},{2,6},{6,2},{3,7},{7,3},{8,12},{12,8},{9,1... | collective-permute-start | bytes 1572872 | tf_op jit(solution)/shard_map/ppermute | solution.py:332

commit v10 on v9

--- a/solution.py
+++ b/solution.py
@@ -64,60 +64,29 @@
         rows[i, capacity * slab :, :] = jnp.ones_like(rows[i, capacity * slab :, :])
 
 
-def split_kernel(grads, master, first, second, out, held, rows, strips, in_sem, out_sem):
-    plane, total, wide = out.shape
+def split_kernel(grads, master, first, second, out, rows):
+    plane, _, wide = out.shape
     count = grads.shape[0]
-    pieces = in_sem.shape[0]
-    size = count // pieces
-    arrivals = [
-        pltpu.make_async_copy(
-            grads.at[pl.ds(i * size, size), :], held.at[pl.ds(i * size, size), :], in_sem.at[i]
-        )
-        for i in range(pieces)
-    ]
-    for arrival in arrivals:
-        arrival.start()
+    for k in range(plane):
+        out[k, :count, :] = grads[:, k * wide : (k + 1) * wide]
     fill_rows(rows, (master, first, second))
     high, low = two_terms(rows[0])
     values = (high, low, rows[1].astype(jnp.bfloat16), rows[2].astype(jnp.bfloat16))
     for t, value in enumerate(values):
         at = count + t * SLOT_ROWS
         for k in range(plane):
-            strips[k, at : at + SLOT_ROWS, :] = value[:, k * wide : (k + 1) * wide]
-    moves = []
-    for i in range(pieces + 1):
-        at, length = i * size, size
-        if i < pieces:
-            arrivals[i].wait()
-            for k in range(plane):
-                strips[k, at : at + size, :] = held[at : at + size, k * wide : (k + 1) * wide]
-        else:
-            length = total - count
-        here = pl.ds(at, length)
-        moves.append(
-            pltpu.make_async_copy(strips.at[:, here, :], out.at[:, here, :], out_sem.at[i])
-        )
-        moves[-1].start()
-    for move in moves:
-        move.wait()
+            out[k, at : at + SLOT_ROWS, :] = value[:, k * wide : (k + 1) * wide]
 
 
 def split(grads, master, first, second, plane):
     count, width = grads.shape
     shape = (plane, count + KINDS * SLOT_ROWS, width // plane)
-    pieces = 4
     return pl.pallas_call(
         split_kernel,
         out_shape=jax.ShapeDtypeStruct(shape, grads.dtype),
-        in_specs=[ANY, VMEM, VMEM, VMEM],
-        out_specs=ANY,
-        scratch_shapes=[
-            pltpu.VMEM((count, width), grads.dtype),
-            pltpu.VMEM((3, SLOT_ROWS, width), jnp.float32),
-            pltpu.VMEM(shape, grads.dtype),
-            pltpu.SemaphoreType.DMA((pieces,)),
-            pltpu.SemaphoreType.DMA((pieces + 1,)),
-        ],
+        in_specs=[VMEM] * 4,
+        out_specs=VMEM,
+        scratch_shapes=[pltpu.VMEM((3, SLOT_ROWS, width), jnp.float32)],
         name="split",
     )(grads, master, first, second)
 
@@ -169,41 +138,35 @@
             out[s] = jnp.where(at[1 + s] > 0, rows[i, s * slab : (s + 1) * slab, :], old[s])
 
 
-def pack_kernel(raw, order, route, out):
+def pack_kernel(raw, out, strips):
     plane, count, _ = raw.shape
-    ring = out.shape[0]
-    rows = order.shape[0]
-    part = rows // ring
+    ring, part = out.shape[0], out.shape[1] // 2
+    rows = ring * part
     total = raw[0, :rows, :].astype(jnp.float32)
     for j in range(1, plane):
         total = total + raw[j, :rows, :].astype(jnp.float32)
-    lines = [
-        raw[j, at : at + SLOT_ROWS, :] for at in range(rows, count, SLOT_ROWS) for j in range(plane)
-    ]
-    high, low = two_terms(total)
-    sources = ((order, high), (order, low), (route, jnp.concatenate(lines, axis=0)))
-    for i, (matrix, source) in enumerate(sources):
-        chosen = choose(matrix[...], source).astype(out.dtype)
-        size = chosen.shape[0] // ring
+    for i, term in enumerate(two_terms(total)):
         for z in range(ring):
-            out[z, i * part : i * part + size, :] = chosen[z * size : (z + 1) * size, :]
-
-
-def reduce_kernel(got, take, out):
+            out[z, i * part : (i + 1) * part, :] = term[z * part : (z + 1) * part, :]
+    for t in range(KINDS):
+        at = rows + t * SLOT_ROWS
+        for j in range(plane):
+            to = (t * plane + j) * SLOT_ROWS
+            strips[to : to + SLOT_ROWS, :] = raw[j, at : at + SLOT_ROWS, :]
+
+
+def reduce_kernel(got, out):
     ring = got.shape[0]
-    part = out.shape[1] // (2 + KINDS)
-    total = got[0, :part, :].astype(jnp.float32) + got[0, part : 2 * part, :].astype(jnp.float32)
-    for z in range(1, ring):
+    part = out.shape[1] // 2
+    total = jnp.zeros(out.shape[1:], jnp.float32)[:part]
+    for z in range(ring):
         total = total + (
-            got[z, :part, :].astype(jnp.float32) + got[z, part : 2 * part, :].astype(jnp.float32)
+            got[z, :part, :].astype(jnp.float32) + got[z, part:, :].astype(jnp.float32)
         )
     high, low = two_terms(total)
-    lines = jnp.concatenate([got[z, 2 * part :, :] for z in range(ring)], axis=0)
-    lines = choose(take[...], lines).astype(out.dtype)
     for z in range(ring):
         out[z, :part, :] = high
-        out[z, part : 2 * part, :] = low
-        out[z, 2 * part :, :] = lines
+        out[z, part:, :] = low
 
 
 def ordered(every, term, part):
@@ -226,18 +189,22 @@
             out[j, layer] = sent[j * SLOT_ROWS : (j + 1) * SLOT_ROWS, :]
 
 
-def step_kernel(element_total, every, got, place, copies, rms):
-    part = place.shape[1] // every.shape[0]
+def step_kernel(element_total, every, got, place, *refs):
+    states, (copies, rms) = refs[:-2], refs[-2:]
+    part = every.shape[1] // 2
     squares = jnp.sum(got[...], axis=0)[SLOT_ROWS - 1 :, :]
     grad_rms = jnp.sqrt(squares / element_total + 1e-06)
     rms[...] = grad_rms
     clip_factor = jnp.minimum(1.0, 1.0 / grad_rms)
-    terms = [ordered(every, t, part).astype(jnp.float32) for t in range(2 + KINDS)]
-    grad = (terms[0] + terms[1]) * clip_factor
-    param = adamw(terms[2] + terms[3], terms[4], terms[5], grad)[0]
-    weights = choose(place[...], param.astype(copies.dtype)).astype(copies.dtype)
+    grad = sum(ordered(every, t, part).astype(jnp.float32) for t in range(2)) * clip_factor
+    size = states[0].shape[0] // KINDS
+    terms = []
+    for t in range(KINDS):
+        lines = jnp.concatenate([s[t * size : (t + 1) * size, :] for s in states], axis=0)
+        terms.append(choose(place[...], lines))
+    param = adamw(terms[0] + terms[1], terms[2], terms[3], grad)[0]
     for x in range(copies.shape[0]):
-        copies[x] = weights
+        copies[x] = param.astype(copies.dtype)
 
 
 def shards(micro_grads, master, moment_one, moment_two, owner, slot):
@@ -252,61 +219,54 @@
     part = rows // ring
     plane_lines = plane * SLOT_ROWS
     bf16, f32, i32 = jnp.bfloat16, jnp.float32, jnp.int32
-    count = jnp.arange(rows, dtype=i32)
     few = jnp.arange(plane_lines, dtype=i32)
 
-    deal = -(-plane * capacity // ring)
-    pair = deal * slab
-    home = owner[0] * capacity + slot[0]
-    rank = jnp.sum((home[None, :] < home[:, None]).astype(i32), axis=1)
     line = owner[0] * SLOT_ROWS + slot[0] * slab
-    member, turn = rank % ring, rank // ring
-
-    def per_row(value):
-        return (value[:, None] + jnp.arange(slab, dtype=i32)[None, :]).reshape(rows)
-
-    line_of = per_row(line)
-    dealt = per_row(member * part + turn * slab)
-    pair_of = per_row(member * pair + turn % deal * slab)
-    order = dealt[None, :] == count[:, None]
-    place = dealt[:, None] == count[None, :]
-    line_at = jnp.sum(jnp.where(order, line_of[None, :], 0), axis=1)
-    pick = (my_z * plane_lines + few)[:, None] == line_at[None, :]
-    mine = line_of[None, :] == (my_z * plane_lines + few)[:, None]
-    pair_at = jnp.sum(jnp.where(mine, pair_of[None, :] + 1, 0), axis=1) - 1
-    kind = jnp.arange(KINDS, dtype=i32)[:, None]
-    goes = jnp.where(pair_at < 0, -1, pair_at)[None, :]
-    goes = jnp.where(goes < 0, -1, (goes // pair * KINDS + kind) * pair + goes % pair)
-    chunks = jnp.arange(ring * KINDS * pair, dtype=i32)
-    route = goes.reshape(1, KINDS * plane_lines) == chunks[:, None]
-    own_line = lax.dynamic_slice_in_dim(line_at, my_z * part, part)
-    within = jnp.arange(part, dtype=i32) % pair
-    comes = (own_line // plane_lines * KINDS + kind) * pair + within[None, :]
-    take = comes.reshape(KINDS * part, 1) == chunks[None, :]
+    line_of = (line[:, None] + jnp.arange(slab, dtype=i32)[None, :]).reshape(rows)
+    pick = (my_z * plane_lines + few)[:, None] == line_of[None, :]
+    steps = [0] + list(range(-1, -ring // 2 - 1, -1)) + list(range(1, (ring + 1) // 2))
+    sources = lax.rem(my_z + ring + jnp.array(steps, dtype=i32), ring)
+    from_line = (sources[:, None] * plane_lines + few[None, :]).reshape(1, ring * plane_lines)
+    place = line_of[:, None] == from_line
 
     raw = exchange(split(micro_grads[0, 0], master[0], moment_one[0], moment_two[0], plane), PLANE)
     my_slots = lax.axis_index((RING, *PLANE)) * SLOT_ROWS
     my_slots = my_slots + slab * jnp.arange(capacity, dtype=i32)
     keep = jnp.any(line[None, :] == my_slots[:, None], axis=1).astype(i32)
     at = jnp.concatenate([lax.axis_index("layer").astype(i32).reshape(1), keep])
-    tables = [t.astype(bf16) for t in (order, route, take, pick, place)]
+    tables = [t.astype(bf16) for t in (pick, place)]
     raw, at, *tables = lax.optimization_barrier((raw, at, *tables))
-    order, route, take, pick, place = [near(t) for t in tables]
-    packed = pl.pallas_call(
+    pick, place = [near(t) for t in tables]
+    packed, strips = pl.pallas_call(
         pack_kernel,
-        out_shape=pltpu.VMEM((ring, 2 * part + KINDS * pair, wide), bf16),
-        in_specs=[VMEM] * 3,
-        out_specs=VMEM,
+        out_shape=(
+            pltpu.VMEM((ring, 2 * part, wide), bf16),
+            pltpu.VMEM((KINDS * plane_lines, wide), bf16),
+        ),
+        in_specs=[VMEM],
+        out_specs=(VMEM, VMEM),
         name="pack",
-    )(near(raw), order, route)
+    )(near(raw))
+    def shift(value, by):
+        return lax.ppermute(value, RING, [(i, (i + by) % ring) for i in range(ring)])
+
+    def two_steps(value, here):
+        (right, left), steps = here, []
+        for _ in range(2):
+            right, left = shift(right, 1), shift(left, -1)
+            steps.append((right, left))
+        return lax.optimization_barrier((exchange(value, RING), steps))
+
+    summed, near_by = two_steps(packed, (strips, strips))
     reduced = pl.pallas_call(
         reduce_kernel,
-        out_shape=pltpu.VMEM((ring, (2 + KINDS) * part, wide), bf16),
-        in_specs=[VMEM] * 2,
+        out_shape=pltpu.VMEM((ring, 2 * part, wide), bf16),
+        in_specs=[VMEM],
         out_specs=VMEM,
         name="reduce",
-    )(near(exchange(packed, RING)), take)
-    every = exchange(reduced, RING)
+    )(near(summed))
+    every, far = two_steps(reduced, near_by[-1])
+    states = [strips, *[p[0] for p in near_by + far], *[p[1] for p in (near_by + far)[: ring // 2 - 1]]]
 
     sent = pl.pallas_call(
         send_kernel,
@@ -323,10 +283,10 @@
             pltpu.VMEM((lax.axis_size(HALF), rows, wide), bf16),
             jax.ShapeDtypeStruct((1, wide), f32),
         ),
-        in_specs=[VMEM] * 3,
+        in_specs=[VMEM] * (3 + ring),
         out_specs=(VMEM, VMEM),
         name="step",
-    )(near(every), near(got), place)
+    )(near(every), near(got), place, *[near(s) for s in states])
     core = lax.axis_index("c")
     halves, got, rms = lax.optimization_barrier((exchange(copies, HALF), got, rms))
     others = lax.ppermute(halves, "c", [(0, 1), (1, 0)])

time: 128 us -> 145 us (1.13)
  blocking collectives: 87.7 us -> 32.4 us
  starting transfers between devices: 14.5 us -> 59.6 us
  waiting for transfers between devices: 14.6 us -> 41.2 us
    all_to_all x4 -> x2, blocking collectives: 87.7 us -> 32.4 us  [exchange(): return lax.all_to_all(chunks, axis, 0, 0, tiled=True)]
    ppermute x0 -> x7, waiting for transfers between devices: none -> 25.3 us  [shift(): lax.ppermute(value, RING, [(i, (i + by) % ring) for i in range(ring)])]
    ppermute x0 -> x7, starting transfers between devices: none -> 24.1 us  [shift(): lax.ppermute(value, RING, [(i, (i + by) % ring) for i in range(ring)])]
    all_to_all x1 -> x3, starting transfers between devices: 10.4 us -> 31.3 us  [exchange(): return lax.all_to_all(chunks, axis, 0, 0, tiled=True)]
    all_to_all x1 -> x3, waiting for transfers between devices: 14.6 us -> 16 us  [exchange(): return lax.all_to_all(chunks, axis, 0, 0, tiled=True)]
  transfers between devices with their start and end apart: 2 -> 11, of which waited for: 1 -> 7; matrix products, arithmetic and copies ran while one was open for 2% -> 1% of each run, Pallas kernels for 2% -> 2%
where the time goes in v10:
time: 145 us; the launch traced here: 144 us
  starting transfers between devices  59.6 us (41%)
  waiting for transfers between devices  41.2 us (28%)
  blocking collectives  32.4 us (22%)
  Pallas kernels  8.4 us (6%)
    all_to_all x2, blocking collectives, exchange(): return lax.all_to_all(chunks, axis, 0, 0, tiled=True)  32.4 us
    all_to_all x3, starting transfers between devices, exchange(): return lax.all_to_all(chunks, axis, 0, 0, tiled=True)  31.3 us
    ppermute x7, waiting for transfers between devices, shift(): lax.ppermute(value, RING, [(i, (i + by) % ring) for i in range(ring)])  25.3 us
    ppermute x7, starting transfers between devices, shift(): lax.ppermute(value, RING, [(i, (i + by) % ring) for i in range(ring)])  24.1 us
    all_to_all x3, waiting for transfers between devices, exchange(): return lax.all_to_all(chunks, axis, 0, 0, tiled=True)  16 us
    ppermute x1, starting transfers between devices, shards(): others = lax.ppermute(halves, 'c', [(0, 1), (1, 0)])  4.16 us
  transfers between devices with their start and end apart: 11, of which 7 were waited for; matrix products, arithmetic and copies ran while one was open for 1% of the time, Pallas kernels for 2%

profile of v10, /device:TPU:1, one launch (start us, length us, event | category | flops | bytes accessed | tf_op | source)
XLA Modules:
  0.0 143.8 jit_solution(4227982536012661098)
XLA Ops:
  0.6 2.6 %split.1 = bf16[16,288,128]{2,1,0:T(8,128)(2,1)} custom-call(bf16[256,2048]{1,0:T(8,128)(2,1)} %bitcast.27, f32[3,2,2048]{2,1,0:T(2,128)} %bitcast.19, f32[3,2,2048]{2,1,0:T(2,128)} %bitcast.21, f32[3,2,2048]{2,1,0:T(2,128)} %bitcast.23), custom_call_target="tpu_custom_call" | custom-call | tf_op jit(solution)/shard_map/split/pallas_call | solution.py:84
  3.2 10.5 %all-to-all-start = ((bf16[16,288,128]{2,1,0:T(8,128)(2,1)}), bf16[16,288,128]{2,1,0:T(8,128)(2,1)S(1)}, u32[]{:S(2)}, u32[]{:S(2)}) async-start(bf16[16,288,128]{2,1,0:T(8,128)(2,1)} %split.1), calls=%async_computation | async-start | bytes 2359296 | tf_op jit(solution)/shard_map/all_to_all | solution.py:38
  13.7 0.2 compare_reduce_fusion
  14.0 0.1 add.102
  14.2 0.6 pad_add_fusion.at
  14.9 0.2 compare_convert_fusion.refs_2_
  15.1 16.0 %all-to-all-done.raw = bf16[16,288,128]{2,1,0:T(8,128)(2,1)S(1)} async-done(((bf16[16,288,128]{2,1,0:T(8,128)(2,1)}), bf16[16,288,128]{2,1,0:T(8,128)(2,1)S(1)}, u32[]{:S(2)}, u32[]{:S(2)}) %all-to-all-start) | async-done | bytes 1179680 | tf_op jit(solution)/shard_map/all_to_all | solution.py:38
  31.0 0.8 pack.1
  31.9 10.7 %all-to-all-start.1 = ((bf16[8,64,128]{2,1,0:T(8,128)(2,1)}), bf16[8,64,128]{2,1,0:T(8,128)(2,1)S(1)}, u32[]{:S(2)}, u32[]{:S(2)}) async-start(bf16[8,64,128]{2,1,0:T(8,128)(2,1)} %get-tuple-element.32), calls=%async_computation.1 | async-start | bytes 262144 | tf_op jit(solution)/shard_map/all_to_all | solution.py:38
  42.5 4.3 %collective-permute-start = (bf16[512,128]{1,0:T(8,128)(2,1)S(1)}, bf16[512,128]{1,0:T(8,128)(2,1)S(1)}, u32[]{:S(2)}, u32[]{:S(2)}) collective-permute-start(bf16[512,128]{1,0:T(8,128)(2,1)S(1)} %get-tuple-element.33.refs_3_), channel_id=1, source_target_pairs={{0,64},{64,128},{128,192},{192,256},{256,320},{320,384},{384,448},... | collective-permute-start | bytes 393224 | tf_op jit(solution)/shard_map/ppermute | solution.py:251
  46.8 3.1 %collective-permute-start.1 = (bf16[512,128]{1,0:T(8,128)(2,1)S(1)}, bf16[512,128]{1,0:T(8,128)(2,1)S(1)}, u32[]{:S(2)}, u32[]{:S(2)}) collective-permute-start(bf16[512,128]{1,0:T(8,128)(2,1)S(1)} %get-tuple-element.33.refs_3_), channel_id=1, source_target_pairs={{0,448},{64,0},{128,64},{192,128},{256,192},{320,256},{384,320},{4... | collective-permute-start | bytes 393224 | tf_op jit(solution)/shard_map/ppermute | solution.py:251
  49.9 7.5 %collective-permute-done.refs_4_ = bf16[512,128]{1,0:T(8,128)(2,1)S(1)} collective-permute-done((bf16[512,128]{1,0:T(8,128)(2,1)S(1)}, bf16[512,128]{1,0:T(8,128)(2,1)S(1)}, u32[]{:S(2)}, u32[]{:S(2)}) %collective-permute-start) | collective-permute-done | bytes 131104 | tf_op jit(solution)/shard_map/ppermute | solution.py:251
  57.4 2.7 %collective-permute-start.2 = (bf16[512,128]{1,0:T(8,128)(2,1)S(1)}, bf16[512,128]{1,0:T(8,128)(2,1)S(1)}, u32[]{:S(2)}, u32[]{:S(2)}) collective-permute-start(bf16[512,128]{1,0:T(8,128)(2,1)S(1)} %collective-permute-done.refs_4_), channel_id=1, source_target_pairs={{0,64},{64,128},{128,192},{192,256},{256,320},{320,384},{384,448},... | collective-permute-start | bytes 393224 | tf_op jit(solution)/shard_map/ppermute | solution.py:251
  60.1 4.7 %collective-permute-start.3 = (bf16[512,128]{1,0:T(8,128)(2,1)S(1)}, bf16[512,128]{1,0:T(8,128)(2,1)S(1)}, u32[]{:S(2)}, u32[]{:S(2)}) collective-permute-start(bf16[512,128]{1,0:T(8,128)(2,1)S(1)} %collective-permute-done.1.refs_8_), channel_id=1, source_target_pairs={{0,448},{64,0},{128,64},{192,128},{256,192},{320,256},{384,320},{4... | collective-permute-start | bytes 393224 | tf_op jit(solution)/shard_map/ppermute | solution.py:251
  64.8 2.0 %collective-permute-done.2.refs_5_ = bf16[512,128]{1,0:T(8,128)(2,1)S(1)} collective-permute-done((bf16[512,128]{1,0:T(8,128)(2,1)S(1)}, bf16[512,128]{1,0:T(8,128)(2,1)S(1)}, u32[]{:S(2)}, u32[]{:S(2)}) %collective-permute-start.2) | collective-permute-done | bytes 131104 | tf_op jit(solution)/shard_map/ppermute | solution.py:251
  66.8 3.2 %collective-permute-done.3.refs_9_ = bf16[512,128]{1,0:T(8,128)(2,1)S(1)} collective-permute-done((bf16[512,128]{1,0:T(8,128)(2,1)S(1)}, bf16[512,128]{1,0:T(8,128)(2,1)S(1)}, u32[]{:S(2)}, u32[]{:S(2)}) %collective-permute-start.3) | collective-permute-done | bytes 131104 | tf_op jit(solution)/shard_map/ppermute | solution.py:251
  70.1 0.7 reduce.1
  70.8 10.2 %all-to-all-start.2 = ((bf16[8,64,128]{2,1,0:T(8,128)(2,1)}), bf16[8,64,128]{2,1,0:T(8,128)(2,1)S(1)}, u32[]{:S(2)}, u32[]{:S(2)}) async-start(bf16[8,64,128]{2,1,0:T(8,128)(2,1)} %reduce.1), calls=%async_computation.2 | async-start | bytes 262144 | tf_op jit(solution)/shard_map/all_to_all | solution.py:38
  80.9 4.3 %collective-permute-start.4 = (bf16[512,128]{1,0:T(8,128)(2,1)S(1)}, bf16[512,128]{1,0:T(8,128)(2,1)S(1)}, u32[]{:S(2)}, u32[]{:S(2)}) collective-permute-start(bf16[512,128]{1,0:T(8,128)(2,1)S(1)} %collective-permute-done.2.refs_5_), channel_id=1, source_target_pairs={{0,64},{64,128},{128,192},{192,256},{256,320},{320,384},{384,448},... | collective-permute-start | bytes 393224 | tf_op jit(solution)/shard_map/ppermute | solution.py:251
  85.2 3.1 %collective-permute-start.5 = (bf16[512,128]{1,0:T(8,128)(2,1)S(1)}, bf16[512,128]{1,0:T(8,128)(2,1)S(1)}, u32[]{:S(2)}, u32[]{:S(2)}) collective-permute-start(bf16[512,128]{1,0:T(8,128)(2,1)S(1)} %collective-permute-done.3.refs_9_), channel_id=1, source_target_pairs={{0,448},{64,0},{128,64},{192,128},{256,192},{320,256},{384,320},{4... | collective-permute-start | bytes 393224 | tf_op jit(solution)/shard_map/ppermute | solution.py:251
  88.4 6.6 %collective-permute-done.4.refs_6_ = bf16[512,128]{1,0:T(8,128)(2,1)S(1)} collective-permute-done((bf16[512,128]{1,0:T(8,128)(2,1)S(1)}, bf16[512,128]{1,0:T(8,128)(2,1)S(1)}, u32[]{:S(2)}, u32[]{:S(2)}) %collective-permute-start.4) | collective-permute-done | bytes 131104 | tf_op jit(solution)/shard_map/ppermute | solution.py:251
  95.0 1.9 %collective-permute-start.6 = (bf16[512,128]{1,0:T(8,128)(2,1)S(1)}, bf16[512,128]{1,0:T(8,128)(2,1)S(1)}, u32[]{:S(2)}, u32[]{:S(2)}) collective-permute-start(bf16[512,128]{1,0:T(8,128)(2,1)S(1)} %collective-permute-done.4.refs_6_), channel_id=1, source_target_pairs={{0,64},{64,128},{128,192},{192,256},{256,320},{320,384},{384,448},... | collective-permute-start | bytes 393224 | tf_op jit(solution)/shard_map/ppermute | solution.py:251
  96.9 0.9 collective-permute-done.5.refs_10_
  97.7 5.0 %collective-permute-done.6.refs_7_ = bf16[512,128]{1,0:T(8,128)(2,1)S(1)} collective-permute-done((bf16[512,128]{1,0:T(8,128)(2,1)S(1)}, bf16[512,128]{1,0:T(8,128)(2,1)S(1)}, u32[]{:S(2)}, u32[]{:S(2)}) %collective-permute-start.6) | collective-permute-done | bytes 131104 | tf_op jit(solution)/shard_map/ppermute | solution.py:251
  102.8 0.2 send.1
  103.0 21.2 %all_to_all.25.refs_1_.got = f32[64,8,128]{2,1,0:T(8,128)S(1)} all-to-all(f32[64,8,128]{2,1,0:T(8,128)S(1)} %bitcast.18), channel_id=1, replica_groups=mesh['z'=8,'pair'=2,'x'=4,'c'=2,'layer'=4] {'pair','x','c','layer'}, dimensions={0} | all-to-all | bytes 524288 | tf_op jit(solution)/shard_map/all_to_all | solution.py:38
  124.1 1.0 step.1
  125.1 11.3 %all_to_all.26.strips = bf16[8,256,128]{2,1,0:T(8,128)(2,1)S(1)} all-to-all(bf16[8,256,128]{2,1,0:T(8,128)(2,1)S(1)} %get-tuple-element.45), channel_id=1, replica_groups=mesh['z'=8,'pair'=2,'x'=4,'c'=2,'layer'=4] {'pair','x'}, dimensions={0} | all-to-all | bytes 1048576 | tf_op jit(solution)/shard_map/all_to_all | solution.py:38
  136.4 4.2 %collective-permute-start.7 = (bf16[8,256,128]{2,1,0:T(8,128)(2,1)S(1)}, bf16[8,256,128]{2,1,0:T(8,128)(2,1)S(1)}, u32[]{:S(2)}, u32[]{:S(2)}) collective-permute-start(bf16[8,256,128]{2,1,0:T(8,128)(2,1)S(1)} %all_to_all.26.strips), channel_id=1, source_target_pairs={{0,4},{4,0},{1,5},{5,1},{2,6},{6,2},{3,7},{7,3},{8,12},{12,8},{9,1... | collective-permute-start | bytes 1572872 | tf_op jit(solution)/shard_map/ppermute | solution.py:292
  140.6 0.9 join.2.refs_0_
  141.5 1.5 %own.1 = (f32[3,2,2048]{2,1,0:T(2,128)}, f32[3,2,2048]{2,1,0:T(2,128)}, f32[3,2,2048]{2,1,0:T(2,128)}) custom-call(s32[4]{0:T(128)} %pad_add_fusion.at, f32[64,8,128]{2,1,0:T(8,128)S(1)} %all_to_all.25.refs_1_.got, f32[1,128]{1,0:T(1,128)S(1)} %copy-done.3, f32[3,2,2048]{2,1,0:T(2,128)S(1)} %bitcast.20, f32[3,2,2048]{2,1,0:T(2,128)S(1)} %bitcast.22, ...), custom_call_target="tpu_custom_call" | custom-call | tf_op jit(solution)/shard_map/own/pallas_call | solution.py:295
  143.0 0.8 join.3
  (26 shorter events, 0.3 us)
Async XLA Ops:
  3.2 10.5 %copy-start.4 = (s32[1,128]{1,0:T(1,128)S(1)}, s32[1,128]{1,0:T(1,128)}, u32[]{:S(2)}) copy-start(s32[1,128]{1,0:T(1,128)} %param.12) | copy-start | bytes 1540
  3.2 10.5 %copy-start.5 = (s32[1,128]{1,0:T(1,128)S(1)}, s32[1,128]{1,0:T(1,128)}, u32[]{:S(2)}) copy-start(s32[1,128]{1,0:T(1,128)} %param.11) | copy-start | bytes 1540
  3.2 11.6 %copy-start.6 = (s32[8]{0:T(128)S(1)}, s32[8]{0:T(128)}, u32[]{:S(2)}) copy-start(s32[8]{0:T(128)} %constant.44.clone) | copy-start | bytes 100
  3.2 27.9 %all-to-all-start = ((bf16[16,288,128]{2,1,0:T(8,128)(2,1)}), bf16[16,288,128]{2,1,0:T(8,128)(2,1)S(1)}, u32[]{:S(2)}, u32[]{:S(2)}) async-start(bf16[16,288,128]{2,1,0:T(8,128)(2,1)} %split.1), calls=%async_computation | async-start | bytes 2359296 | tf_op jit(solution)/shard_map/all_to_all | solution.py:38
  31.9 38.2 %all-to-all-start.1 = ((bf16[8,64,128]{2,1,0:T(8,128)(2,1)}), bf16[8,64,128]{2,1,0:T(8,128)(2,1)S(1)}, u32[]{:S(2)}, u32[]{:S(2)}) async-start(bf16[8,64,128]{2,1,0:T(8,128)(2,1)} %get-tuple-element.32), calls=%async_computation.1 | async-start | bytes 262144 | tf_op jit(solution)/shard_map/all_to_all | solution.py:38
  42.5 14.9 %collective-permute-start = (bf16[512,128]{1,0:T(8,128)(2,1)S(1)}, bf16[512,128]{1,0:T(8,128)(2,1)S(1)}, u32[]{:S(2)}, u32[]{:S(2)}) collective-permute-start(bf16[512,128]{1,0:T(8,128)(2,1)S(1)} %get-tuple-element.33.refs_3_), channel_id=1, source_target_pairs={{0,64},{64,128},{128,192},{192,256},{256,320},{320,384},{384,448},... | collective-permute-start | bytes 393224 | tf_op jit(solution)/shard_map/ppermute | solution.py:251
  46.8 13.3 %collective-permute-start.1 = (bf16[512,128]{1,0:T(8,128)(2,1)S(1)}, bf16[512,128]{1,0:T(8,128)(2,1)S(1)}, u32[]{:S(2)}, u32[]{:S(2)}) collective-permute-start(bf16[512,128]{1,0:T(8,128)(2,1)S(1)} %get-tuple-element.33.refs_3_), channel_id=1, source_target_pairs={{0,448},{64,0},{128,64},{192,128},{256,192},{320,256},{384,320},{4... | collective-permute-start | bytes 393224 | tf_op jit(solution)/shard_map/ppermute | solution.py:251
  57.4 9.4 %collective-permute-start.2 = (bf16[512,128]{1,0:T(8,128)(2,1)S(1)}, bf16[512,128]{1,0:T(8,128)(2,1)S(1)}, u32[]{:S(2)}, u32[]{:S(2)}) collective-permute-start(bf16[512,128]{1,0:T(8,128)(2,1)S(1)} %collective-permute-done.refs_4_), channel_id=1, source_target_pairs={{0,64},{64,128},{128,192},{192,256},{256,320},{320,384},{384,448},... | collective-permute-start | bytes 393224 | tf_op jit(solution)/shard_map/ppermute | solution.py:251
  60.1 10.0 %collective-permute-start.3 = (bf16[512,128]{1,0:T(8,128)(2,1)S(1)}, bf16[512,128]{1,0:T(8,128)(2,1)S(1)}, u32[]{:S(2)}, u32[]{:S(2)}) collective-permute-start(bf16[512,128]{1,0:T(8,128)(2,1)S(1)} %collective-permute-done.1.refs_8_), channel_id=1, source_target_pairs={{0,448},{64,0},{128,64},{192,128},{256,192},{320,256},{384,320},{4... | collective-permute-start | bytes 393224 | tf_op jit(solution)/shard_map/ppermute | solution.py:251
  70.8 32.0 %all-to-all-start.2 = ((bf16[8,64,128]{2,1,0:T(8,128)(2,1)}), bf16[8,64,128]{2,1,0:T(8,128)(2,1)S(1)}, u32[]{:S(2)}, u32[]{:S(2)}) async-start(bf16[8,64,128]{2,1,0:T(8,128)(2,1)} %reduce.1), calls=%async_computation.2 | async-start | bytes 262144 | tf_op jit(solution)/shard_map/all_to_all | solution.py:38
  80.9 14.0 %collective-permute-start.4 = (bf16[512,128]{1,0:T(8,128)(2,1)S(1)}, bf16[512,128]{1,0:T(8,128)(2,1)S(1)}, u32[]{:S(2)}, u32[]{:S(2)}) collective-permute-start(bf16[512,128]{1,0:T(8,128)(2,1)S(1)} %collective-permute-done.2.refs_5_), channel_id=1, source_target_pairs={{0,64},{64,128},{128,192},{192,256},{256,320},{320,384},{384,448},... | collective-permute-start | bytes 393224 | tf_op jit(solution)/shard_map/ppermute | solution.py:251
  85.2 12.5 %collective-permute-start.5 = (bf16[512,128]{1,0:T(8,128)(2,1)S(1)}, bf16[512,128]{1,0:T(8,128)(2,1)S(1)}, u32[]{:S(2)}, u32[]{:S(2)}) collective-permute-start(bf16[512,128]{1,0:T(8,128)(2,1)S(1)} %collective-permute-done.3.refs_9_), channel_id=1, source_target_pairs={{0,448},{64,0},{128,64},{192,128},{256,192},{320,256},{384,320},{4... | collective-permute-start | bytes 393224 | tf_op jit(solution)/shard_map/ppermute | solution.py:251
  95.0 7.8 %collective-permute-start.6 = (bf16[512,128]{1,0:T(8,128)(2,1)S(1)}, bf16[512,128]{1,0:T(8,128)(2,1)S(1)}, u32[]{:S(2)}, u32[]{:S(2)}) collective-permute-start(bf16[512,128]{1,0:T(8,128)(2,1)S(1)} %collective-permute-done.4.refs_6_), channel_id=1, source_target_pairs={{0,64},{64,128},{128,192},{192,256},{256,320},{320,384},{384,448},... | collective-permute-start | bytes 393224 | tf_op jit(solution)/shard_map/ppermute | solution.py:251
  125.1 16.3 %copy-start = (f32[1,3,2,2048]{3,2,1,0:T(2,128)S(1)}, f32[1,3,2,2048]{3,2,1,0:T(2,128)}, u32[]{:S(2)}) copy-start(f32[1,3,2,2048]{3,2,1,0:T(2,128)} %param.8) | copy-start | bytes 147460
  125.1 16.3 %copy-start.1 = (f32[1,3,2,2048]{3,2,1,0:T(2,128)S(1)}, f32[1,3,2,2048]{3,2,1,0:T(2,128)}, u32[]{:S(2)}) copy-start(f32[1,3,2,2048]{3,2,1,0:T(2,128)} %param.9) | copy-start | bytes 147460
  125.1 16.3 %copy-start.2 = (f32[1,3,2,2048]{3,2,1,0:T(2,128)S(1)}, f32[1,3,2,2048]{3,2,1,0:T(2,128)}, u32[]{:S(2)}) copy-start(f32[1,3,2,2048]{3,2,1,0:T(2,128)} %param.10) | copy-start | bytes 147460
  125.1 16.3 %copy-start.3 = (f32[1,128]{1,0:T(1,128)S(1)}, f32[1,128]{1,0:T(1,128)}, u32[]{:S(2)}) copy-start(f32[1,128]{1,0:T(1,128)} %get-tuple-element.48.rms) | copy-start | bytes 1540
  136.4 6.6 %collective-permute-start.7 = (bf16[8,256,128]{2,1,0:T(8,128)(2,1)S(1)}, bf16[8,256,128]{2,1,0:T(8,128)(2,1)S(1)}, u32[]{:S(2)}, u32[]{:S(2)}) collective-permute-start(bf16[8,256,128]{2,1,0:T(8,128)(2,1)S(1)} %all_to_all.26.strips), channel_id=1, source_target_pairs={{0,4},{4,0},{1,5},{5,1},{2,6},{6,2},{3,7},{7,3},{8,12},{12,8},{9,1... | collective-permute-start | bytes 1572872 | tf_op jit(solution)/shard_map/ppermute | solution.py:292

commit v11 on v9

--- a/solution.py
+++ b/solution.py
@@ -15,10 +15,11 @@
 adam_eps = 1e-08
 step_number = 100.0
 
-RING = "z"
+RING = ("z", "side")
+SIDES = 2
 PLANE = ("pair", "x", "c")
 PLANE_SHAPE = (2, 4, 2)
-HALF = ("pair", "x")
+FORM = ("side", "pair", "x")
 SLOT_ROWS = 8
 KINDS = 4
 
@@ -64,92 +65,62 @@
         rows[i, capacity * slab :, :] = jnp.ones_like(rows[i, capacity * slab :, :])
 
 
-def split_kernel(grads, master, first, second, out, held, rows, strips, in_sem, out_sem):
-    plane, total, wide = out.shape
+def split_kernel(grads, master, first, second, out, rows):
+    plane, _, wide = out.shape
     count = grads.shape[0]
-    pieces = in_sem.shape[0]
-    size = count // pieces
-    arrivals = [
-        pltpu.make_async_copy(
-            grads.at[pl.ds(i * size, size), :], held.at[pl.ds(i * size, size), :], in_sem.at[i]
-        )
-        for i in range(pieces)
-    ]
-    for arrival in arrivals:
-        arrival.start()
+    for k in range(plane):
+        out[k, :count, :] = grads[:, k * wide : (k + 1) * wide]
     fill_rows(rows, (master, first, second))
     high, low = two_terms(rows[0])
     values = (high, low, rows[1].astype(jnp.bfloat16), rows[2].astype(jnp.bfloat16))
     for t, value in enumerate(values):
         at = count + t * SLOT_ROWS
         for k in range(plane):
-            strips[k, at : at + SLOT_ROWS, :] = value[:, k * wide : (k + 1) * wide]
+            out[k, at : at + SLOT_ROWS, :] = value[:, k * wide : (k + 1) * wide]
+
+
+def split(grads, master, first, second, plane):
+    count, width = grads.shape
+    shape = (plane, count + KINDS * SLOT_ROWS, width // plane)
+    return pl.pallas_call(
+        split_kernel,
+        out_shape=jax.ShapeDtypeStruct(shape, grads.dtype),
+        in_specs=[VMEM] * 4,
+        out_specs=VMEM,
+        scratch_shapes=[pltpu.VMEM((3, SLOT_ROWS, width), jnp.float32)],
+        name="split",
+    )(grads, master, first, second)
+
+
+def join_kernel(core, strips, place, *refs):
+    out, placed, sem = refs[-3:]
+    count, _, wide = placed.shape
     moves = []
-    for i in range(pieces + 1):
-        at, length = i * size, size
-        if i < pieces:
-            arrivals[i].wait()
-            for k in range(plane):
-                strips[k, at : at + size, :] = held[at : at + size, k * wide : (k + 1) * wide]
-        else:
-            length = total - count
-        here = pl.ds(at, length)
-        moves.append(
-            pltpu.make_async_copy(strips.at[:, here, :], out.at[:, here, :], out_sem.at[i])
-        )
+    for i in range(count):
+        rows = jnp.concatenate([strips[side * count + i] for side in range(SIDES)], axis=0)
+        placed[i] = choose(place[...], rows).astype(placed.dtype)
+        lane = pl.multiple_of((2 * i + core[0]) * wide, wide)
+        moves.append(pltpu.make_async_copy(placed.at[i], out.at[:, pl.ds(lane, wide)], sem.at[i]))
         moves[-1].start()
     for move in moves:
         move.wait()
 
 
-def split(grads, master, first, second, plane):
-    count, width = grads.shape
-    shape = (plane, count + KINDS * SLOT_ROWS, width // plane)
-    pieces = 4
-    return pl.pallas_call(
-        split_kernel,
-        out_shape=jax.ShapeDtypeStruct(shape, grads.dtype),
-        in_specs=[ANY, VMEM, VMEM, VMEM],
-        out_specs=ANY,
-        scratch_shapes=[
-            pltpu.VMEM((count, width), grads.dtype),
-            pltpu.VMEM((3, SLOT_ROWS, width), jnp.float32),
-            pltpu.VMEM(shape, grads.dtype),
-            pltpu.SemaphoreType.DMA((pieces,)),
-            pltpu.SemaphoreType.DMA((pieces + 1,)),
-        ],
-        name="split",
-    )(grads, master, first, second)
-
-
-def join_kernel(core, strips, *refs):
-    out, sem = refs[-2:]
-    count, _, wide = strips.shape
-    moves = [
-        pltpu.make_async_copy(
-            strips.at[i],
-            out.at[:, pl.ds(pl.multiple_of((2 * i + core[0]) * wide, wide), wide)],
-            sem.at[i],
-        )
-        for i in range(count)
-    ]
-    for move in moves:
-        move.start()
-    for move in moves:
-        move.wait()
-
-
-def join(core, strips, *before):
-    count, rows, wide = strips.shape
+def join(core, strips, place, *before):
+    count, wide = strips.shape[0] // SIDES, strips.shape[2]
+    rows = place.shape[0]
     return pl.pallas_call(
         join_kernel,
         out_shape=jax.ShapeDtypeStruct((rows, 2 * count * wide), strips.dtype),
-        in_specs=[SMEM, VMEM] + [ANY] * len(before),
+        in_specs=[SMEM, VMEM, VMEM] + [ANY] * len(before),
         out_specs=ANY,
-        scratch_shapes=[pltpu.SemaphoreType.DMA((count,))],
-        input_output_aliases={2: 0} if before else {},
+        scratch_shapes=[
+            pltpu.VMEM((count, rows, wide), strips.dtype),
+            pltpu.SemaphoreType.DMA((count,)),
+        ],
+        input_output_aliases={3: 0} if before else {},
         name="join",
-    )(core.reshape(1), near(strips), *before)
+    )(core.reshape(1), near(strips), place, *before)
 
 
 def own_kernel(at, got, rms, master, first, second, *refs):
@@ -191,7 +162,8 @@
 
 def reduce_kernel(got, take, out):
     ring = got.shape[0]
-    part = out.shape[1] // (2 + KINDS)
+    part = take.shape[0] // KINDS
+    half = part // SIDES
     total = got[0, :part, :].astype(jnp.float32) + got[0, part : 2 * part, :].astype(jnp.float32)
     for z in range(1, ring):
         total = total + (
@@ -203,7 +175,10 @@
     for z in range(ring):
         out[z, :part, :] = high
         out[z, part : 2 * part, :] = low
-        out[z, 2 * part :, :] = lines
+        for t in range(KINDS):
+            at = t * part + z % SIDES * half
+            to = 2 * part + t * half
+            out[z, to : to + half, :] = lines[at : at + half, :]
 
 
 def ordered(every, term, part):
@@ -226,18 +201,25 @@
             out[j, layer] = sent[j * SLOT_ROWS : (j + 1) * SLOT_ROWS, :]
 
 
-def step_kernel(element_total, every, got, place, copies, rms):
-    part = place.shape[1] // every.shape[0]
+def step_kernel(element_total, side, every, got, copies, rms):
+    ring = every.shape[0]
+    half = copies.shape[1] // ring
+    part = half * SIDES
     squares = jnp.sum(got[...], axis=0)[SLOT_ROWS - 1 :, :]
     grad_rms = jnp.sqrt(squares / element_total + 1e-06)
     rms[...] = grad_rms
     clip_factor = jnp.minimum(1.0, 1.0 / grad_rms)
-    terms = [ordered(every, t, part).astype(jnp.float32) for t in range(2 + KINDS)]
-    grad = (terms[0] + terms[1]) * clip_factor
-    param = adamw(terms[2] + terms[3], terms[4], terms[5], grad)[0]
-    weights = choose(place[...], param.astype(copies.dtype)).astype(copies.dtype)
-    for x in range(copies.shape[0]):
-        copies[x] = weights
+
+    def stack(at):
+        rows = [every[z, pl.ds(at, half), :] for z in range(ring)]
+        return jnp.concatenate(rows, axis=0).astype(jnp.float32)
+
+    mine = pl.multiple_of(side[0] * half, half)
+    grad = (stack(mine) + stack(pl.multiple_of(part + mine, half))) * clip_factor
+    terms = [stack(2 * part + t * half) for t in range(KINDS)]
+    param = adamw(terms[0] + terms[1], terms[2], terms[3], grad)[0].astype(copies.dtype)
+    for i in range(copies.shape[0]):
+        copies[i] = param
 
 
 def shards(micro_grads, master, moment_one, moment_two, owner, slot):
@@ -269,7 +251,9 @@
     dealt = per_row(member * part + turn * slab)
     pair_of = per_row(member * pair + turn % deal * slab)
     order = dealt[None, :] == count[:, None]
-    place = dealt[:, None] == count[None, :]
+    half = part // SIDES
+    formed = dealt % part // half * (rows // SIDES) + dealt // part * half + dealt % half
+    place = formed[:, None] == count[None, :]
     line_at = jnp.sum(jnp.where(order, line_of[None, :], 0), axis=1)
     pick = (my_z * plane_lines + few)[:, None] == line_at[None, :]
     mine = line_of[None, :] == (my_z * plane_lines + few)[:, None]
@@ -285,7 +269,7 @@
     take = comes.reshape(KINDS * part, 1) == chunks[None, :]
 
     raw = exchange(split(micro_grads[0, 0], master[0], moment_one[0], moment_two[0], plane), PLANE)
-    my_slots = lax.axis_index((RING, *PLANE)) * SLOT_ROWS
+    my_slots = lax.axis_index((*RING, *PLANE)) * SLOT_ROWS
     my_slots = my_slots + slab * jnp.arange(capacity, dtype=i32)
     keep = jnp.any(line[None, :] == my_slots[:, None], axis=1).astype(i32)
     at = jnp.concatenate([lax.axis_index("layer").astype(i32).reshape(1), keep])
@@ -301,7 +285,7 @@
     )(near(raw), order, route)
     reduced = pl.pallas_call(
         reduce_kernel,
-        out_shape=pltpu.VMEM((ring, (2 + KINDS) * part, wide), bf16),
+        out_shape=pltpu.VMEM((ring, 2 * part + KINDS * part // SIDES, wide), bf16),
         in_specs=[VMEM] * 2,
         out_specs=VMEM,
         name="reduce",
@@ -320,17 +304,17 @@
     copies, rms = pl.pallas_call(
         lambda *refs: step_kernel(float(layers * rows * width), *refs),
         out_shape=(
-            pltpu.VMEM((lax.axis_size(HALF), rows, wide), bf16),
+            pltpu.VMEM((lax.axis_size(FORM), rows // SIDES, wide), bf16),
             jax.ShapeDtypeStruct((1, wide), f32),
         ),
-        in_specs=[VMEM] * 3,
+        in_specs=[SMEM] + [VMEM] * 2,
         out_specs=(VMEM, VMEM),
         name="step",
-    )(near(every), near(got), place)
+    )(lax.axis_index("side").astype(i32).reshape(1), near(every), near(got))
     core = lax.axis_index("c")
-    halves, got, rms = lax.optimization_barrier((exchange(copies, HALF), got, rms))
+    halves, got, rms = lax.optimization_barrier((exchange(copies, FORM), got, rms))
     others = lax.ppermute(halves, "c", [(0, 1), (1, 0)])
-    weights = join(core, halves)
+    weights = join(core, halves, place)
 
     new = pl.pallas_call(
         own_kernel,
@@ -344,15 +328,15 @@
         name="own",
     )(at, near(got), near(rms), *[near(o[0]) for o in (master, moment_one, moment_two)])
     others, weights = lax.optimization_barrier((others, weights))
-    weights = join(1 - core, others, weights)
+    weights = join(1 - core, others, place, weights)
     return (new[0][None], new[1][None], new[2][None], weights[None], rms[0, 0])
 
 
 def solution(mesh):
     ring = mesh.shape["dp"] // math.prod(PLANE_SHAPE)
-    devices = mesh.devices.reshape(ring, *PLANE_SHAPE, mesh.shape["layer"])
-    split_mesh = Mesh(devices, (RING, *PLANE, "layer"))
-    dp = (RING, *PLANE)
+    devices = mesh.devices.reshape(ring // SIDES, SIDES, *PLANE_SHAPE, mesh.shape["layer"])
+    split_mesh = Mesh(devices, (*RING, *PLANE, "layer"))
+    dp = (*RING, *PLANE)
     in_specs = (
         P("layer", dp, None, None),
         P("layer", dp, None, None),

time: 128 us -> 129 us (level)
  no operation moved by 1% of the time
where the time goes in v11:
time: 129 us
  blocking collectives  88 us (68%)
  starting transfers between devices  14.9 us (12%)
  waiting for transfers between devices  14.6 us (11%)
  Pallas kernels  7.7 us (6%)
  other arithmetic  2.11 us (2%)
    all_to_all x4, blocking collectives, exchange(): return lax.all_to_all(chunks, axis, 0, 0, tiled=True)  88 us
    all_to_all x1, waiting for transfers between devices, exchange(): return lax.all_to_all(chunks, axis, 0, 0, tiled=True)  14.6 us
    all_to_all x1, starting transfers between devices, exchange(): return lax.all_to_all(chunks, axis, 0, 0, tiled=True)  10.5 us
    ppermute x1, starting transfers between devices, shards(): others = lax.ppermute(halves, 'c', [(0, 1), (1, 0)])  4.42 us
  transfers between devices with their start and end apart: 2, of which 1 were waited for; matrix products, arithmetic and copies ran while one was open for 2% of the time, Pallas kernels for 2%

profile of v11, /device:TPU:1, one launch (start us, length us, event | category | flops | bytes accessed | tf_op | source)
XLA Modules:
  0.0 128.7 jit_solution(3421455773154269343)
XLA Ops:
  0.6 2.5 %split.1 = bf16[16,288,128]{2,1,0:T(8,128)(2,1)} custom-call(bf16[256,2048]{1,0:T(8,128)(2,1)} %bitcast.30, f32[3,2,2048]{2,1,0:T(2,128)} %bitcast.22, f32[3,2,2048]{2,1,0:T(2,128)} %bitcast.24, f32[3,2,2048]{2,1,0:T(2,128)} %bitcast.26), custom_call_target="tpu_custom_call" | custom-call | tf_op jit(solution)/shard_map/split/pallas_call | solution.py:85
  3.2 10.5 %all-to-all-start = ((bf16[16,288,128]{2,1,0:T(8,128)(2,1)}), bf16[16,288,128]{2,1,0:T(8,128)(2,1)S(1)}, u32[]{:S(2)}, u32[]{:S(2)}) async-start(bf16[16,288,128]{2,1,0:T(8,128)(2,1)} %split.1), calls=%async_computation | async-start | bytes 2359296 | tf_op jit(solution)/shard_map/all_to_all | solution.py:39
  13.7 0.2 compare_reduce_fusion
  13.9 0.2 convert_reduce_fusion
  14.1 0.1 iota_add_fusion.1
  14.2 0.1 add.339
  14.3 0.1 add_add_fusion
  14.4 0.1 add.354
  14.6 0.1 iota_add_fusion
  14.7 0.1 add.343
  14.8 0.1 select_reduce_fusion
  14.9 0.1 and_select_fusion.4
  15.0 0.1 add.368
  15.1 0.7 pad_add_fusion.at
  15.8 0.2 select_reduce_fusion.1
  16.0 0.1 compare_convert_fusion.pick
  16.1 0.1 fusion.3.take
  16.2 0.1 fusion.1
  16.3 0.1 fusion.route
  16.4 14.6 %all-to-all-done.raw = bf16[16,288,128]{2,1,0:T(8,128)(2,1)S(1)} async-done(((bf16[16,288,128]{2,1,0:T(8,128)(2,1)}), bf16[16,288,128]{2,1,0:T(8,128)(2,1)S(1)}, u32[]{:S(2)}, u32[]{:S(2)}) %all-to-all-start) | async-done | bytes 1179680 | tf_op jit(solution)/shard_map/all_to_all | solution.py:39
  31.0 0.5 pack.1
  31.5 25.8 %all_to_all.25.got = bf16[8,112,128]{2,1,0:T(8,128)(2,1)S(1)} all-to-all(bf16[8,112,128]{2,1,0:T(8,128)(2,1)S(1)} %pack.1), channel_id=1, replica_groups=mesh['z'=4,'side'=2,'pair'=2,'x'=4,'c'=2,'layer'=4] {'z','side'}, dimensions={0} | all-to-all | bytes 458752 | tf_op jit(solution)/shard_map/all_to_all | solution.py:39
  57.2 0.2 reduce.1
  57.4 25.0 %all_to_all.26.every.refs_1_ = bf16[8,128,128]{2,1,0:T(8,128)(2,1)S(1)} all-to-all(bf16[8,128,128]{2,1,0:T(8,128)(2,1)S(1)} %reduce.1), channel_id=1, replica_groups=mesh['z'=4,'side'=2,'pair'=2,'x'=4,'c'=2,'layer'=4] {'z','side'}, dimensions={0} | all-to-all | bytes 524288 | tf_op jit(solution)/shard_map/all_to_all | solution.py:39
  82.4 0.2 send.1
  82.6 19.7 %all_to_all.27.refs_2_.got = f32[64,8,128]{2,1,0:T(8,128)S(1)} all-to-all(f32[64,8,128]{2,1,0:T(8,128)S(1)} %bitcast.21), channel_id=1, replica_groups=mesh['z'=4,'side'=2,'pair'=2,'x'=4,'c'=2,'layer'=4] {'pair','x','c','lay..., dimensions={0} | all-to-all | bytes 524288 | tf_op jit(solution)/shard_map/all_to_all | solution.py:39
  102.3 0.6 step.1
  102.9 17.5 %all_to_all.28.strips = bf16[16,128,128]{2,1,0:T(8,128)(2,1)S(1)} all-to-all(bf16[16,128,128]{2,1,0:T(8,128)(2,1)S(1)} %get-tuple-element.28), channel_id=1, replica_groups=mesh['z'=4,'side'=2,'pair'=2,'x'=4,'c'=2,'layer'=4] {'side','pair','x'}, dimensions={0} | all-to-all | bytes 1048576 | tf_op jit(solution)/shard_map/all_to_all | solution.py:39
  120.5 4.4 %collective-permute-start = (bf16[16,128,128]{2,1,0:T(8,128)(2,1)S(1)}, bf16[16,128,128]{2,1,0:T(8,128)(2,1)S(1)}, u32[]{:S(2)}, u32[]{:S(2)}) collective-permute-start(bf16[16,128,128]{2,1,0:T(8,128)(2,1)S(1)} %all_to_all.28.strips), channel_id=1, source_target_pairs={{0,4},{4,0},{1,5},{5,1},{2,6},{6,2},{3,7},{7,3},{8,12},{12,8},{9,1... | collective-permute-start | bytes 1572872 | tf_op jit(solution)/shard_map/ppermute | solution.py:316
  124.9 1.1 join.2.refs_0_
  126.1 1.5 %own.1 = (f32[3,2,2048]{2,1,0:T(2,128)}, f32[3,2,2048]{2,1,0:T(2,128)}, f32[3,2,2048]{2,1,0:T(2,128)}) custom-call(s32[4]{0:T(128)} %pad_add_fusion.at, f32[64,8,128]{2,1,0:T(8,128)S(1)} %all_to_all.27.refs_2_.got, f32[1,128]{1,0:T(1,128)S(1)} %copy-done.3, f32[3,2,2048]{2,1,0:T(2,128)S(1)} %bitcast.23, f32[3,2,2048]{2,1,0:T(2,128)S(1)} %bitcast.25, ...), custom_call_target="tpu_custom_call" | custom-call | tf_op jit(solution)/shard_map/own/pallas_call | solution.py:319
  127.6 1.1 join.3
  (24 shorter events, 0.1 us)
Async XLA Ops:
  3.2 10.5 %copy-start.4 = (s32[1,128]{1,0:T(1,128)S(1)}, s32[1,128]{1,0:T(1,128)}, u32[]{:S(2)}) copy-start(s32[1,128]{1,0:T(1,128)} %param.11) | copy-start | bytes 1540
  3.2 10.5 %copy-start.5 = (s32[1,128]{1,0:T(1,128)S(1)}, s32[1,128]{1,0:T(1,128)}, u32[]{:S(2)}) copy-start(s32[1,128]{1,0:T(1,128)} %param.10) | copy-start | bytes 1540
  3.2 27.9 %all-to-all-start = ((bf16[16,288,128]{2,1,0:T(8,128)(2,1)}), bf16[16,288,128]{2,1,0:T(8,128)(2,1)S(1)}, u32[]{:S(2)}, u32[]{:S(2)}) async-start(bf16[16,288,128]{2,1,0:T(8,128)(2,1)} %split.1), calls=%async_computation | async-start | bytes 2359296 | tf_op jit(solution)/shard_map/all_to_all | solution.py:39
  102.9 23.1 %copy-start = (f32[1,3,2,2048]{3,2,1,0:T(2,128)S(1)}, f32[1,3,2,2048]{3,2,1,0:T(2,128)}, u32[]{:S(2)}) copy-start(f32[1,3,2,2048]{3,2,1,0:T(2,128)} %param.7) | copy-start | bytes 147460
  102.9 23.1 %copy-start.1 = (f32[1,3,2,2048]{3,2,1,0:T(2,128)S(1)}, f32[1,3,2,2048]{3,2,1,0:T(2,128)}, u32[]{:S(2)}) copy-start(f32[1,3,2,2048]{3,2,1,0:T(2,128)} %param.8) | copy-start | bytes 147460
  102.9 23.1 %copy-start.2 = (f32[1,3,2,2048]{3,2,1,0:T(2,128)S(1)}, f32[1,3,2,2048]{3,2,1,0:T(2,128)}, u32[]{:S(2)}) copy-start(f32[1,3,2,2048]{3,2,1,0:T(2,128)} %param.9) | copy-start | bytes 147460
  102.9 23.1 %copy-start.3 = (f32[1,128]{1,0:T(1,128)S(1)}, f32[1,128]{1,0:T(1,128)}, u32[]{:S(2)}) copy-start(f32[1,128]{1,0:T(1,128)} %get-tuple-element.31.rms) | copy-start | bytes 1540
  120.5 7.1 %collective-permute-start = (bf16[16,128,128]{2,1,0:T(8,128)(2,1)S(1)}, bf16[16,128,128]{2,1,0:T(8,128)(2,1)S(1)}, u32[]{:S(2)}, u32[]{:S(2)}) collective-permute-start(bf16[16,128,128]{2,1,0:T(8,128)(2,1)S(1)} %all_to_all.28.strips), channel_id=1, source_target_pairs={{0,4},{4,0},{1,5},{5,1},{2,6},{6,2},{3,7},{7,3},{8,12},{12,8},{9,1... | collective-permute-start | bytes 1572872 | tf_op jit(solution)/shard_map/ppermute | solution.py:316

commit v12 on v9

--- a/solution.py
+++ b/solution.py
@@ -64,60 +64,29 @@
         rows[i, capacity * slab :, :] = jnp.ones_like(rows[i, capacity * slab :, :])
 
 
-def split_kernel(grads, master, first, second, out, held, rows, strips, in_sem, out_sem):
-    plane, total, wide = out.shape
+def split_kernel(grads, master, first, second, out, rows):
+    plane, _, wide = out.shape
     count = grads.shape[0]
-    pieces = in_sem.shape[0]
-    size = count // pieces
-    arrivals = [
-        pltpu.make_async_copy(
-            grads.at[pl.ds(i * size, size), :], held.at[pl.ds(i * size, size), :], in_sem.at[i]
-        )
-        for i in range(pieces)
-    ]
-    for arrival in arrivals:
-        arrival.start()
+    for k in range(plane):
+        out[k, :count, :] = grads[:, k * wide : (k + 1) * wide]
     fill_rows(rows, (master, first, second))
     high, low = two_terms(rows[0])
     values = (high, low, rows[1].astype(jnp.bfloat16), rows[2].astype(jnp.bfloat16))
     for t, value in enumerate(values):
         at = count + t * SLOT_ROWS
         for k in range(plane):
-            strips[k, at : at + SLOT_ROWS, :] = value[:, k * wide : (k + 1) * wide]
-    moves = []
-    for i in range(pieces + 1):
-        at, length = i * size, size
-        if i < pieces:
-            arrivals[i].wait()
-            for k in range(plane):
-                strips[k, at : at + size, :] = held[at : at + size, k * wide : (k + 1) * wide]
-        else:
-            length = total - count
-        here = pl.ds(at, length)
-        moves.append(
-            pltpu.make_async_copy(strips.at[:, here, :], out.at[:, here, :], out_sem.at[i])
-        )
-        moves[-1].start()
-    for move in moves:
-        move.wait()
+            out[k, at : at + SLOT_ROWS, :] = value[:, k * wide : (k + 1) * wide]
 
 
 def split(grads, master, first, second, plane):
     count, width = grads.shape
     shape = (plane, count + KINDS * SLOT_ROWS, width // plane)
-    pieces = 4
     return pl.pallas_call(
         split_kernel,
         out_shape=jax.ShapeDtypeStruct(shape, grads.dtype),
-        in_specs=[ANY, VMEM, VMEM, VMEM],
-        out_specs=ANY,
-        scratch_shapes=[
-            pltpu.VMEM((count, width), grads.dtype),
-            pltpu.VMEM((3, SLOT_ROWS, width), jnp.float32),
-            pltpu.VMEM(shape, grads.dtype),
-            pltpu.SemaphoreType.DMA((pieces,)),
-            pltpu.SemaphoreType.DMA((pieces + 1,)),
-        ],
+        in_specs=[VMEM] * 4,
+        out_specs=VMEM,
+        scratch_shapes=[pltpu.VMEM((3, SLOT_ROWS, width), jnp.float32)],
         name="split",
     )(grads, master, first, second)
 

time: 128 us -> 128 us (level)
  no operation moved by 1% of the time
where the time goes in v12:
time: 128 us
  blocking collectives  87.7 us (69%)
  starting transfers between devices  14.7 us (11%)
  waiting for transfers between devices  14.6 us (11%)
  Pallas kernels  7.12 us (6%)
  other arithmetic  2.1 us (2%)
    all_to_all x4, blocking collectives, exchange(): return lax.all_to_all(chunks, axis, 0, 0, tiled=True)  87.7 us
    all_to_all x1, waiting for transfers between devices, exchange(): return lax.all_to_all(chunks, axis, 0, 0, tiled=True)  14.6 us
    all_to_all x1, starting transfers between devices, exchange(): return lax.all_to_all(chunks, axis, 0, 0, tiled=True)  10.5 us
    ppermute x1, starting transfers between devices, shards(): others = lax.ppermute(halves, 'c', [(0, 1), (1, 0)])  4.16 us
  transfers between devices with their start and end apart: 2, of which 1 were waited for; matrix products, arithmetic and copies ran while one was open for 2% of the time, Pallas kernels for 2%

profile of v12, /device:TPU:1, one launch (start us, length us, event | category | flops | bytes accessed | tf_op | source)
XLA Modules:
  0.0 127.6 jit_solution(12906298431117349645)
XLA Ops:
  0.6 2.5 %split.1 = bf16[16,288,128]{2,1,0:T(8,128)(2,1)} custom-call(bf16[256,2048]{1,0:T(8,128)(2,1)} %bitcast.29, f32[3,2,2048]{2,1,0:T(2,128)} %bitcast.21, f32[3,2,2048]{2,1,0:T(2,128)} %bitcast.23, f32[3,2,2048]{2,1,0:T(2,128)} %bitcast.25), custom_call_target="tpu_custom_call" | custom-call | tf_op jit(solution)/shard_map/split/pallas_call | solution.py:84
  3.2 10.5 %all-to-all-start = ((bf16[16,288,128]{2,1,0:T(8,128)(2,1)}), bf16[16,288,128]{2,1,0:T(8,128)(2,1)S(1)}, u32[]{:S(2)}, u32[]{:S(2)}) async-start(bf16[16,288,128]{2,1,0:T(8,128)(2,1)} %split.1), calls=%async_computation | async-start | bytes 2359296 | tf_op jit(solution)/shard_map/all_to_all | solution.py:38
  13.7 0.2 compare_reduce_fusion
  13.9 0.2 convert_reduce_fusion
  14.1 0.1 iota_add_fusion.1
  14.2 0.1 add.287
  14.3 0.1 add_add_fusion
  14.4 0.1 add.301
  14.6 0.1 iota_add_fusion
  14.7 0.1 add.291
  14.8 0.1 select_reduce_fusion
  14.9 0.1 and_select_fusion
  15.0 0.1 add.315
  15.1 0.7 pad_add_fusion.at
  15.8 0.2 select_reduce_fusion.1
  16.0 0.1 compare_convert_fusion.pick
  16.1 0.1 fusion.3.take
  16.2 0.1 fusion.2
  16.3 0.1 fusion.route
  16.4 14.6 %all-to-all-done.raw = bf16[16,288,128]{2,1,0:T(8,128)(2,1)S(1)} async-done(((bf16[16,288,128]{2,1,0:T(8,128)(2,1)}), bf16[16,288,128]{2,1,0:T(8,128)(2,1)S(1)}, u32[]{:S(2)}, u32[]{:S(2)}) %all-to-all-start) | async-done | bytes 1179680 | tf_op jit(solution)/shard_map/all_to_all | solution.py:38
  31.0 0.5 pack.1
  31.5 25.8 %all_to_all.25.got = bf16[8,112,128]{2,1,0:T(8,128)(2,1)S(1)} all-to-all(bf16[8,112,128]{2,1,0:T(8,128)(2,1)S(1)} %pack.1), channel_id=1, replica_groups=mesh['z'=8,'pair'=2,'x'=4,'c'=2,'layer'=4] {'z'}, dimensions={0} | all-to-all | bytes 458752 | tf_op jit(solution)/shard_map/all_to_all | solution.py:38
  57.2 0.2 reduce.1
  57.4 31.2 %all_to_all.26.every.refs_0_ = bf16[8,192,128]{2,1,0:T(8,128)(2,1)S(1)} all-to-all(bf16[8,192,128]{2,1,0:T(8,128)(2,1)S(1)} %reduce.1), channel_id=1, replica_groups=mesh['z'=8,'pair'=2,'x'=4,'c'=2,'layer'=4] {'z'}, dimensions={0} | all-to-all | bytes 786432 | tf_op jit(solution)/shard_map/all_to_all | solution.py:38
  88.6 0.2 send.1
  88.8 19.5 %all_to_all.27.refs_1_.got = f32[64,8,128]{2,1,0:T(8,128)S(1)} all-to-all(f32[64,8,128]{2,1,0:T(8,128)S(1)} %bitcast.20), channel_id=1, replica_groups=mesh['z'=8,'pair'=2,'x'=4,'c'=2,'layer'=4] {'pair','x','c','layer'}, dimensions={0} | all-to-all | bytes 524288 | tf_op jit(solution)/shard_map/all_to_all | solution.py:38
  108.3 0.6 step.1
  108.9 11.3 %all_to_all.28.strips = bf16[8,256,128]{2,1,0:T(8,128)(2,1)S(1)} all-to-all(bf16[8,256,128]{2,1,0:T(8,128)(2,1)S(1)} %get-tuple-element.29), channel_id=1, replica_groups=mesh['z'=8,'pair'=2,'x'=4,'c'=2,'layer'=4] {'pair','x'}, dimensions={0} | all-to-all | bytes 1048576 | tf_op jit(solution)/shard_map/all_to_all | solution.py:38
  120.1 4.2 %collective-permute-start = (bf16[8,256,128]{2,1,0:T(8,128)(2,1)S(1)}, bf16[8,256,128]{2,1,0:T(8,128)(2,1)S(1)}, u32[]{:S(2)}, u32[]{:S(2)}) collective-permute-start(bf16[8,256,128]{2,1,0:T(8,128)(2,1)S(1)} %all_to_all.28.strips), channel_id=1, source_target_pairs={{0,4},{4,0},{1,5},{5,1},{2,6},{6,2},{3,7},{7,3},{8,12},{12,8},{9,1... | collective-permute-start | bytes 1572872 | tf_op jit(solution)/shard_map/ppermute | solution.py:301
  124.3 0.9 join.2.refs_0_
  125.2 1.5 %own.1 = (f32[3,2,2048]{2,1,0:T(2,128)}, f32[3,2,2048]{2,1,0:T(2,128)}, f32[3,2,2048]{2,1,0:T(2,128)}) custom-call(s32[4]{0:T(128)} %pad_add_fusion.at, f32[64,8,128]{2,1,0:T(8,128)S(1)} %all_to_all.27.refs_1_.got, f32[1,128]{1,0:T(1,128)S(1)} %copy-done.3, f32[3,2,2048]{2,1,0:T(2,128)S(1)} %bitcast.22, f32[3,2,2048]{2,1,0:T(2,128)S(1)} %bitcast.24, ...), custom_call_target="tpu_custom_call" | custom-call | tf_op jit(solution)/shard_map/own/pallas_call | solution.py:304
  126.7 0.8 join.3
  (23 shorter events, 0.1 us)
Async XLA Ops:
  3.2 10.5 %copy-start.4 = (s32[1,128]{1,0:T(1,128)S(1)}, s32[1,128]{1,0:T(1,128)}, u32[]{:S(2)}) copy-start(s32[1,128]{1,0:T(1,128)} %param.11) | copy-start | bytes 1540
  3.2 10.5 %copy-start.5 = (s32[1,128]{1,0:T(1,128)S(1)}, s32[1,128]{1,0:T(1,128)}, u32[]{:S(2)}) copy-start(s32[1,128]{1,0:T(1,128)} %param.10) | copy-start | bytes 1540
  3.2 27.9 %all-to-all-start = ((bf16[16,288,128]{2,1,0:T(8,128)(2,1)}), bf16[16,288,128]{2,1,0:T(8,128)(2,1)S(1)}, u32[]{:S(2)}, u32[]{:S(2)}) async-start(bf16[16,288,128]{2,1,0:T(8,128)(2,1)} %split.1), calls=%async_computation | async-start | bytes 2359296 | tf_op jit(solution)/shard_map/all_to_all | solution.py:38
  108.9 16.3 %copy-start = (f32[1,3,2,2048]{3,2,1,0:T(2,128)S(1)}, f32[1,3,2,2048]{3,2,1,0:T(2,128)}, u32[]{:S(2)}) copy-start(f32[1,3,2,2048]{3,2,1,0:T(2,128)} %param.7) | copy-start | bytes 147460
  108.9 16.3 %copy-start.1 = (f32[1,3,2,2048]{3,2,1,0:T(2,128)S(1)}, f32[1,3,2,2048]{3,2,1,0:T(2,128)}, u32[]{:S(2)}) copy-start(f32[1,3,2,2048]{3,2,1,0:T(2,128)} %param.8) | copy-start | bytes 147460
  108.9 16.3 %copy-start.2 = (f32[1,3,2,2048]{3,2,1,0:T(2,128)S(1)}, f32[1,3,2,2048]{3,2,1,0:T(2,128)}, u32[]{:S(2)}) copy-start(f32[1,3,2,2048]{3,2,1,0:T(2,128)} %param.9) | copy-start | bytes 147460
  108.9 16.3 %copy-start.3 = (f32[1,128]{1,0:T(1,128)S(1)}, f32[1,128]{1,0:T(1,128)}, u32[]{:S(2)}) copy-start(f32[1,128]{1,0:T(1,128)} %get-tuple-element.32.rms) | copy-start | bytes 1540
  120.1 6.6 %collective-permute-start = (bf16[8,256,128]{2,1,0:T(8,128)(2,1)S(1)}, bf16[8,256,128]{2,1,0:T(8,128)(2,1)S(1)}, u32[]{:S(2)}, u32[]{:S(2)}) collective-permute-start(bf16[8,256,128]{2,1,0:T(8,128)(2,1)S(1)} %all_to_all.28.strips), channel_id=1, source_target_pairs={{0,4},{4,0},{1,5},{5,1},{2,6},{6,2},{3,7},{7,3},{8,12},{12,8},{9,1... | collective-permute-start | bytes 1572872 | tf_op jit(solution)/shard_map/ppermute | solution.py:301

commit v13 on v12

--- a/solution.py
+++ b/solution.py
@@ -21,6 +21,7 @@
 HALF = ("pair", "x")
 SLOT_ROWS = 8
 KINDS = 4
+EXTRA = 4
 
 
 def adamw(param, first, second, grad):
@@ -158,36 +159,48 @@
             out[z, i * part : i * part + size, :] = chosen[z * size : (z + 1) * size, :]
 
 
-def reduce_kernel(got, take, out):
+def reduce_kernel(got, take, spread, out):
     ring = got.shape[0]
-    part = out.shape[1] // (2 + KINDS)
+    part = take.shape[0] // KINDS
+    extra = spread.shape[0] // ring
     total = got[0, :part, :].astype(jnp.float32) + got[0, part : 2 * part, :].astype(jnp.float32)
     for z in range(1, ring):
         total = total + (
             got[z, :part, :].astype(jnp.float32) + got[z, part : 2 * part, :].astype(jnp.float32)
         )
     high, low = two_terms(total)
+    lows = choose(spread[...], low)
+    squares = jnp.sum(total * total) + jnp.zeros((extra, total.shape[1]), jnp.float32)
+    first, _ = two_terms(squares)
+    second, _ = two_terms(squares - first.astype(jnp.float32))
+    third = squares - first.astype(jnp.float32) - second.astype(jnp.float32)
+    row = lax.broadcasted_iota(jnp.int32, squares.shape, 0)
+    parts = (first.astype(jnp.float32), second.astype(jnp.float32), third)
     lines = jnp.concatenate([got[z, 2 * part :, :] for z in range(ring)], axis=0)
     lines = choose(take[...], lines).astype(out.dtype)
     for z in range(ring):
+        block = lows[z * extra : (z + 1) * extra, :]
+        for i, value in enumerate(parts):
+            block = jnp.where(row == extra - EXTRA + i, value, block)
         out[z, :part, :] = high
-        out[z, part : 2 * part, :] = low
-        out[z, 2 * part :, :] = lines
-
-
-def ordered(every, term, part):
-    return jnp.concatenate(
-        [every[z, term * part : (term + 1) * part, :] for z in range(every.shape[0])], axis=0
-    )
-
-
-def send_kernel(every, pick, out):
+        out[z, part : part + extra, :] = block.astype(out.dtype)
+        out[z, part + extra :, :] = lines
+
+
+def stack(every, at, size):
+    return jnp.concatenate([every[z, at : at + size, :] for z in range(every.shape[0])], axis=0)
+
+
+def send_kernel(every, pick, pick_low, out):
     plane, layers, _, wide = out.shape
-    part = pick.shape[1] // every.shape[0]
-    high, low = ordered(every, 0, part), ordered(every, 1, part)
-    total = high.astype(jnp.float32) + low.astype(jnp.float32)
-    squares = jnp.sum(total * total)
-    sent = choose(pick[...], high) + choose(pick[...], low)
+    ring = every.shape[0]
+    part, extra = pick.shape[1] // ring, pick_low.shape[1] // ring
+    high, low = stack(every, 0, part), stack(every, part, extra)
+    row = lax.broadcasted_iota(jnp.int32, low.shape, 0) % extra
+    counted = (row >= extra - EXTRA) & (row < extra - EXTRA + 3)
+    squares = jnp.where(counted, low.astype(jnp.float32), 0.0)
+    squares = jnp.sum(squares, axis=0, keepdims=True)
+    sent = choose(pick[...], high) + choose(pick_low[...], low)
     line = lax.broadcasted_iota(jnp.int32, sent.shape, 0)
     sent = jnp.where(line % SLOT_ROWS == SLOT_ROWS - 1, squares, sent)
     for j in range(plane):
@@ -197,13 +210,14 @@
 
 def step_kernel(element_total, every, got, place, copies, rms):
     part = place.shape[1] // every.shape[0]
+    states = every.shape[1] - KINDS * part
     squares = jnp.sum(got[...], axis=0)[SLOT_ROWS - 1 :, :]
     grad_rms = jnp.sqrt(squares / element_total + 1e-06)
     rms[...] = grad_rms
     clip_factor = jnp.minimum(1.0, 1.0 / grad_rms)
-    terms = [ordered(every, t, part).astype(jnp.float32) for t in range(2 + KINDS)]
-    grad = (terms[0] + terms[1]) * clip_factor
-    param = adamw(terms[2] + terms[3], terms[4], terms[5], grad)[0]
+    grad = stack(every, 0, part).astype(jnp.float32) * clip_factor
+    terms = [stack(every, states + t * part, part).astype(jnp.float32) for t in range(KINDS)]
+    param = adamw(terms[0] + terms[1], terms[2], terms[3], grad)[0]
     weights = choose(place[...], param.astype(copies.dtype)).astype(copies.dtype)
     for x in range(copies.shape[0]):
         copies[x] = weights
@@ -252,15 +266,20 @@
     within = jnp.arange(part, dtype=i32) % pair
     comes = (own_line // plane_lines * KINDS + kind) * pair + within[None, :]
     take = comes.reshape(KINDS * part, 1) == chunks[None, :]
+    extra = pair + EXTRA
+    special = jnp.arange(ring * extra, dtype=i32)
+    spread = special[:, None] == (own_line // plane_lines * extra + within)[None, :]
+    low_at = jnp.where(pair_at < 0, -1, pair_at // pair * extra + pair_at % pair)
+    pick_low = low_at[:, None] == special[None, :]
 
     raw = exchange(split(micro_grads[0, 0], master[0], moment_one[0], moment_two[0], plane), PLANE)
     my_slots = lax.axis_index((RING, *PLANE)) * SLOT_ROWS
     my_slots = my_slots + slab * jnp.arange(capacity, dtype=i32)
     keep = jnp.any(line[None, :] == my_slots[:, None], axis=1).astype(i32)
     at = jnp.concatenate([lax.axis_index("layer").astype(i32).reshape(1), keep])
-    tables = [t.astype(bf16) for t in (order, route, take, pick, place)]
+    tables = [t.astype(bf16) for t in (order, route, take, spread, pick, pick_low, place)]
     raw, at, *tables = lax.optimization_barrier((raw, at, *tables))
-    order, route, take, pick, place = [near(t) for t in tables]
+    order, route, take, spread, pick, pick_low, place = [near(t) for t in tables]
     packed = pl.pallas_call(
         pack_kernel,
         out_shape=pltpu.VMEM((ring, 2 * part + KINDS * pair, wide), bf16),
@@ -270,20 +289,20 @@
     )(near(raw), order, route)
     reduced = pl.pallas_call(
         reduce_kernel,
-        out_shape=pltpu.VMEM((ring, (2 + KINDS) * part, wide), bf16),
-        in_specs=[VMEM] * 2,
+        out_shape=pltpu.VMEM((ring, (1 + KINDS) * part + extra, wide), bf16),
+        in_specs=[VMEM] * 3,
         out_specs=VMEM,
         name="reduce",
-    )(near(exchange(packed, RING)), take)
+    )(near(exchange(packed, RING)), take, spread)
     every = exchange(reduced, RING)
 
     sent = pl.pallas_call(
         send_kernel,
         out_shape=pltpu.VMEM((plane, layers, SLOT_ROWS, wide), f32),
-        in_specs=[VMEM] * 2,
+        in_specs=[VMEM] * 3,
         out_specs=VMEM,
         name="send",
-    )(near(every), pick)
+    )(near(every), pick, pick_low)
     got = exchange(sent.reshape(plane * layers, SLOT_ROWS, wide), (*PLANE, "layer"))
 
     copies, rms = pl.pallas_call(

time: 128 us -> 127 us (level)
  blocking collectives: 87.7 us -> 86.4 us
    all_to_all x4, blocking collectives: 87.7 us -> 86.4 us  [exchange(): return lax.all_to_all(chunks, axis, 0, 0, tiled=True)]
where the time goes in v13:
time: 127 us; the launch traced here: 126 us
  blocking collectives  86.4 us (68%)
  starting transfers between devices  14.7 us (12%)
  waiting for transfers between devices  14.6 us (11%)
  Pallas kernels  7.11 us (6%)
  other arithmetic  2.12 us (2%)
    all_to_all x4, blocking collectives, exchange(): return lax.all_to_all(chunks, axis, 0, 0, tiled=True)  86.4 us
    all_to_all x1, waiting for transfers between devices, exchange(): return lax.all_to_all(chunks, axis, 0, 0, tiled=True)  14.6 us
    all_to_all x1, starting transfers between devices, exchange(): return lax.all_to_all(chunks, axis, 0, 0, tiled=True)  10.5 us
    ppermute x1, starting transfers between devices, shards(): others = lax.ppermute(halves, 'c', [(0, 1), (1, 0)])  4.16 us
  transfers between devices with their start and end apart: 2, of which 1 were waited for; matrix products, arithmetic and copies ran while one was open for 2% of the time, Pallas kernels for 2%

profile of v13, /device:TPU:1, one launch (start us, length us, event | category | flops | bytes accessed | tf_op | source)
XLA Modules:
  0.0 126.2 jit_solution(743457303530014262)
XLA Ops:
  0.6 2.5 %split.1 = bf16[16,288,128]{2,1,0:T(8,128)(2,1)} custom-call(bf16[256,2048]{1,0:T(8,128)(2,1)} %bitcast.29, f32[3,2,2048]{2,1,0:T(2,128)} %bitcast.21, f32[3,2,2048]{2,1,0:T(2,128)} %bitcast.23, f32[3,2,2048]{2,1,0:T(2,128)} %bitcast.25), custom_call_target="tpu_custom_call" | custom-call | tf_op jit(solution)/shard_map/split/pallas_call | solution.py:85
  3.2 10.5 %all-to-all-start = ((bf16[16,288,128]{2,1,0:T(8,128)(2,1)}), bf16[16,288,128]{2,1,0:T(8,128)(2,1)S(1)}, u32[]{:S(2)}, u32[]{:S(2)}) async-start(bf16[16,288,128]{2,1,0:T(8,128)(2,1)} %split.1), calls=%async_computation | async-start | bytes 2359296 | tf_op jit(solution)/shard_map/all_to_all | solution.py:39
  13.7 0.2 compare_reduce_fusion
  13.9 0.2 convert_reduce_fusion
  14.2 0.1 add.316
  14.3 0.1 add_add_fusion
  14.4 0.1 add.330
  14.6 0.1 iota_add_fusion
  14.7 0.1 add.320
  14.8 0.1 select_reduce_fusion
  14.9 0.1 multiply_add_fusion.1
  15.0 0.1 add.344
  15.1 0.6 pad_add_fusion.at
  15.7 0.2 select_reduce_fusion.1
  15.9 0.1 fusion.5.pick_low
  16.0 0.1 compare_convert_fusion.pick
  16.1 0.1 fusion.3.take
  16.2 0.1 fusion.2
  16.3 0.1 fusion.route
  16.4 14.6 %all-to-all-done.raw = bf16[16,288,128]{2,1,0:T(8,128)(2,1)S(1)} async-done(((bf16[16,288,128]{2,1,0:T(8,128)(2,1)}), bf16[16,288,128]{2,1,0:T(8,128)(2,1)S(1)}, u32[]{:S(2)}, u32[]{:S(2)}) %all-to-all-start) | async-done | bytes 1179680 | tf_op jit(solution)/shard_map/all_to_all | solution.py:39
  31.0 0.5 pack.1
  31.5 25.8 %all_to_all.25.got = bf16[8,112,128]{2,1,0:T(8,128)(2,1)S(1)} all-to-all(bf16[8,112,128]{2,1,0:T(8,128)(2,1)S(1)} %pack.1), channel_id=1, replica_groups=mesh['z'=8,'pair'=2,'x'=4,'c'=2,'layer'=4] {'z'}, dimensions={0} | all-to-all | bytes 458752 | tf_op jit(solution)/shard_map/all_to_all | solution.py:39
  57.2 0.2 reduce.1
  57.4 29.9 %all_to_all.26.every.refs_0_ = bf16[8,176,128]{2,1,0:T(8,128)(2,1)S(1)} all-to-all(bf16[8,176,128]{2,1,0:T(8,128)(2,1)S(1)} %reduce.1), channel_id=1, replica_groups=mesh['z'=8,'pair'=2,'x'=4,'c'=2,'layer'=4] {'z'}, dimensions={0} | all-to-all | bytes 720896 | tf_op jit(solution)/shard_map/all_to_all | solution.py:39
  87.3 0.2 send.1
  87.5 19.5 %all_to_all.27.refs_1_.got = f32[64,8,128]{2,1,0:T(8,128)S(1)} all-to-all(f32[64,8,128]{2,1,0:T(8,128)S(1)} %bitcast.20), channel_id=1, replica_groups=mesh['z'=8,'pair'=2,'x'=4,'c'=2,'layer'=4] {'pair','x','c','layer'}, dimensions={0} | all-to-all | bytes 524288 | tf_op jit(solution)/shard_map/all_to_all | solution.py:39
  107.0 0.6 step.1
  107.6 11.3 %all_to_all.28.strips = bf16[8,256,128]{2,1,0:T(8,128)(2,1)S(1)} all-to-all(bf16[8,256,128]{2,1,0:T(8,128)(2,1)S(1)} %get-tuple-element.33), channel_id=1, replica_groups=mesh['z'=8,'pair'=2,'x'=4,'c'=2,'layer'=4] {'pair','x'}, dimensions={0} | all-to-all | bytes 1048576 | tf_op jit(solution)/shard_map/all_to_all | solution.py:39
  118.8 4.2 %collective-permute-start = (bf16[8,256,128]{2,1,0:T(8,128)(2,1)S(1)}, bf16[8,256,128]{2,1,0:T(8,128)(2,1)S(1)}, u32[]{:S(2)}, u32[]{:S(2)}) collective-permute-start(bf16[8,256,128]{2,1,0:T(8,128)(2,1)S(1)} %all_to_all.28.strips), channel_id=1, source_target_pairs={{0,4},{4,0},{1,5},{5,1},{2,6},{6,2},{3,7},{7,3},{8,12},{12,8},{9,1... | collective-permute-start | bytes 1572872 | tf_op jit(solution)/shard_map/ppermute | solution.py:320
  123.0 0.9 join.2.refs_0_
  123.9 1.5 %own.1 = (f32[3,2,2048]{2,1,0:T(2,128)}, f32[3,2,2048]{2,1,0:T(2,128)}, f32[3,2,2048]{2,1,0:T(2,128)}) custom-call(s32[4]{0:T(128)} %pad_add_fusion.at, f32[64,8,128]{2,1,0:T(8,128)S(1)} %all_to_all.27.refs_1_.got, f32[1,128]{1,0:T(1,128)S(1)} %copy-done.3, f32[3,2,2048]{2,1,0:T(2,128)S(1)} %bitcast.22, f32[3,2,2048]{2,1,0:T(2,128)S(1)} %bitcast.24, ...), custom_call_target="tpu_custom_call" | custom-call | tf_op jit(solution)/shard_map/own/pallas_call | solution.py:323
  125.4 0.8 join.3
  (26 shorter events, 0.2 us)
Async XLA Ops:
  3.2 10.5 %copy-start.4 = (s32[1,128]{1,0:T(1,128)S(1)}, s32[1,128]{1,0:T(1,128)}, u32[]{:S(2)}) copy-start(s32[1,128]{1,0:T(1,128)} %param.11) | copy-start | bytes 1540
  3.2 10.5 %copy-start.5 = (s32[1,128]{1,0:T(1,128)S(1)}, s32[1,128]{1,0:T(1,128)}, u32[]{:S(2)}) copy-start(s32[1,128]{1,0:T(1,128)} %param.10) | copy-start | bytes 1540
  3.2 27.9 %all-to-all-start = ((bf16[16,288,128]{2,1,0:T(8,128)(2,1)}), bf16[16,288,128]{2,1,0:T(8,128)(2,1)S(1)}, u32[]{:S(2)}, u32[]{:S(2)}) async-start(bf16[16,288,128]{2,1,0:T(8,128)(2,1)} %split.1), calls=%async_computation | async-start | bytes 2359296 | tf_op jit(solution)/shard_map/all_to_all | solution.py:39
  107.6 16.3 %copy-start = (f32[1,3,2,2048]{3,2,1,0:T(2,128)S(1)}, f32[1,3,2,2048]{3,2,1,0:T(2,128)}, u32[]{:S(2)}) copy-start(f32[1,3,2,2048]{3,2,1,0:T(2,128)} %param.7) | copy-start | bytes 147460
  107.6 16.3 %copy-start.1 = (f32[1,3,2,2048]{3,2,1,0:T(2,128)S(1)}, f32[1,3,2,2048]{3,2,1,0:T(2,128)}, u32[]{:S(2)}) copy-start(f32[1,3,2,2048]{3,2,1,0:T(2,128)} %param.8) | copy-start | bytes 147460
  107.6 16.3 %copy-start.2 = (f32[1,3,2,2048]{3,2,1,0:T(2,128)S(1)}, f32[1,3,2,2048]{3,2,1,0:T(2,128)}, u32[]{:S(2)}) copy-start(f32[1,3,2,2048]{3,2,1,0:T(2,128)} %param.9) | copy-start | bytes 147460
  107.6 16.3 %copy-start.3 = (f32[1,128]{1,0:T(1,128)S(1)}, f32[1,128]{1,0:T(1,128)}, u32[]{:S(2)}) copy-start(f32[1,128]{1,0:T(1,128)} %get-tuple-element.36.rms) | copy-start | bytes 1540
  118.8 6.6 %collective-permute-start = (bf16[8,256,128]{2,1,0:T(8,128)(2,1)S(1)}, bf16[8,256,128]{2,1,0:T(8,128)(2,1)S(1)}, u32[]{:S(2)}, u32[]{:S(2)}) collective-permute-start(bf16[8,256,128]{2,1,0:T(8,128)(2,1)S(1)} %all_to_all.28.strips), channel_id=1, source_target_pairs={{0,4},{4,0},{1,5},{5,1},{2,6},{6,2},{3,7},{7,3},{8,12},{12,8},{9,1... | collective-permute-start | bytes 1572872 | tf_op jit(solution)/shard_map/ppermute | solution.py:320

commit v14 on v13

--- a/solution.py
+++ b/solution.py
@@ -65,29 +65,34 @@
         rows[i, capacity * slab :, :] = jnp.ones_like(rows[i, capacity * slab :, :])
 
 
-def split_kernel(grads, master, first, second, out, rows):
-    plane, _, wide = out.shape
+def split_kernel(grads, master, first, second, out, rows, tight):
+    plane, total, wide = out.shape
     count = grads.shape[0]
+    lines = (total - count) // KINDS
     for k in range(plane):
         out[k, :count, :] = grads[:, k * wide : (k + 1) * wide]
     fill_rows(rows, (master, first, second))
     high, low = two_terms(rows[0])
-    values = (high, low, rows[1].astype(jnp.bfloat16), rows[2].astype(jnp.bfloat16))
+    values = (high.astype(jnp.float32), low.astype(jnp.float32), rows[1], rows[2])
     for t, value in enumerate(values):
-        at = count + t * SLOT_ROWS
-        for k in range(plane):
-            out[k, at : at + SLOT_ROWS, :] = value[:, k * wide : (k + 1) * wide]
+        tight[t * lines : (t + 1) * lines, :] = value[:lines]
+    terms = tight[...].astype(jnp.bfloat16)
+    for k in range(plane):
+        out[k, count:, :] = terms[:, k * wide : (k + 1) * wide]
 
 
 def split(grads, master, first, second, plane):
     count, width = grads.shape
-    shape = (plane, count + KINDS * SLOT_ROWS, width // plane)
+    lines = KINDS * master.shape[0] * master.shape[1]
     return pl.pallas_call(
         split_kernel,
-        out_shape=jax.ShapeDtypeStruct(shape, grads.dtype),
+        out_shape=jax.ShapeDtypeStruct((plane, count + lines, width // plane), grads.dtype),
         in_specs=[VMEM] * 4,
         out_specs=VMEM,
-        scratch_shapes=[pltpu.VMEM((3, SLOT_ROWS, width), jnp.float32)],
+        scratch_shapes=[
+            pltpu.VMEM((3, SLOT_ROWS, width), jnp.float32),
+            pltpu.VMEM((lines, width), jnp.float32),
+        ],
         name="split",
     )(grads, master, first, second)
 
@@ -140,16 +145,14 @@
 
 
 def pack_kernel(raw, order, route, out):
-    plane, count, _ = raw.shape
+    plane = raw.shape[0]
     ring = out.shape[0]
     rows = order.shape[0]
     part = rows // ring
     total = raw[0, :rows, :].astype(jnp.float32)
     for j in range(1, plane):
         total = total + raw[j, :rows, :].astype(jnp.float32)
-    lines = [
-        raw[j, at : at + SLOT_ROWS, :] for at in range(rows, count, SLOT_ROWS) for j in range(plane)
-    ]
+    lines = [raw[j, rows:, :] for j in range(plane)]
     high, low = two_terms(total)
     sources = ((order, high), (order, low), (route, jnp.concatenate(lines, axis=0)))
     for i, (matrix, source) in enumerate(sources):
@@ -171,11 +174,11 @@
     high, low = two_terms(total)
     lows = choose(spread[...], low)
     squares = jnp.sum(total * total) + jnp.zeros((extra, total.shape[1]), jnp.float32)
-    first, _ = two_terms(squares)
-    second, _ = two_terms(squares - first.astype(jnp.float32))
-    third = squares - first.astype(jnp.float32) - second.astype(jnp.float32)
+    parts = []
+    for _ in range(3):
+        parts.append(squares.astype(jnp.bfloat16).astype(jnp.float32))
+        squares = jnp.where(jnp.abs(parts[-1]) < jnp.inf, squares - parts[-1], 0.0)
     row = lax.broadcasted_iota(jnp.int32, squares.shape, 0)
-    parts = (first.astype(jnp.float32), second.astype(jnp.float32), third)
     lines = jnp.concatenate([got[z, 2 * part :, :] for z in range(ring)], axis=0)
     lines = choose(take[...], lines).astype(out.dtype)
     for z in range(ring):
@@ -261,7 +264,8 @@
     goes = jnp.where(pair_at < 0, -1, pair_at)[None, :]
     goes = jnp.where(goes < 0, -1, (goes // pair * KINDS + kind) * pair + goes % pair)
     chunks = jnp.arange(ring * KINDS * pair, dtype=i32)
-    route = goes.reshape(1, KINDS * plane_lines) == chunks[:, None]
+    goes = goes.reshape(KINDS, plane, SLOT_ROWS)[:, :, :lines].transpose(1, 0, 2)
+    route = goes.reshape(1, plane * KINDS * lines) == chunks[:, None]
     own_line = lax.dynamic_slice_in_dim(line_at, my_z * part, part)
     within = jnp.arange(part, dtype=i32) % pair
     comes = (own_line // plane_lines * KINDS + kind) * pair + within[None, :]

time: 127 us -> 126 us (level)
  no operation moved by 1% of the time
where the time goes in v14:
time: 126 us
  blocking collectives  86.4 us (69%)
  starting transfers between devices  14.7 us (12%)
  waiting for transfers between devices  13.9 us (11%)
  Pallas kernels  7.08 us (6%)
  other arithmetic  2.21 us (2%)
    all_to_all x4, blocking collectives, exchange(): return lax.all_to_all(chunks, axis, 0, 0, tiled=True)  86.4 us
    all_to_all x1, waiting for transfers between devices, exchange(): return lax.all_to_all(chunks, axis, 0, 0, tiled=True)  13.9 us
    all_to_all x1, starting transfers between devices, exchange(): return lax.all_to_all(chunks, axis, 0, 0, tiled=True)  10.5 us
    ppermute x1, starting transfers between devices, shards(): others = lax.ppermute(halves, 'c', [(0, 1), (1, 0)])  4.16 us
    pallas_call x1, Pallas kernels, split(): pl.pallas_call(split_kernel, out_shape=jax.ShapeDtypeStruct((plane, count...  2.53 us
  transfers between devices with their start and end apart: 2, of which 1 were waited for; matrix products, arithmetic and copies ran while one was open for 2% of the time, Pallas kernels for 2%

profile of v14, /device:TPU:1, one launch (start us, length us, event | category | flops | bytes accessed | tf_op | source)
XLA Modules:
  0.0 125.9 jit_solution(18117383180582504792)
XLA Ops:
  0.6 2.5 %split.1 = bf16[16,280,128]{2,1,0:T(8,128)(2,1)} custom-call(bf16[256,2048]{1,0:T(8,128)(2,1)} %bitcast.32, f32[3,2,2048]{2,1,0:T(2,128)} %bitcast.24, f32[3,2,2048]{2,1,0:T(2,128)} %bitcast.26, f32[3,2,2048]{2,1,0:T(2,128)} %bitcast.28), custom_call_target="tpu_custom_call" | custom-call | tf_op jit(solution)/shard_map/split/pallas_call | solution.py:87
  3.2 10.5 %all-to-all-start = ((bf16[16,280,128]{2,1,0:T(8,128)(2,1)}), bf16[16,280,128]{2,1,0:T(8,128)(2,1)S(1)}, u32[]{:S(2)}, u32[]{:S(2)}) async-start(bf16[16,280,128]{2,1,0:T(8,128)(2,1)} %split.1), calls=%async_computation | async-start | bytes 2293760 | tf_op jit(solution)/shard_map/all_to_all | solution.py:39
  13.7 0.2 compare_reduce_fusion
  13.9 0.2 convert_reduce_fusion
  14.2 0.1 add.309
  14.3 0.1 add_add_fusion
  14.4 0.1 add.323
  14.6 0.1 iota_add_fusion
  14.7 0.1 add.313
  14.8 0.2 select_reduce_fusion.1
  15.2 0.1 eq.137
  15.3 0.1 select_reduce_fusion
  15.4 0.1 multiply_add_fusion.1
  15.6 0.1 add.337
  15.6 0.7 pad_add_fusion.at
  16.3 0.1 fusion.5.pick_low
  16.4 0.1 compare_convert_fusion.pick
  16.5 0.1 fusion.3.take
  16.6 0.1 fusion.2
  16.8 13.9 %all-to-all-done.raw = bf16[16,280,128]{2,1,0:T(8,128)(2,1)S(1)} async-done(((bf16[16,280,128]{2,1,0:T(8,128)(2,1)}), bf16[16,280,128]{2,1,0:T(8,128)(2,1)S(1)}, u32[]{:S(2)}, u32[]{:S(2)}) %all-to-all-start) | async-done | bytes 1146912 | tf_op jit(solution)/shard_map/all_to_all | solution.py:39
  30.7 0.4 pack.1
  31.1 25.8 %all_to_all.25.got = bf16[8,112,128]{2,1,0:T(8,128)(2,1)S(1)} all-to-all(bf16[8,112,128]{2,1,0:T(8,128)(2,1)S(1)} %pack.1), channel_id=1, replica_groups=mesh['z'=8,'pair'=2,'x'=4,'c'=2,'layer'=4] {'z'}, dimensions={0} | all-to-all | bytes 458752 | tf_op jit(solution)/shard_map/all_to_all | solution.py:39
  56.9 0.2 reduce.1
  57.1 29.9 %all_to_all.26.every.refs_0_ = bf16[8,176,128]{2,1,0:T(8,128)(2,1)S(1)} all-to-all(bf16[8,176,128]{2,1,0:T(8,128)(2,1)S(1)} %reduce.1), channel_id=1, replica_groups=mesh['z'=8,'pair'=2,'x'=4,'c'=2,'layer'=4] {'z'}, dimensions={0} | all-to-all | bytes 720896 | tf_op jit(solution)/shard_map/all_to_all | solution.py:39
  87.0 0.2 send.1
  87.1 19.4 %all_to_all.27.refs_1_.got = f32[64,8,128]{2,1,0:T(8,128)S(1)} all-to-all(f32[64,8,128]{2,1,0:T(8,128)S(1)} %bitcast.23), channel_id=1, replica_groups=mesh['z'=8,'pair'=2,'x'=4,'c'=2,'layer'=4] {'pair','x','c','layer'}, dimensions={0} | all-to-all | bytes 524288 | tf_op jit(solution)/shard_map/all_to_all | solution.py:39
  106.6 0.6 step.1
  107.2 11.3 %all_to_all.28.strips = bf16[8,256,128]{2,1,0:T(8,128)(2,1)S(1)} all-to-all(bf16[8,256,128]{2,1,0:T(8,128)(2,1)S(1)} %get-tuple-element.33), channel_id=1, replica_groups=mesh['z'=8,'pair'=2,'x'=4,'c'=2,'layer'=4] {'pair','x'}, dimensions={0} | all-to-all | bytes 1048576 | tf_op jit(solution)/shard_map/all_to_all | solution.py:39
  118.4 4.2 %collective-permute-start = (bf16[8,256,128]{2,1,0:T(8,128)(2,1)S(1)}, bf16[8,256,128]{2,1,0:T(8,128)(2,1)S(1)}, u32[]{:S(2)}, u32[]{:S(2)}) collective-permute-start(bf16[8,256,128]{2,1,0:T(8,128)(2,1)S(1)} %all_to_all.28.strips), channel_id=1, source_target_pairs={{0,4},{4,0},{1,5},{5,1},{2,6},{6,2},{3,7},{7,3},{8,12},{12,8},{9,1... | collective-permute-start | bytes 1572872 | tf_op jit(solution)/shard_map/ppermute | solution.py:324
  122.6 0.9 join.2.refs_0_
  123.5 1.5 %own.1 = (f32[3,2,2048]{2,1,0:T(2,128)}, f32[3,2,2048]{2,1,0:T(2,128)}, f32[3,2,2048]{2,1,0:T(2,128)}) custom-call(s32[4]{0:T(128)} %pad_add_fusion.at, f32[64,8,128]{2,1,0:T(8,128)S(1)} %all_to_all.27.refs_1_.got, f32[1,128]{1,0:T(1,128)S(1)} %copy-done.3, f32[3,2,2048]{2,1,0:T(2,128)S(1)} %bitcast.25, f32[3,2,2048]{2,1,0:T(2,128)S(1)} %bitcast.27, ...), custom_call_target="tpu_custom_call" | custom-call | tf_op jit(solution)/shard_map/own/pallas_call | solution.py:327
  125.0 0.8 join.3
  (29 shorter events, 0.4 us)
Async XLA Ops:
  3.2 10.5 %copy-start.4 = (s32[1,128]{1,0:T(1,128)S(1)}, s32[1,128]{1,0:T(1,128)}, u32[]{:S(2)}) copy-start(s32[1,128]{1,0:T(1,128)} %param.11) | copy-start | bytes 1540
  3.2 10.5 %copy-start.5 = (s32[1,128]{1,0:T(1,128)S(1)}, s32[1,128]{1,0:T(1,128)}, u32[]{:S(2)}) copy-start(s32[1,128]{1,0:T(1,128)} %param.10) | copy-start | bytes 1540
  3.2 27.5 %all-to-all-start = ((bf16[16,280,128]{2,1,0:T(8,128)(2,1)}), bf16[16,280,128]{2,1,0:T(8,128)(2,1)S(1)}, u32[]{:S(2)}, u32[]{:S(2)}) async-start(bf16[16,280,128]{2,1,0:T(8,128)(2,1)} %split.1), calls=%async_computation | async-start | bytes 2293760 | tf_op jit(solution)/shard_map/all_to_all | solution.py:39
  107.2 16.3 %copy-start = (f32[1,3,2,2048]{3,2,1,0:T(2,128)S(1)}, f32[1,3,2,2048]{3,2,1,0:T(2,128)}, u32[]{:S(2)}) copy-start(f32[1,3,2,2048]{3,2,1,0:T(2,128)} %param.7) | copy-start | bytes 147460
  107.2 16.3 %copy-start.1 = (f32[1,3,2,2048]{3,2,1,0:T(2,128)S(1)}, f32[1,3,2,2048]{3,2,1,0:T(2,128)}, u32[]{:S(2)}) copy-start(f32[1,3,2,2048]{3,2,1,0:T(2,128)} %param.8) | copy-start | bytes 147460
  107.2 16.3 %copy-start.2 = (f32[1,3,2,2048]{3,2,1,0:T(2,128)S(1)}, f32[1,3,2,2048]{3,2,1,0:T(2,128)}, u32[]{:S(2)}) copy-start(f32[1,3,2,2048]{3,2,1,0:T(2,128)} %param.9) | copy-start | bytes 147460
  107.2 16.3 %copy-start.3 = (f32[1,128]{1,0:T(1,128)S(1)}, f32[1,128]{1,0:T(1,128)}, u32[]{:S(2)}) copy-start(f32[1,128]{1,0:T(1,128)} %get-tuple-element.36.rms) | copy-start | bytes 1540
  118.4 6.6 %collective-permute-start = (bf16[8,256,128]{2,1,0:T(8,128)(2,1)S(1)}, bf16[8,256,128]{2,1,0:T(8,128)(2,1)S(1)}, u32[]{:S(2)}, u32[]{:S(2)}) collective-permute-start(bf16[8,256,128]{2,1,0:T(8,128)(2,1)S(1)} %all_to_all.28.strips), channel_id=1, source_target_pairs={{0,4},{4,0},{1,5},{5,1},{2,6},{6,2},{3,7},{7,3},{8,12},{12,8},{9,1... | collective-permute-start | bytes 1572872 | tf_op jit(solution)/shard_map/ppermute | solution.py:324

commit v15 on v14

--- a/solution.py
+++ b/solution.py
@@ -83,52 +83,58 @@
 
 def split(grads, master, first, second, plane):
     count, width = grads.shape
-    lines = KINDS * master.shape[0] * master.shape[1]
+    capacity, slab, _ = master.shape
+    lines = KINDS * capacity * slab
+    steps = 2
+    part = width // steps
+    state = pl.BlockSpec((capacity, slab, part), lambda i: (0, 0, i))
     return pl.pallas_call(
         split_kernel,
+        grid=(steps,),
         out_shape=jax.ShapeDtypeStruct((plane, count + lines, width // plane), grads.dtype),
-        in_specs=[VMEM] * 4,
-        out_specs=VMEM,
+        in_specs=[pl.BlockSpec((count, part), lambda i: (0, i)), state, state, state],
+        out_specs=pl.BlockSpec(
+            (plane // steps, count + lines, width // plane), lambda i: (i, 0, 0)
+        ),
         scratch_shapes=[
-            pltpu.VMEM((3, SLOT_ROWS, width), jnp.float32),
-            pltpu.VMEM((lines, width), jnp.float32),
+            pltpu.VMEM((3, SLOT_ROWS, part), jnp.float32),
+            pltpu.VMEM((lines, part), jnp.float32),
         ],
         name="split",
     )(grads, master, first, second)
 
 
-def join_kernel(core, strips, *refs):
-    out, sem = refs[-2:]
+def put_strips(core, strips, out, sem):
     count, _, wide = strips.shape
-    moves = [
-        pltpu.make_async_copy(
-            strips.at[i],
-            out.at[:, pl.ds(pl.multiple_of((2 * i + core[0]) * wide, wide), wide)],
-            sem.at[i],
-        )
-        for i in range(count)
-    ]
-    for move in moves:
-        move.start()
-    for move in moves:
+    moves = []
+    for i in range(count):
+        lane = pl.multiple_of((2 * i + core[0]) * wide, wide)
+        moves.append(pltpu.make_async_copy(strips.at[i], out.at[:, pl.ds(lane, wide)], sem.at[i]))
+        moves[-1].start()
+    return moves
+
+
+def join_kernel(core, strips, before, out, sem):
+    del before
+    for move in put_strips(core, strips, out, sem):
         move.wait()
 
 
-def join(core, strips, *before):
-    count, rows, wide = strips.shape
+def join(core, strips, before):
     return pl.pallas_call(
         join_kernel,
-        out_shape=jax.ShapeDtypeStruct((rows, 2 * count * wide), strips.dtype),
-        in_specs=[SMEM, VMEM] + [ANY] * len(before),
+        out_shape=jax.ShapeDtypeStruct(before.shape, before.dtype),
+        in_specs=[SMEM, VMEM, ANY],
         out_specs=ANY,
-        scratch_shapes=[pltpu.SemaphoreType.DMA((count,))],
-        input_output_aliases={2: 0} if before else {},
+        scratch_shapes=[pltpu.SemaphoreType.DMA(strips.shape[:1])],
+        input_output_aliases={2: 0},
         name="join",
-    )(core.reshape(1), near(strips), *before)
-
-
-def own_kernel(at, got, rms, master, first, second, *refs):
-    outs, rows, grads = refs[:3], refs[3], refs[4]
+    )(core.reshape(1), near(strips), before)
+
+
+def own_kernel(at, core, got, rms, master, first, second, strips, *refs):
+    outs, weights, rows, grads, sem = refs[:3], refs[3], refs[4], refs[5], refs[6]
+    moves = put_strips(core, strips, weights, sem)
     wide = got.shape[2]
     count = grads.shape[1] // wide
     layers = got.shape[0] // count
@@ -142,6 +148,8 @@
         rows[i] = new[i]
         for s in range(capacity):
             out[s] = jnp.where(at[1 + s] > 0, rows[i, s * slab : (s + 1) * slab, :], old[s])
+    for move in moves:
+        move.wait()
 
 
 def pack_kernel(raw, order, route, out):
@@ -322,19 +330,27 @@
     core = lax.axis_index("c")
     halves, got, rms = lax.optimization_barrier((exchange(copies, HALF), got, rms))
     others = lax.ppermute(halves, "c", [(0, 1), (1, 0)])
-    weights = join(core, halves)
-
-    new = pl.pallas_call(
+
+    *new, weights = pl.pallas_call(
         own_kernel,
-        out_shape=(jax.ShapeDtypeStruct(master.shape[1:], f32),) * 3,
-        in_specs=[SMEM] + [VMEM] * 5,
-        out_specs=(VMEM,) * 3,
+        out_shape=(jax.ShapeDtypeStruct(master.shape[1:], f32),) * 3
+        + (jax.ShapeDtypeStruct((rows, width), bf16),),
+        in_specs=[SMEM] * 2 + [VMEM] * 6,
+        out_specs=(VMEM, VMEM, VMEM, ANY),
         scratch_shapes=[
             pltpu.VMEM((3, SLOT_ROWS, width), f32),
             pltpu.VMEM((SLOT_ROWS, width), f32),
+            pltpu.SemaphoreType.DMA(halves.shape[:1]),
         ],
         name="own",
-    )(at, near(got), near(rms), *[near(o[0]) for o in (master, moment_one, moment_two)])
+    )(
+        at,
+        core.reshape(1),
+        near(got),
+        near(rms),
+        *[near(o[0]) for o in (master, moment_one, moment_two)],
+        near(halves),
+    )
     others, weights = lax.optimization_barrier((others, weights))
     weights = join(1 - core, others, weights)
     return (new[0][None], new[1][None], new[2][None], weights[None], rms[0, 0])

time: 126 us -> 127 us (level)
    pallas_call x3 -> x2, Pallas kernels: 4.23 us -> 3.1 us  [the longest x1 2.25 us: split(): pl.pallas_call(split_kernel, grid=(steps,), out_shape=jax.ShapeDtypeStruc...]
where the time goes in v15:
time: 127 us; the launch traced here: 126 us
  blocking collectives  86.4 us (68%)
  starting transfers between devices  14.7 us (12%)
  waiting for transfers between devices  14 us (11%)
  Pallas kernels  6.64 us (5%)
  other arithmetic  2.13 us (2%)
  local copies, waits for them, and re-layouts  1.4 us (1%)
    all_to_all x4, blocking collectives, exchange(): return lax.all_to_all(chunks, axis, 0, 0, tiled=True)  86.4 us
    all_to_all x1, waiting for transfers between devices, exchange(): return lax.all_to_all(chunks, axis, 0, 0, tiled=True)  14 us
    all_to_all x1, starting transfers between devices, exchange(): return lax.all_to_all(chunks, axis, 0, 0, tiled=True)  10.5 us
    ppermute x1, starting transfers between devices, shards(): others = lax.ppermute(halves, 'c', [(0, 1), (1, 0)])  4.16 us
  transfers between devices with their start and end apart: 2, of which 1 were waited for; matrix products, arithmetic and copies ran while one was open for 2% of the time, Pallas kernels for 2%

profile of v15, /device:TPU:1, one launch (start us, length us, event | category | flops | bytes accessed | tf_op | source)
XLA Modules:
  0.0 126.1 jit_solution(10362383167261148786)
XLA Ops:
  0.6 2.2 %split.1 = bf16[16,280,128]{2,1,0:T(8,128)(2,1)} custom-call(bf16[256,2048]{1,0:T(8,128)(2,1)} %bitcast.31, f32[3,2,2048]{2,1,0:T(2,128)} %bitcast.24, f32[3,2,2048]{2,1,0:T(2,128)} %bitcast.26, f32[3,2,2048]{2,1,0:T(2,128)} %bitcast.28), custom_call_target="tpu_custom_call" | custom-call | tf_op jit(solution)/shard_map/split/pallas_call | solution.py:91
  2.9 10.5 %all-to-all-start = ((bf16[16,280,128]{2,1,0:T(8,128)(2,1)}), bf16[16,280,128]{2,1,0:T(8,128)(2,1)S(1)}, u32[]{:S(2)}, u32[]{:S(2)}) async-start(bf16[16,280,128]{2,1,0:T(8,128)(2,1)} %split.1), calls=%async_computation | async-start | bytes 2293760 | tf_op jit(solution)/shard_map/all_to_all | solution.py:39
  13.4 0.2 compare_reduce_fusion
  13.6 0.2 convert_reduce_fusion
  13.9 0.1 add.309
  14.1 0.1 add_add_fusion
  14.2 0.1 add.323
  14.3 0.1 iota_add_fusion
  14.4 0.1 add.313
  14.5 0.2 select_reduce_fusion.1
  14.9 0.1 eq.137
  15.0 0.1 select_reduce_fusion
  15.2 0.1 multiply_add_fusion.1
  15.3 0.1 add.337
  15.4 0.6 pad_add_fusion.at
  16.0 0.1 fusion.5.pick_low
  16.0 0.1 compare_convert_fusion.pick
  16.1 0.1 fusion.3.take
  16.2 0.1 fusion.2
  16.4 14.0 %all-to-all-done.raw = bf16[16,280,128]{2,1,0:T(8,128)(2,1)S(1)} async-done(((bf16[16,280,128]{2,1,0:T(8,128)(2,1)}), bf16[16,280,128]{2,1,0:T(8,128)(2,1)S(1)}, u32[]{:S(2)}, u32[]{:S(2)}) %all-to-all-start) | async-done | bytes 1146912 | tf_op jit(solution)/shard_map/all_to_all | solution.py:39
  30.4 0.4 pack.1
  30.8 25.8 %all_to_all.25.got = bf16[8,112,128]{2,1,0:T(8,128)(2,1)S(1)} all-to-all(bf16[8,112,128]{2,1,0:T(8,128)(2,1)S(1)} %pack.1), channel_id=1, replica_groups=mesh['z'=8,'pair'=2,'x'=4,'c'=2,'layer'=4] {'z'}, dimensions={0} | all-to-all | bytes 458752 | tf_op jit(solution)/shard_map/all_to_all | solution.py:39
  56.6 0.2 reduce.1
  56.8 29.9 %all_to_all.26.every.refs_0_ = bf16[8,176,128]{2,1,0:T(8,128)(2,1)S(1)} all-to-all(bf16[8,176,128]{2,1,0:T(8,128)(2,1)S(1)} %reduce.1), channel_id=1, replica_groups=mesh['z'=8,'pair'=2,'x'=4,'c'=2,'layer'=4] {'z'}, dimensions={0} | all-to-all | bytes 720896 | tf_op jit(solution)/shard_map/all_to_all | solution.py:39
  86.7 0.2 send.1
  86.9 19.6 %all_to_all.27.refs_1_.got = f32[64,8,128]{2,1,0:T(8,128)S(1)} all-to-all(f32[64,8,128]{2,1,0:T(8,128)S(1)} %bitcast.23), channel_id=1, replica_groups=mesh['z'=8,'pair'=2,'x'=4,'c'=2,'layer'=4] {'pair','x','c','layer'}, dimensions={0} | all-to-all | bytes 524288 | tf_op jit(solution)/shard_map/all_to_all | solution.py:39
  106.5 0.6 step.1
  107.1 11.1 %all_to_all.28.strips = bf16[8,256,128]{2,1,0:T(8,128)(2,1)S(1)} all-to-all(bf16[8,256,128]{2,1,0:T(8,128)(2,1)S(1)} %get-tuple-element.34), channel_id=1, replica_groups=mesh['z'=8,'pair'=2,'x'=4,'c'=2,'layer'=4] {'pair','x'}, dimensions={0} | all-to-all | bytes 1048576 | tf_op jit(solution)/shard_map/all_to_all | solution.py:39
  118.2 4.2 %collective-permute-start = (bf16[8,256,128]{2,1,0:T(8,128)(2,1)S(1)}, bf16[8,256,128]{2,1,0:T(8,128)(2,1)S(1)}, u32[]{:S(2)}, u32[]{:S(2)}) collective-permute-start(bf16[8,256,128]{2,1,0:T(8,128)(2,1)S(1)} %all_to_all.28.strips), channel_id=1, source_target_pairs={{0,4},{4,0},{1,5},{5,1},{2,6},{6,2},{3,7},{7,3},{8,12},{12,8},{9,1... | collective-permute-start | bytes 1572872 | tf_op jit(solution)/shard_map/ppermute | solution.py:332
  122.4 0.6 copy-done.3
  123.0 2.2 %own.1 = (f32[3,2,2048]{2,1,0:T(2,128)}, f32[3,2,2048]{2,1,0:T(2,128)}, f32[3,2,2048]{2,1,0:T(2,128)}, bf16[256,2048]{1,0:T(8,128)(2,1)}) custom-call(s32[4]{0:T(128)} %pad_add_fusion.at, s32[1]{0:T(128)} %bitcast.8.core, f32[64,8,128]{2,1,0:T(8,128)S(1)} %all_to_all.27.refs_1_.got, f32[1,128]{1,0:T(1,128)S(1)} %copy-done.3, f32[3,2,2048]{2,1,0:T(2,128)S(1)} %bitcast.25, ...), custom_call_target="tpu_custom_call" | custom-call | tf_op jit(solution)/shard_map/own/pallas_call | solution.py:334
  125.2 0.9 join.1
  (28 shorter events, 0.4 us)
Async XLA Ops:
  2.9 10.5 %copy-start.4 = (s32[1,128]{1,0:T(1,128)S(1)}, s32[1,128]{1,0:T(1,128)}, u32[]{:S(2)}) copy-start(s32[1,128]{1,0:T(1,128)} %param.11) | copy-start | bytes 1540
  2.9 10.5 %copy-start.5 = (s32[1,128]{1,0:T(1,128)S(1)}, s32[1,128]{1,0:T(1,128)}, u32[]{:S(2)}) copy-start(s32[1,128]{1,0:T(1,128)} %param.10) | copy-start | bytes 1540
  2.9 27.5 %all-to-all-start = ((bf16[16,280,128]{2,1,0:T(8,128)(2,1)}), bf16[16,280,128]{2,1,0:T(8,128)(2,1)S(1)}, u32[]{:S(2)}, u32[]{:S(2)}) async-start(bf16[16,280,128]{2,1,0:T(8,128)(2,1)} %split.1), calls=%async_computation | async-start | bytes 2293760 | tf_op jit(solution)/shard_map/all_to_all | solution.py:39
  86.9 35.5 %copy-start = (f32[1,3,2,2048]{3,2,1,0:T(2,128)S(1)}, f32[1,3,2,2048]{3,2,1,0:T(2,128)}, u32[]{:S(2)}) copy-start(f32[1,3,2,2048]{3,2,1,0:T(2,128)} %param.7) | copy-start | bytes 147460
  86.9 35.5 %copy-start.1 = (f32[1,3,2,2048]{3,2,1,0:T(2,128)S(1)}, f32[1,3,2,2048]{3,2,1,0:T(2,128)}, u32[]{:S(2)}) copy-start(f32[1,3,2,2048]{3,2,1,0:T(2,128)} %param.8) | copy-start | bytes 147460
  86.9 35.5 %copy-start.2 = (f32[1,3,2,2048]{3,2,1,0:T(2,128)S(1)}, f32[1,3,2,2048]{3,2,1,0:T(2,128)}, u32[]{:S(2)}) copy-start(f32[1,3,2,2048]{3,2,1,0:T(2,128)} %param.9) | copy-start | bytes 147460
  118.2 7.0 %collective-permute-start = (bf16[8,256,128]{2,1,0:T(8,128)(2,1)S(1)}, bf16[8,256,128]{2,1,0:T(8,128)(2,1)S(1)}, u32[]{:S(2)}, u32[]{:S(2)}) collective-permute-start(bf16[8,256,128]{2,1,0:T(8,128)(2,1)S(1)} %all_to_all.28.strips), channel_id=1, source_target_pairs={{0,4},{4,0},{1,5},{5,1},{2,6},{6,2},{3,7},{7,3},{8,12},{12,8},{9,1... | collective-permute-start | bytes 1572872 | tf_op jit(solution)/shard_map/ppermute | solution.py:332
  122.4 0.7 copy-start.3

commit v16 on v14

--- a/solution.py
+++ b/solution.py
@@ -83,15 +83,22 @@
 
 def split(grads, master, first, second, plane):
     count, width = grads.shape
-    lines = KINDS * master.shape[0] * master.shape[1]
+    capacity, slab, _ = master.shape
+    lines = KINDS * capacity * slab
+    steps = 2
+    part = width // steps
+    state = pl.BlockSpec((capacity, slab, part), lambda i: (0, 0, i))
     return pl.pallas_call(
         split_kernel,
+        grid=(steps,),
         out_shape=jax.ShapeDtypeStruct((plane, count + lines, width // plane), grads.dtype),
-        in_specs=[VMEM] * 4,
-        out_specs=VMEM,
+        in_specs=[pl.BlockSpec((count, part), lambda i: (0, i)), state, state, state],
+        out_specs=pl.BlockSpec(
+            (plane // steps, count + lines, width // plane), lambda i: (i, 0, 0)
+        ),
         scratch_shapes=[
-            pltpu.VMEM((3, SLOT_ROWS, width), jnp.float32),
-            pltpu.VMEM((lines, width), jnp.float32),
+            pltpu.VMEM((3, SLOT_ROWS, part), jnp.float32),
+            pltpu.VMEM((lines, part), jnp.float32),
         ],
         name="split",
     )(grads, master, first, second)
@@ -313,7 +320,7 @@
         lambda *refs: step_kernel(float(layers * rows * width), *refs),
         out_shape=(
             pltpu.VMEM((lax.axis_size(HALF), rows, wide), bf16),
-            jax.ShapeDtypeStruct((1, wide), f32),
+            pltpu.VMEM((1, wide), f32),
         ),
         in_specs=[VMEM] * 3,
         out_specs=(VMEM, VMEM),

time: 126 us -> 126 us (level)
  no operation moved by 1% of the time
where the time goes in v16:
time: 126 us; the launch traced here: 125 us
  blocking collectives  86.4 us (69%)
  starting transfers between devices  14.7 us (12%)
  waiting for transfers between devices  13.9 us (11%)
  Pallas kernels  6.59 us (5%)
  other arithmetic  2.21 us (2%)
    all_to_all x4, blocking collectives, exchange(): return lax.all_to_all(chunks, axis, 0, 0, tiled=True)  86.4 us
    all_to_all x1, waiting for transfers between devices, exchange(): return lax.all_to_all(chunks, axis, 0, 0, tiled=True)  13.9 us
    all_to_all x1, starting transfers between devices, exchange(): return lax.all_to_all(chunks, axis, 0, 0, tiled=True)  10.5 us
    ppermute x1, starting transfers between devices, shards(): others = lax.ppermute(halves, 'c', [(0, 1), (1, 0)])  4.16 us
  transfers between devices with their start and end apart: 2, of which 1 were waited for; matrix products, arithmetic and copies ran while one was open for 2% of the time, Pallas kernels for 2%

profile of v16, /device:TPU:1, one launch (start us, length us, event | category | flops | bytes accessed | tf_op | source)
XLA Modules:
  0.0 125.4 jit_solution(4035388794699624733)
XLA Ops:
  0.6 2.2 %split.1 = bf16[16,280,128]{2,1,0:T(8,128)(2,1)} custom-call(bf16[256,2048]{1,0:T(8,128)(2,1)} %bitcast.32, f32[3,2,2048]{2,1,0:T(2,128)} %bitcast.24, f32[3,2,2048]{2,1,0:T(2,128)} %bitcast.26, f32[3,2,2048]{2,1,0:T(2,128)} %bitcast.28), custom_call_target="tpu_custom_call" | custom-call | tf_op jit(solution)/shard_map/split/pallas_call | solution.py:91
  2.9 10.5 %all-to-all-start = ((bf16[16,280,128]{2,1,0:T(8,128)(2,1)}), bf16[16,280,128]{2,1,0:T(8,128)(2,1)S(1)}, u32[]{:S(2)}, u32[]{:S(2)}) async-start(bf16[16,280,128]{2,1,0:T(8,128)(2,1)} %split.1), calls=%async_computation | async-start | bytes 2293760 | tf_op jit(solution)/shard_map/all_to_all | solution.py:39
  13.4 0.2 compare_reduce_fusion
  13.6 0.2 convert_reduce_fusion
  13.9 0.1 add.309
  14.1 0.1 add_add_fusion
  14.2 0.1 add.323
  14.3 0.1 iota_add_fusion
  14.4 0.1 add.313
  14.5 0.2 select_reduce_fusion.1
  14.9 0.1 eq.137
  15.0 0.1 select_reduce_fusion
  15.2 0.1 multiply_add_fusion.1
  15.3 0.1 add.337
  15.4 0.7 pad_add_fusion.at
  16.0 0.1 fusion.5.pick_low
  16.1 0.1 compare_convert_fusion.pick
  16.2 0.1 fusion.3.take
  16.3 0.1 fusion.2
  16.5 13.9 %all-to-all-done.raw = bf16[16,280,128]{2,1,0:T(8,128)(2,1)S(1)} async-done(((bf16[16,280,128]{2,1,0:T(8,128)(2,1)}), bf16[16,280,128]{2,1,0:T(8,128)(2,1)S(1)}, u32[]{:S(2)}, u32[]{:S(2)}) %all-to-all-start) | async-done | bytes 1146912 | tf_op jit(solution)/shard_map/all_to_all | solution.py:39
  30.4 0.4 pack.1
  30.8 25.8 %all_to_all.25.got = bf16[8,112,128]{2,1,0:T(8,128)(2,1)S(1)} all-to-all(bf16[8,112,128]{2,1,0:T(8,128)(2,1)S(1)} %pack.1), channel_id=1, replica_groups=mesh['z'=8,'pair'=2,'x'=4,'c'=2,'layer'=4] {'z'}, dimensions={0} | all-to-all | bytes 458752 | tf_op jit(solution)/shard_map/all_to_all | solution.py:39
  56.6 0.2 reduce.1
  56.8 29.9 %all_to_all.26.every.refs_0_ = bf16[8,176,128]{2,1,0:T(8,128)(2,1)S(1)} all-to-all(bf16[8,176,128]{2,1,0:T(8,128)(2,1)S(1)} %reduce.1), channel_id=1, replica_groups=mesh['z'=8,'pair'=2,'x'=4,'c'=2,'layer'=4] {'z'}, dimensions={0} | all-to-all | bytes 720896 | tf_op jit(solution)/shard_map/all_to_all | solution.py:39
  86.7 0.2 send.1
  86.9 19.4 %all_to_all.27.refs_1_.got = f32[64,8,128]{2,1,0:T(8,128)S(1)} all-to-all(f32[64,8,128]{2,1,0:T(8,128)S(1)} %bitcast.23), channel_id=1, replica_groups=mesh['z'=8,'pair'=2,'x'=4,'c'=2,'layer'=4] {'pair','x','c','layer'}, dimensions={0} | all-to-all | bytes 524288 | tf_op jit(solution)/shard_map/all_to_all | solution.py:39
  106.3 0.4 step.1
  106.7 11.3 %all_to_all.28.strips = bf16[8,256,128]{2,1,0:T(8,128)(2,1)S(1)} all-to-all(bf16[8,256,128]{2,1,0:T(8,128)(2,1)S(1)} %get-tuple-element.33), channel_id=1, replica_groups=mesh['z'=8,'pair'=2,'x'=4,'c'=2,'layer'=4] {'pair','x'}, dimensions={0} | all-to-all | bytes 1048576 | tf_op jit(solution)/shard_map/all_to_all | solution.py:39
  118.0 4.2 %collective-permute-start = (bf16[8,256,128]{2,1,0:T(8,128)(2,1)S(1)}, bf16[8,256,128]{2,1,0:T(8,128)(2,1)S(1)}, u32[]{:S(2)}, u32[]{:S(2)}) collective-permute-start(bf16[8,256,128]{2,1,0:T(8,128)(2,1)S(1)} %all_to_all.28.strips), channel_id=1, source_target_pairs={{0,4},{4,0},{1,5},{5,1},{2,6},{6,2},{3,7},{7,3},{8,12},{12,8},{9,1... | collective-permute-start | bytes 1572872 | tf_op jit(solution)/shard_map/ppermute | solution.py:331
  122.2 0.9 join.2.refs_0_
  123.1 1.5 %own.1 = (f32[3,2,2048]{2,1,0:T(2,128)}, f32[3,2,2048]{2,1,0:T(2,128)}, f32[3,2,2048]{2,1,0:T(2,128)}) custom-call(s32[4]{0:T(128)} %pad_add_fusion.at, f32[64,8,128]{2,1,0:T(8,128)S(1)} %all_to_all.27.refs_1_.got, f32[1,128]{1,0:T(1,128)S(1)} %get-tuple-element.36.rms, f32[3,2,2048]{2,1,0:T(2,128)S(1)} %bitcast.25, f32[3,2,2048]{2,1,0:T(2,128)S(1)} %bitcast.27, ...), custom_call_target="tpu_custom_call" | custom-call | tf_op jit(solution)/shard_map/own/pallas_call | solution.py:334
  124.6 0.8 join.3
  (29 shorter events, 0.4 us)
Async XLA Ops:
  2.9 10.5 %copy-start.4 = (s32[1,128]{1,0:T(1,128)S(1)}, s32[1,128]{1,0:T(1,128)}, u32[]{:S(2)}) copy-start(s32[1,128]{1,0:T(1,128)} %param.11) | copy-start | bytes 1540
  2.9 10.5 %copy-start.5 = (s32[1,128]{1,0:T(1,128)S(1)}, s32[1,128]{1,0:T(1,128)}, u32[]{:S(2)}) copy-start(s32[1,128]{1,0:T(1,128)} %param.10) | copy-start | bytes 1540
  2.9 27.5 %all-to-all-start = ((bf16[16,280,128]{2,1,0:T(8,128)(2,1)}), bf16[16,280,128]{2,1,0:T(8,128)(2,1)S(1)}, u32[]{:S(2)}, u32[]{:S(2)}) async-start(bf16[16,280,128]{2,1,0:T(8,128)(2,1)} %split.1), calls=%async_computation | async-start | bytes 2293760 | tf_op jit(solution)/shard_map/all_to_all | solution.py:39
  106.7 16.3 %copy-start.3 = (f32[1,128]{1,0:T(1,128)}, f32[1,128]{1,0:T(1,128)S(1)}, u32[]{:S(2)}) copy-start(f32[1,128]{1,0:T(1,128)S(1)} %get-tuple-element.36.rms) | copy-start | bytes 1540
  106.7 16.3 %copy-start = (f32[1,3,2,2048]{3,2,1,0:T(2,128)S(1)}, f32[1,3,2,2048]{3,2,1,0:T(2,128)}, u32[]{:S(2)}) copy-start(f32[1,3,2,2048]{3,2,1,0:T(2,128)} %param.7) | copy-start | bytes 147460
  106.7 16.3 %copy-start.1 = (f32[1,3,2,2048]{3,2,1,0:T(2,128)S(1)}, f32[1,3,2,2048]{3,2,1,0:T(2,128)}, u32[]{:S(2)}) copy-start(f32[1,3,2,2048]{3,2,1,0:T(2,128)} %param.8) | copy-start | bytes 147460
  106.7 16.3 %copy-start.2 = (f32[1,3,2,2048]{3,2,1,0:T(2,128)S(1)}, f32[1,3,2,2048]{3,2,1,0:T(2,128)}, u32[]{:S(2)}) copy-start(f32[1,3,2,2048]{3,2,1,0:T(2,128)} %param.9) | copy-start | bytes 147460
  118.0 6.6 %collective-permute-start = (bf16[8,256,128]{2,1,0:T(8,128)(2,1)S(1)}, bf16[8,256,128]{2,1,0:T(8,128)(2,1)S(1)}, u32[]{:S(2)}, u32[]{:S(2)}) collective-permute-start(bf16[8,256,128]{2,1,0:T(8,128)(2,1)S(1)} %all_to_all.28.strips), channel_id=1, source_target_pairs={{0,4},{4,0},{1,5},{5,1},{2,6},{6,2},{3,7},{7,3},{8,12},{12,8},{9,1... | collective-permute-start | bytes 1572872 | tf_op jit(solution)/shard_map/ppermute | solution.py:331
